TPU v7x, 32 devices: a whole 2x2x4 slice. The times are simulated.
32 devices in a mesh: groups: 2 (over x), lon: 16 (over z, y, core).
Axes of the slice: x: 2, y: 2, z: 4, core: 2. Of those that a mesh axis runs over, the one named last changes fastest.
Arguments:
- atm_in: bfloat16 [256, 48, 640], P(('groups', 'lon')), parts along dimension 0, may hold values from -6 to 6
- ocean_in: bfloat16 [512, 95, 128], P(('groups', 'lon')), parts along dimension 0, may hold values from -6 to 6
- lift_weight: bfloat16 [48, 256], replicated, may hold values from -0.875 to 0.875
- conv_weight: bfloat16 [3, 3, 256, 256], replicated, may hold values from -0.125 to 0.125
- flux_weight: bfloat16 [256, 16], replicated, may hold values from -0.375 to 0.375
- ocean_weight: bfloat16 [95, 256], replicated, may hold values from -0.625 to 0.625
- couple_weight: bfloat16 [16, 256], replicated, may hold values from -3 to 3
- mix_weight: bfloat16 [256, 256], replicated, may hold values from -0.375 to 0.375
- regrid_weight: bfloat16 [256, 4, 128, 128], P('lon'), may hold values from 0 to 1, as said below
- pair_tile: int32 [256, 3], P('lon'), may hold values from 0 to 39, as said below
- ocean_mask: int32 [256], P('lon'), may hold values from 0 to 1, as said below
Outputs:
- atm_hidden: bfloat16 [256, 256, 640], P(('groups', 'lon')), parts along dimension 0
- ocean_hidden: bfloat16 [512, 256, 128], P(('groups', 'lon')), parts along dimension 0
There are 2 independent parts, one for each index of `groups`. A program takes and returns all parts, laid end to end along the dimension named above; an argument that names none is the same for every part. Nothing has to cross between parts.
Inputs may be any that keep to these rules, and one draw needn't show every extreme that they name: `regrid_weight`: block p = 3 is zero except for the northernmost 2 tiles of each strip (local index 14 and above); blocks 0 to 2 are positive. `pair_tile`: within one of the band of the ocean tile's latitude; column 1 is the band itself. `ocean_mask`: each device's 16 tiles hold between 2 and 8 ones, its northernmost 2 tiles always among them; some device has exactly 8.
All inputs are finite; a program needn't handle non-finite values.
Results may differ from a plain program's by a relative error of at most 0.0053.
Values may be sent and summed in bfloat16 or wider, within the bound.
No kernel may reach another device: no remote copies, remote signals or barrier semaphores. Data moves between devices by JAX's collectives and lax.ppermute only.
A program may use at most 128 MiB of HBM per device.

v0:
```python
import jax
import jax.numpy as jnp
from jax import lax
from jax.sharding import PartitionSpec as P

TLAT = 16


def with_halo(block, sides, width):
    for axis, dim in sides:
        count = lax.axis_size(axis)
        forward = [(i, i + 1) for i in range(count - 1)]
        forward.append((count - 1, 0))
        backward = [(target, source) for source, target in forward]
        low = lax.ppermute(
            lax.slice_in_dim(block, block.shape[dim] - width, None, axis=dim), axis, forward
        )
        high = lax.ppermute(lax.slice_in_dim(block, 0, width, axis=dim), axis, backward)
        block = jnp.concatenate([low, block, high], axis=dim)
    return block


def partner(block, axis, bit):
    count = lax.axis_size(axis)
    route = []
    for low in range(count):
        high = low | 1 << bit
        if high != low and high < count:
            route += [(low, high), (high, low)]
    return lax.ppermute(block, axis, route)


def encode_ocean(states, blocks, got, ocean_weight, couple_weight, mix_weight):
    numer = jnp.einsum("spfa,spoa->sfo", got, blocks, preferred_element_type=jnp.float32)
    denom = jnp.sum(blocks, axis=(1, 3), dtype=jnp.float32)
    regrid = (numer / denom[:, None, :]).astype(jnp.bfloat16)
    base = jnp.einsum("sco,ch->sho", states, ocean_weight, preferred_element_type=jnp.float32)
    base = (
        base + jnp.einsum("sfo,fh->sho", regrid, couple_weight, preferred_element_type=jnp.float32)
    ).astype(jnp.bfloat16)
    mixed = jnp.einsum("sho,hk->sko", base, mix_weight, preferred_element_type=jnp.float32)
    return (base.astype(jnp.float32) + jax.nn.gelu(mixed)).astype(jnp.bfloat16)


def per_device(
    atm_in,
    ocean_in,
    lift_weight,
    conv_weight,
    flux_weight,
    ocean_weight,
    couple_weight,
    mix_weight,
    regrid_weight,
    pair_tile,
    ocean_mask,
):
    columns = atm_in.shape[0]
    lat_rows = atm_in.shape[2]
    hidden_width = lift_weight.shape[1]
    lifted = jnp.einsum(
        "xcy,co->xoy", atm_in, lift_weight, preferred_element_type=jnp.float32
    ).astype(jnp.bfloat16)
    padded = with_halo(lifted, (("lon", 0),), 1)
    padded = jnp.pad(padded, ((0, 0), (0, 0), (1, 1)))
    conv = jnp.zeros((columns, hidden_width, lat_rows), jnp.float32)
    for shift_x in range(3):
        for shift_y in range(3):
            conv = conv + jnp.einsum(
                "xcy,co->xoy",
                padded[shift_x : shift_x + columns, :, shift_y : shift_y + lat_rows],
                conv_weight[shift_x, shift_y],
                preferred_element_type=jnp.float32,
            )
    atm_hidden = (lifted.astype(jnp.float32) + jax.nn.gelu(conv)).astype(jnp.bfloat16)
    flux = jnp.einsum(
        "xhy,hf->xfy", atm_hidden, flux_weight, preferred_element_type=jnp.float32
    ).astype(jnp.bfloat16)
    flux_count = flux.shape[1]
    tiles_lat = lat_rows // TLAT
    tiles = (
        flux.reshape(columns, flux_count, tiles_lat, TLAT)
        .transpose(2, 1, 0, 3)
        .reshape(tiles_lat, flux_count, columns * TLAT)
    )
    near = with_halo(tiles[None], (("lon", 0),), 1)
    near = near.reshape((3 * tiles_lat,) + tiles.shape[1:])
    northern = tiles[tiles_lat - 1]
    strips = lax.axis_size("lon")
    mirrored = northern
    for bit in range(strips.bit_length() - 1):
        mirrored = partner(mirrored, "lon", bit)
    table = jnp.concatenate([near, mirrored[None]], 0)
    local_tiles = ocean_in.shape[0]
    index = jnp.concatenate(
        [
            pair_tile + jnp.arange(3, dtype=jnp.int32)[None, :] * tiles_lat,
            jnp.full((local_tiles, 1), 3 * tiles_lat, jnp.int32),
        ],
        1,
    )
    got = jnp.take(table, index, axis=0)
    result = encode_ocean(ocean_in, regrid_weight, got, ocean_weight, couple_weight, mix_weight)
    ocean_hidden = jnp.where(ocean_mask[:, None, None] == 1, result, jnp.zeros_like(result))
    return (atm_hidden, ocean_hidden)


def solution(mesh):
    in_specs = (
        P(("groups", "lon"), None, None),
        P(("groups", "lon"), None, None),
        P(),
        P(),
        P(),
        P(),
        P(),
        P(),
        P("lon", None, None, None),
        P("lon", None),
        P("lon"),
    )
    out_specs = (P(("groups", "lon"), None, None), P(("groups", "lon"), None, None))
    return jax.shard_map(
        per_device, mesh=mesh, in_specs=in_specs, out_specs=out_specs, check_vma=False
    )
```

profile of v0, /device:TPU:0, one launch (start us, length us, event | category | flops | bytes accessed | tf_op | source)
XLA Modules:
  0.0 97.5 jit_solution(10864364514326306454)
XLA Ops:
  0.6 0.0 copy-start
  0.6 0.0 copy-start.5
  0.7 1.0 %copy-done = bf16[8,48,640]{2,1,0:T(8,128)(2,1)S(1)} copy-done((bf16[8,48,640]{2,1,0:T(8,128)(2,1)S(1)}, bf16[8,48,640]{2,1,0:T(8,128)(2,1)}, u32[]{:S(2)}) %copy-start) | copy-done | bytes 491544
  1.7 1.6 %convert_bitcast_fusion = bf16[8,256,640]{2,1,0:T(8,128)(2,1)S(1)} fusion(bf16[8,48,640]{2,1,0:T(8,128)(2,1)S(1)} %copy-done, bf16[48,256]{1,0:T(8,128)(2,1)} %param.13), kind=kOutput, calls=%fused_computation.41 | convolution fusion | flops 127139840 | bytes 3137536 | tf_op jit(solution)/shard_map/xcy,co->xoy/dot_general | solution.py:61
  3.3 0.1 fusion.88
  3.3 0.5 collective-permute-start
  3.9 5.0 %collective-permute-start.1 = (bf16[1,256,640]{2,1,0:T(8,128)(2,1)S(1)}, bf16[1,256,640]{2,1,0:T(8,128)(2,1)S(1)}, u32[]{:S(2)}, u32[]{:S(2)}) collective-permute-start(bf16[1,256,640]{2,1,0:T(8,128)(2,1)S(1)} %get-tuple-element.3), channel_id=1, source_target_pairs={{1,0},{2,1},{3,2},{4,3},{5,4},{6,5},{7,6},{8,7},{9,8},{10,9},{11,1... | collective-permute-start | bytes 983048 | tf_op jit(solution)/shard_map/ppermute | solution.py:18
  8.9 0.0 copy-start.2
  9.0 0.0 copy-start.6
  9.0 0.0 copy-start.7
  9.0 3.2 %fusion.61 = f32[8,640,256]{1,2,0:T(8,128)} fusion(bf16[8,256,640]{2,1,0:T(8,128)(2,1)S(1)} %convert_bitcast_fusion, bf16[3,3,256,256]{3,2,1,0:T(8,128)(2,1)S(1)} %copy-done.5), kind=kOutput, calls=%fused_computation.69 | convolution fusion | flops 671088640 | bytes 7995392 | tf_op jit(solution)/shard_map/xcy,co->xoy/dot_general | solution.py:69
  12.2 0.1 broadcast_add_fusion
  12.3 0.4 convert_reduce_fusion
  12.6 1.8 %fusion.51 = f32[256,16,128]{2,0,1:T(8,128)} fusion(bf16[16,95,128]{2,0,1:T(8,128)(2,1)S(1)} %copy-done.6, bf16[95,256]{1,0:T(8,128)(2,1)S(1)} %copy-done.7), kind=kOutput, calls=%fused_computation.61 | convolution fusion | flops 99614720 | bytes 2534912 | tf_op jit(solution)/shard_map/sco,ch->sho/dot_general | solution.py:37
  14.4 2.6 %fusion.14 = bf16[10,256,642]{2,1,0:T(8,128)(2,1)S(1)} fusion(bf16[1,256,640]{2,1,0:T(8,128)(2,1)S(1)} %collective-permute-done.1, bf16[8,256,640]{2,1,0:T(8,128)(2,1)S(1)} %convert_bitcast_fusion, bf16[1,256,640]{2,1,0:T(8,128)(2,1)S(1)} %collective-permute-done), kind=kLoop, calls=%fused_computation.19 | loop fusion | flops 19722240 | bytes 6563840 | tf_op jit(solution)/shard_map/concatenate | solution.py:19
  17.1 3.5 %fusion.25 = f32[8,640,256]{1,2,0:T(8,128)} fusion(bf16[10,256,642]{2,1,0:T(8,128)(2,1)S(1)} %fusion.14, bf16[3,3,256,256]{3,2,1,0:T(8,128)(2,1)S(1)} %copy-done.5), kind=kOutput, calls=%fused_computation.31 | convolution fusion | flops 671088640 | bytes 7995392 | tf_op jit(solution)/shard_map/xcy,co->xoy/dot_general | solution.py:69
  20.6 3.5 %fusion.27 = f32[8,640,256]{1,2,0:T(8,128)} fusion(bf16[10,256,642]{2,1,0:T(8,128)(2,1)S(1)} %fusion.14, bf16[3,3,256,256]{3,2,1,0:T(8,128)(2,1)S(1)} %copy-done.5), kind=kOutput, calls=%fused_computation.33 | convolution fusion | flops 671088640 | bytes 7995392 | tf_op jit(solution)/shard_map/xcy,co->xoy/dot_general | solution.py:69
  24.1 3.2 %fusion.29 = f32[8,640,256]{1,2,0:T(8,128)} fusion(bf16[10,256,642]{2,1,0:T(8,128)(2,1)S(1)} %fusion.14, bf16[3,3,256,256]{3,2,1,0:T(8,128)(2,1)S(1)} %copy-done.5), kind=kOutput, calls=%fused_computation.35 | convolution fusion | flops 671088640 | bytes 7995392 | tf_op jit(solution)/shard_map/xcy,co->xoy/dot_general | solution.py:69
  27.4 3.7 %fusion.31 = f32[8,640,256]{1,2,0:T(8,128)} fusion(bf16[10,256,642]{2,1,0:T(8,128)(2,1)S(1)} %fusion.14, bf16[3,3,256,256]{3,2,1,0:T(8,128)(2,1)S(1)} %copy-done.5), kind=kOutput, calls=%fused_computation.37 | convolution fusion | flops 671088640 | bytes 7995392 | tf_op jit(solution)/shard_map/xcy,co->xoy/dot_general | solution.py:69
  31.0 3.2 %fusion.33 = f32[8,640,256]{1,2,0:T(8,128)} fusion(bf16[10,256,642]{2,1,0:T(8,128)(2,1)S(1)} %fusion.14, bf16[3,3,256,256]{3,2,1,0:T(8,128)(2,1)S(1)} %copy-done.5), kind=kOutput, calls=%fused_computation.39 | convolution fusion | flops 671088640 | bytes 7995392 | tf_op jit(solution)/shard_map/xcy,co->xoy/dot_general | solution.py:69
  34.2 3.2 %fusion.15 = f32[8,640,256]{1,2,0:T(8,128)} fusion(bf16[8,256,640]{2,1,0:T(8,128)(2,1)S(1)} %convert_bitcast_fusion, bf16[1,256,640]{2,1,0:T(8,128)(2,1)S(1)} %collective-permute-done, bf16[3,3,256,256]{3,2,1,0:T(8,128)(2,1)S(1)} %copy-done.5), kind=kOutput, calls=%fused_computation.21 | convolution fusion | flops 676986880 | bytes 8323072 | tf_op jit(solution)/shard_map/xcy,co->xoy/dot_general | solution.py:69
  37.4 3.2 %fusion.19 = f32[8,640,256]{1,2,0:T(8,128)} fusion(bf16[1,256,640]{2,1,0:T(8,128)(2,1)S(1)} %collective-permute-done.1, bf16[8,256,640]{2,1,0:T(8,128)(2,1)S(1)} %convert_bitcast_fusion, bf16[3,3,256,256]{3,2,1,0:T(8,128)(2,1)S(1)} %copy-done.5), kind=kOutput, calls=%fused_computation.25 | convolution fusion | flops 676986880 | bytes 8323072 | tf_op jit(solution)/shard_map/xcy,co->xoy/dot_general | solution.py:69
  40.6 17.7 %fusion.9 = bf16[8,256,640]{2,1,0:T(8,128)(2,1)} fusion(f32[8,640,256]{1,2,0:T(8,128)} %fusion.19, f32[8,640,256]{1,2,0:T(8,128)} %fusion.25, f32[8,640,256]{1,2,0:T(8,128)} %fusion.27, f32[8,640,256]{1,2,0:T(8,128)} %fusion.61, f32[8,640,256]{1,2,0:T(8,128)} %fusion.29, f32[8,640,256]{1,2,0:T(8,128)} %fusion.31, f32[8,640,256]{1,2,0:T(8,128)} %fusion.33, ...), kind=kOutput, calls=%fused_computation.13 | convolution fusion | flops 695992320 | bytes 49938432 | tf_op jit(solution)/shard_map/xcy,co->xoy/dot_general | solution.py:69
  58.3 2.2 %fusion.47 = bf16[8,16,640]{2,1,0:T(8,128)(2,1)S(1)} fusion(bf16[8,256,640]{2,1,0:T(8,128)(2,1)} %fusion.9, bf16[256,16]{0,1:T(8,128)(2,1)S(1)} %copy-done.8), kind=kOutput, calls=%fused_computation.54 | convolution fusion | flops 42024960 | bytes 2793472 | tf_op jit(solution)/shard_map/xhy,hf->xfy/dot_general | solution.py:76
  60.5 0.9 reshape.26
  61.5 0.1 slice.97
  61.6 0.1 squeeze.39
  61.7 2.1 %collective-permute-start.4 = (bf16[16,128]{1,0:T(8,128)(2,1)S(1)}, bf16[16,128]{1,0:T(8,128)(2,1)S(1)}, u32[]{:S(2)}, u32[]{:S(2)}) collective-permute-start(bf16[16,128]{1,0:T(8,128)(2,1)S(1)} %squeeze.39), channel_id=1, source_target_pairs={{0,1},{1,0},{2,3},{3,2},{4,5},{5,4},{6,7},{7,6},{8,9},{9,8},{10,11... | collective-permute-start | bytes 12296 | tf_op jit(solution)/shard_map/ppermute | solution.py:30
  63.8 0.1 copy.115
  63.9 0.1 reshape.30
  64.0 0.0 copy-start.9
  64.0 1.8 %copy.110 = bf16[40,16,8,16]{0,3,2,1:T(8,128)(2,1)S(1)} copy(bf16[40,16,8,16]{3,0,1,2:T(8,128)(2,1)} %bitcast.98) | data formatting | bytes 327680 | tf_op jit(solution)/shard_map/transpose | solution.py:83
  65.8 0.8 collective-permute-start.2
  66.6 3.7 %collective-permute-start.3 = (bf16[1,40,16,128]{1,3,2,0:T(8,128)(2,1)S(1)}, bf16[1,40,16,128]{1,3,2,0:T(8,128)(2,1)}, u32[]{:S(2)}, u32[]{:S(2)}) collective-permute-start(bf16[1,40,16,128]{1,3,2,0:T(8,128)(2,1)S(1)} %bitcast.100), channel_id=1, source_target_pairs={{1,0},{2,1},{3,2},{4,3},{5,4},{6,5},{7,6},{8,7},{9,8},{10,9},{11,1... | collective-permute-start | bytes 491528 | tf_op jit(solution)/shard_map/ppermute | solution.py:18
  70.3 11.0 %collective-permute-done.5 = bf16[16,128]{1,0:T(8,128)(2,1)S(1)} collective-permute-done((bf16[16,128]{1,0:T(8,128)(2,1)S(1)}, bf16[16,128]{1,0:T(8,128)(2,1)S(1)}, u32[]{:S(2)}, u32[]{:S(2)}) %collective-permute-start.5) | collective-permute-done | bytes 4128 | tf_op jit(solution)/shard_map/ppermute | solution.py:30
  81.4 0.4 collective-permute-start.6
  81.7 0.1 copy.109
  81.8 0.2 copy.112
  82.1 2.9 %collective-permute-done.6 = bf16[16,128]{1,0:T(8,128)(2,1)S(1)} collective-permute-done((bf16[16,128]{1,0:T(8,128)(2,1)S(1)}, bf16[16,128]{1,0:T(8,128)(2,1)S(1)}, u32[]{:S(2)}, u32[]{:S(2)}) %collective-permute-start.6) | collective-permute-done | bytes 4128 | tf_op jit(solution)/shard_map/ppermute | solution.py:30
  85.0 1.4 %collective-permute-start.7 = (bf16[16,128]{1,0:T(8,128)(2,1)S(1)}, bf16[16,128]{1,0:T(8,128)(2,1)S(1)}, u32[]{:S(2)}, u32[]{:S(2)}) collective-permute-start(bf16[16,128]{1,0:T(8,128)(2,1)S(1)} %collective-permute-done.6), channel_id=1, source_target_pairs={{0,8},{8,0},{1,9},{9,1},{2,10},{10,2},{3,11},{11,3},{4,12},{12,4},... | collective-permute-start | bytes 12296 | tf_op jit(solution)/shard_map/ppermute | solution.py:30
  86.4 1.3 %copy.111 = bf16[1,40,16,128]{3,2,1,0:T(8,128)(2,1)S(1)} copy(bf16[1,40,16,128]{1,3,2,0:T(8,128)(2,1)} %collective-permute-done.2) | data formatting | bytes 327680 | tf_op jit(solution)/shard_map/ppermute | solution.py:15
  87.6 1.3 %copy.113 = bf16[1,40,16,128]{3,2,1,0:T(8,128)(2,1)S(1)} copy(bf16[1,40,16,128]{1,3,2,0:T(8,128)(2,1)} %collective-permute-done.3) | data formatting | bytes 327680 | tf_op jit(solution)/shard_map/ppermute | solution.py:18
  88.9 0.1 pad_maximum_fusion.1
  89.0 0.5 collective-permute-done.7
  89.5 0.6 gather_fusion
  90.2 0.0 copy-start.11
  90.2 3.6 %fusion.46 = bf16[16,256,128]{2,1,0:T(8,128)(2,1)} fusion(f32[256,16,128]{2,0,1:T(8,128)} %fusion.51, bf16[16,4,128,128]{3,2,1,0:T(8,128)(2,1)S(1)} %copy-done.3, bf16[16,4,16,128]{3,2,1,0:T(8,128)(2,1)S(1)} %bitcast.103, pred[16,4]{1,0:T(8,128)(4,1)S(1)} %copy.109, f32[16,128]{1,0:T(8,128)S(1)} %convert_reduce_fusion, bf16[16,256]{1,0:T(8,128)(2,1)S(1)} %copy-done.9), kind=kOutput, calls=%fused_computation.52 | convolution fusion | flops 51576832 | bytes 5521472 | tf_op jit(solution)/shard_map/sfo,fh->sho/dot_general | solution.py:39
  93.8 3.7 %fusion.50 = bf16[16,256,128]{2,1,0:T(8,128)(2,1)} fusion(bf16[16,256,128]{2,1,0:T(8,128)(2,1)} %fusion.46, pred[16]{0:T(512)(128)(4,1)S(1)} %broadcast_compare_fusion, bf16[256,256]{1,0:T(8,128)(2,1)S(1)} %copy-done.11), kind=kOutput, calls=%fused_computation.58 | convolution fusion | flops 274726912 | bytes 2228240 | tf_op jit(solution)/shard_map/sho,hk->sko/dot_general | solution.py:41
  (31 shorter events, 0.2 us)
Async XLA Ops:
  0.6 1.0 %copy-start = (bf16[8,48,640]{2,1,0:T(8,128)(2,1)S(1)}, bf16[8,48,640]{2,1,0:T(8,128)(2,1)}, u32[]{:S(2)}) copy-start(bf16[8,48,640]{2,1,0:T(8,128)(2,1)} %param.11) | copy-start | bytes 1474564
  0.6 8.3 %copy-start.5 = (bf16[3,3,256,256]{3,2,1,0:T(8,128)(2,1)S(1)}, bf16[3,3,256,256]{3,2,1,0:T(8,128)(2,1)}, u32[]{:S(2)}) copy-start(bf16[3,3,256,256]{3,2,1,0:T(8,128)(2,1)} %param.14) | copy-start | bytes 3538948
  3.3 11.1 %collective-permute-start = (bf16[1,256,640]{2,1,0:T(8,128)(2,1)S(1)}, bf16[1,256,640]{2,1,0:T(8,128)(2,1)S(1)}, u32[]{:S(2)}, u32[]{:S(2)}) collective-permute-start(bf16[1,256,640]{2,1,0:T(8,128)(2,1)S(1)} %get-tuple-element.2), channel_id=1, source_target_pairs={{0,1},{1,2},{2,3},{3,4},{4,5},{5,6},{6,7},{7,8},{8,9},{9,10},{10,1... | collective-permute-start | bytes 983048 | tf_op jit(solution)/shard_map/ppermute | solution.py:15
  3.9 10.6 %collective-permute-start.1 = (bf16[1,256,640]{2,1,0:T(8,128)(2,1)S(1)}, bf16[1,256,640]{2,1,0:T(8,128)(2,1)S(1)}, u32[]{:S(2)}, u32[]{:S(2)}) collective-permute-start(bf16[1,256,640]{2,1,0:T(8,128)(2,1)S(1)} %get-tuple-element.3), channel_id=1, source_target_pairs={{1,0},{2,1},{3,2},{4,3},{5,4},{6,5},{7,6},{8,7},{9,8},{10,9},{11,1... | collective-permute-start | bytes 983048 | tf_op jit(solution)/shard_map/ppermute | solution.py:18
  8.9 3.2 %copy-start.12 = (s32[16]{0:T(128)S(1)}, s32[16]{0:T(128)}, u32[]{:S(2)}) copy-start(s32[16]{0:T(128)} %param.21) | copy-start | bytes 196
  8.9 3.3 %copy-start.10 = (s32[16,3]{0,1:T(4,128)S(1)}, s32[16,3]{0,1:T(4,128)}, u32[]{:S(2)}) copy-start(s32[16,3]{0,1:T(4,128)} %param.20) | copy-start | bytes 580
  8.9 3.3 %copy-start.2 = (bf16[16,4,128,128]{3,2,1,0:T(8,128)(2,1)S(1)}, bf16[16,4,128,128]{3,2,1,0:T(8,128)(2,1)}, u32[]{:S(2)}) copy-start(bf16[16,4,128,128]{3,2,1,0:T(8,128)(2,1)} %param.19) | copy-start | bytes 6291460
  9.0 3.7 %copy-start.6 = (bf16[16,95,128]{2,0,1:T(8,128)(2,1)S(1)}, bf16[16,95,128]{2,0,1:T(8,128)(2,1)}, u32[]{:S(2)}) copy-start(bf16[16,95,128]{2,0,1:T(8,128)(2,1)} %param.12) | copy-start | bytes 1167364
  9.0 3.7 %copy-start.7 = (bf16[95,256]{1,0:T(8,128)(2,1)S(1)}, bf16[95,256]{1,0:T(8,128)(2,1)}, u32[]{:S(2)}) copy-start(bf16[95,256]{1,0:T(8,128)(2,1)} %param.16) | copy-start | bytes 145924
  17.1 13.9 %copy-start.1 = (bf16[10,256,642]{2,1,0:T(8,128)(2,1)}, bf16[10,256,642]{2,1,0:T(8,128)(2,1)S(1)}, u32[]{:S(2)}) copy-start(bf16[10,256,642]{2,1,0:T(8,128)(2,1)S(1)} %fusion.14) | copy-start | bytes 9861124
  40.6 17.7 %copy-start.8 = (bf16[256,16]{0,1:T(8,128)(2,1)S(1)}, bf16[256,16]{0,1:T(8,128)(2,1)}, u32[]{:S(2)}) copy-start(bf16[256,16]{0,1:T(8,128)(2,1)} %param.15) | copy-start | bytes 24580
  61.5 2.4 %copy-start.4 = (bf16[8,16,40,16]{3,2,1,0:T(8,128)(2,1)}, bf16[8,16,40,16]{3,2,1,0:T(8,128)(2,1)S(1)}, u32[]{:S(2)}) copy-start(bf16[8,16,40,16]{3,2,1,0:T(8,128)(2,1)S(1)} %reshape.26) | copy-start | bytes 491524
  61.7 8.6 %collective-permute-start.4 = (bf16[16,128]{1,0:T(8,128)(2,1)S(1)}, bf16[16,128]{1,0:T(8,128)(2,1)S(1)}, u32[]{:S(2)}, u32[]{:S(2)}) collective-permute-start(bf16[16,128]{1,0:T(8,128)(2,1)S(1)} %squeeze.39), channel_id=1, source_target_pairs={{0,1},{1,0},{2,3},{3,2},{4,5},{5,4},{6,7},{7,6},{8,9},{9,8},{10,11... | collective-permute-start | bytes 12296 | tf_op jit(solution)/shard_map/ppermute | solution.py:30
  64.0 26.2 %copy-start.3 = (bf16[16,4,128,128]{3,2,1,0:T(8,128)(2,1)S(1)}, bf16[16,4,128,128]{3,2,1,0:T(8,128)(2,1)}, u32[]{:S(2)}) copy-start(bf16[16,4,128,128]{3,2,1,0:T(8,128)(2,1)} %param.19) | copy-start | bytes 6291460
  64.0 26.2 %copy-start.9 = (bf16[16,256]{1,0:T(8,128)(2,1)S(1)}, bf16[16,256]{1,0:T(8,128)(2,1)}, u32[]{:S(2)}) copy-start(bf16[16,256]{1,0:T(8,128)(2,1)} %param.17) | copy-start | bytes 24580
  65.8 20.6 %collective-permute-start.2 = (bf16[1,40,16,128]{1,3,2,0:T(8,128)(2,1)S(1)}, bf16[1,40,16,128]{1,3,2,0:T(8,128)(2,1)}, u32[]{:S(2)}, u32[]{:S(2)}) collective-permute-start(bf16[1,40,16,128]{1,3,2,0:T(8,128)(2,1)S(1)} %bitcast.99), channel_id=1, source_target_pairs={{0,1},{1,2},{2,3},{3,4},{4,5},{5,6},{6,7},{7,8},{8,9},{9,10},{10,1... | collective-permute-start | bytes 491528 | tf_op jit(solution)/shard_map/ppermute | solution.py:15
  66.6 21.0 %collective-permute-start.3 = (bf16[1,40,16,128]{1,3,2,0:T(8,128)(2,1)S(1)}, bf16[1,40,16,128]{1,3,2,0:T(8,128)(2,1)}, u32[]{:S(2)}, u32[]{:S(2)}) collective-permute-start(bf16[1,40,16,128]{1,3,2,0:T(8,128)(2,1)S(1)} %bitcast.100), channel_id=1, source_target_pairs={{1,0},{2,1},{3,2},{4,3},{5,4},{6,5},{7,6},{8,7},{9,8},{10,9},{11,1... | collective-permute-start | bytes 491528 | tf_op jit(solution)/shard_map/ppermute | solution.py:18
  70.3 11.0 %collective-permute-start.5 = (bf16[16,128]{1,0:T(8,128)(2,1)S(1)}, bf16[16,128]{1,0:T(8,128)(2,1)S(1)}, u32[]{:S(2)}, u32[]{:S(2)}) collective-permute-start(bf16[16,128]{1,0:T(8,128)(2,1)S(1)} %collective-permute-done.4), channel_id=1, source_target_pairs={{0,2},{2,0},{1,3},{3,1},{4,6},{6,4},{5,7},{7,5},{8,10},{10,8},{9,1... | collective-permute-start | bytes 12296 | tf_op jit(solution)/shard_map/ppermute | solution.py:30
  81.4 3.6 %collective-permute-start.6 = (bf16[16,128]{1,0:T(8,128)(2,1)S(1)}, bf16[16,128]{1,0:T(8,128)(2,1)S(1)}, u32[]{:S(2)}, u32[]{:S(2)}) collective-permute-start(bf16[16,128]{1,0:T(8,128)(2,1)S(1)} %collective-permute-done.5), channel_id=1, source_target_pairs={{0,4},{4,0},{1,5},{5,1},{2,6},{6,2},{3,7},{7,3},{8,12},{12,8},{9,1... | collective-permute-start | bytes 12296 | tf_op jit(solution)/shard_map/ppermute | solution.py:30
  85.0 4.5 %collective-permute-start.7 = (bf16[16,128]{1,0:T(8,128)(2,1)S(1)}, bf16[16,128]{1,0:T(8,128)(2,1)S(1)}, u32[]{:S(2)}, u32[]{:S(2)}) collective-permute-start(bf16[16,128]{1,0:T(8,128)(2,1)S(1)} %collective-permute-done.6), channel_id=1, source_target_pairs={{0,8},{8,0},{1,9},{9,1},{2,10},{10,2},{3,11},{11,3},{4,12},{12,4},... | collective-permute-start | bytes 12296 | tf_op jit(solution)/shard_map/ppermute | solution.py:30
  90.2 3.6 %copy-start.11 = (bf16[256,256]{1,0:T(8,128)(2,1)S(1)}, bf16[256,256]{1,0:T(8,128)(2,1)}, u32[]{:S(2)}) copy-start(bf16[256,256]{1,0:T(8,128)(2,1)} %param.18) | copy-start | bytes 393220
where the time goes:
time: 97.8 us; the launch traced here: 97.5 us
  matrix products  57.3 us (59%)
  waiting for transfers between devices  14.4 us (15%)
  starting transfers between devices  14 us (14%)
  local copies, waits for them, and re-layouts  7.75 us (8%)
  other arithmetic  3.18 us (3%)
    dot_general x9, matrix products, per_device(): jnp.einsum('xcy,co->xoy', padded[shift_x:shift_x + columns, :, shift_y:sh...  44.4 us
    ppermute x4, waiting for transfers between devices, partner(): return lax.ppermute(block, axis, route)  14.4 us
    ppermute x2, starting transfers between devices, with_halo(): lax.ppermute(lax.slice_in_dim(block, 0, width, axis=dim), axis, backward)  8.73 us
    ppermute x4, starting transfers between devices, partner(): return lax.ppermute(block, axis, route)  3.87 us
    dot_general x1, matrix products, encode_ocean(): jnp.einsum('sho,hk->sko', base, mix_weight, preferred_element_type=jnp.fl...  3.67 us
    dot_general x1, matrix products, encode_ocean(): jnp.einsum('sfo,fh->sho', regrid, couple_weight, preferred_element_type=j...  3.6 us
    concatenate x2, other arithmetic, with_halo(): block = jnp.concatenate([low, block, high], axis=dim)  2.68 us
    dot_general x1, matrix products, per_device(): jnp.einsum('xhy,hf->xfy', atm_hidden, flux_weight, preferred_element_type...  2.19 us
  transfers between devices with their start and end apart: 8, of which 3 were waited for; matrix products, arithmetic and copies ran while one was open for 11% of the time, Pallas kernels for 0%

commit v1 on v0

v1 whole, which is shorter than its diff:
```python
import functools

import jax
import jax.numpy as jnp
from jax import lax
from jax.experimental import pallas as pl
from jax.experimental.pallas import tpu as pltpu
from jax.sharding import PartitionSpec as P

TLAT = 16
MAXACT = 8
FOLDB = 2
F32 = jnp.float32
BF16 = jnp.bfloat16
ROOT = 0.7978845608028654
CUBIC = ROOT * 0.044715

ANY = pl.BlockSpec(memory_space=pl.ANY)
VM = pl.BlockSpec(memory_space=pltpu.VMEM)
SM = pl.BlockSpec(memory_space=pltpu.SMEM)


def dot(a, b):
    return lax.dot_general(a, b, (((1,), (0,)), ((), ())), preferred_element_type=F32)


def dot_t(a, b):
    return lax.dot_general(a, b, (((1,), (1,)), ((), ())), preferred_element_type=F32)


def gelu(x):
    half = 0.5 * x
    return half + half * jnp.tanh(x * (ROOT + CUBIC * (x * x)))


def put_shifts(taps, row, column):
    chans, lats = column.shape
    wide = column.astype(F32)
    lane = lax.broadcasted_iota(jnp.int32, wide.shape, 1)
    south = jnp.where(lane == 0, 0.0, pltpu.roll(wide, 1, 1))
    north = jnp.where(lane == lats - 1, 0.0, pltpu.roll(wide, lats - 1, 1))
    taps[pl.ds(row, chans), :] = south.astype(BF16)
    taps[pl.ds(row + chans, chans), :] = column
    taps[pl.ds(row + 2 * chans, chans), :] = north.astype(BF16)


def encode_pair(taps, rows, w1_ref, w2_ref, fw, hid, slots, flux, fslots):
    width = hid.shape[1]
    lats = hid.shape[2]
    deep = w1_ref.shape[1]

    def window(which, part, lo, hi):
        return taps[pl.ds(rows[which] + part * deep, deep), lo:hi]

    pieces = []
    full = lats // 256 * 256
    for which in range(2):
        for lo in range(0, full, 256):
            pieces.append(((which, lo, lo + 256),))
    if full < lats:
        pieces.append(((0, full, lats), (1, full, lats)))
    for piece in pieces:
        first = [window(w, 0, lo, hi) for w, lo, hi in piece]
        second = [window(w, 1, lo, hi) for w, lo, hi in piece]
        first = first[0] if len(first) == 1 else jnp.concatenate(first, 1)
        second = second[0] if len(second) == 1 else jnp.concatenate(second, 1)
        both = dot(w1_ref[...], first)
        conv = both[:width] + dot(w2_ref[...], second)
        lifted = both[width:].astype(BF16).astype(F32)
        out = (lifted + gelu(conv)).astype(BF16)
        head = dot(fw, out).astype(BF16).astype(F32)
        at = 0
        for w, lo, hi in piece:
            hid[slots[w], :, lo:hi] = out[:, at : at + hi - lo]
            flux[fslots[w], :, lo:hi] = head[:, at : at + hi - lo]
            at += hi - lo


def inner_kernel(
    x_hbm, lift_hbm, conv_hbm, fw_hbm,
    hid_hbm, flux, w1, w2, fwt,
    x, lift, conv, fw, hid, taps, comp, sems,
):
    columns, chans, lats = x.shape
    width = lift.shape[1]
    copies = [
        pltpu.make_async_copy(lift_hbm, lift, sems.at[0]),
        pltpu.make_async_copy(x_hbm, x, sems.at[1]),
        pltpu.make_async_copy(fw_hbm, fw, sems.at[2]),
    ]
    for a in range(3):
        copies.append(pltpu.make_async_copy(conv_hbm.at[a], conv.at[a], sems.at[3 + a]))
    for c in copies:
        c.start()
    span = 3 * chans
    taps[pl.ds(columns * span, span), :] = jnp.zeros((span, lats), BF16)
    comp[pl.ds(9 * chans, 2 * width - 9 * chans), :] = jnp.zeros((2 * width - 9 * chans, width), F32)
    copies[1].wait()
    for i in range(columns):
        put_shifts(taps, i * span, x[i])
    copies[0].wait()
    liftv = lift[...]
    low = jnp.zeros((4 * chans, width), F32)
    high = jnp.zeros((width - 5 * chans, width), F32)
    place = jnp.concatenate([low, liftv.astype(F32), high], 0)
    w1[pl.ds(width, width), :] = place.T.astype(BF16)
    copies[2].wait()
    fwt[...] = fw[...].astype(F32).T.astype(BF16)
    for a in range(3):
        copies[3 + a].wait()
        for b in range(3):
            comp[pl.ds((3 * a + b) * chans, chans), :] = dot(liftv, conv[a, b])
    w1[pl.ds(0, width), :] = comp[pl.ds(0, width), :].T.astype(BF16)
    w2[...] = comp[pl.ds(width, width), :].T.astype(BF16)

    def pair(i, _):
        rows = [pl.multiple_of(2 * i * span, 16), pl.multiple_of((2 * i + 1) * span, 16)]
        encode_pair(taps, rows, w1, w2, fwt[...], hid, [2 * i, 2 * i + 1], flux, [2 * i + 1, 2 * i + 2])
        pltpu.make_async_copy(hid.at[pl.ds(2 * i, 2)], hid_hbm.at[pl.ds(2 * i + 1, 2)], sems.at[0]).start()
        return 0

    pairs = (columns - 2) // 2
    lax.fori_loop(0, pairs, pair, 0)
    pltpu.make_async_copy(hid, hid_hbm.at[pl.ds(1, 2 * pairs)], sems.at[0]).wait()


def interior(x, lift, conv, fw):
    columns, chans, lats = x.shape
    width = lift.shape[1]
    fluxes = fw.shape[1]
    return pl.pallas_call(
        inner_kernel,
        out_shape=(
            jax.ShapeDtypeStruct((columns, width, lats), BF16),
            jax.ShapeDtypeStruct((columns, fluxes, lats), F32),
            jax.ShapeDtypeStruct((2 * width, width), BF16),
            jax.ShapeDtypeStruct((width, width), BF16),
            jax.ShapeDtypeStruct((fluxes, width), BF16),
        ),
        in_specs=[ANY] * 4,
        out_specs=(ANY, VM, VM, VM, VM),
        scratch_shapes=[
            pltpu.VMEM((columns, chans, lats), BF16),
            pltpu.VMEM((chans, width), BF16),
            pltpu.VMEM((3, 3, width, width), BF16),
            pltpu.VMEM((width, fluxes), BF16),
            pltpu.VMEM((columns - 2, width, lats), BF16),
            pltpu.VMEM(((columns + 1) * 3 * chans, lats), BF16),
            pltpu.VMEM((2 * width, width), F32),
            pltpu.SemaphoreType.DMA((6,)),
        ],
        cost_estimate=pl.CostEstimate(flops=4 * 10**9, bytes_accessed=4 * 10**6, transcendentals=10**6),
        name="interior",
    )(x, lift, conv, fw)


def swap_blocks(values, lanes):
    count = len(values)
    lane = lax.broadcasted_iota(jnp.int32, values[0].shape, 1)
    step = count // 2
    while step:
        shift = step * TLAT
        upper = (lane & shift) != 0
        fresh = list(values)
        for i in range(count):
            if i & step:
                continue
            low, high = values[i], values[i + step]
            fresh[i] = jnp.where(upper, pltpu.roll(high, shift, 1), low)
            fresh[i + step] = jnp.where(upper, high, pltpu.roll(low, lanes - shift, 1))
        values = fresh
        step //= 2
    return values


def edge_kernel(x_hbm, west_hbm, east_hbm, flux_in, w1, w2, fwt, edges, tiles, north, x, taps, flux, sems):
    columns, chans, lats = x_hbm.shape
    span = 3 * chans
    copies = [
        pltpu.make_async_copy(x_hbm.at[pl.ds(0, 2)], x.at[pl.ds(1, 2)], sems.at[0]),
        pltpu.make_async_copy(x_hbm.at[pl.ds(columns - 2, 2)], x.at[pl.ds(3, 2)], sems.at[1]),
        pltpu.make_async_copy(west_hbm, x.at[pl.ds(0, 1)], sems.at[2]),
        pltpu.make_async_copy(east_hbm, x.at[pl.ds(5, 1)], sems.at[3]),
    ]
    for c in copies:
        c.start()
    taps[pl.ds(6 * span, span), :] = jnp.zeros((span, lats), BF16)
    copies[0].wait()
    put_shifts(taps, span, x[1])
    put_shifts(taps, 2 * span, x[2])
    copies[1].wait()
    put_shifts(taps, 3 * span, x[3])
    put_shifts(taps, 4 * span, x[4])
    copies[2].wait()
    put_shifts(taps, 0, x[0])
    copies[3].wait()
    put_shifts(taps, 5 * span, x[5])
    encode_pair(taps, [0, 3 * span], w1, w2, fwt[...], edges, [0, 1], flux, [0, 1])
    group = 128 // TLAT
    for g in range(lats // 128):
        at = slice(g * 128, g * 128 + 128)
        values = [flux[0, :, at]]
        values += [flux_in[i, :, at] for i in range(1, columns - 1)]
        values += [flux[1, :, at]]
        for a, v in enumerate(swap_blocks(values, 128)):
            tiles[g * group + a] = v.astype(BF16)
            if g == lats // 128 - 1 and a == group - 1:
                north[...] = v.astype(BF16)


def edge(x, west, east, flux_in, w1, w2, fwt):
    columns, chans, lats = x.shape
    width = w2.shape[0]
    fluxes = fwt.shape[0]
    cells = columns * TLAT
    return pl.pallas_call(
        edge_kernel,
        out_shape=(
            jax.ShapeDtypeStruct((2, width, lats), BF16),
            jax.ShapeDtypeStruct((lats // TLAT, fluxes, cells), BF16),
            jax.ShapeDtypeStruct((fluxes, cells), BF16),
        ),
        in_specs=[ANY, ANY, ANY, VM, VM, VM, VM],
        out_specs=(VM, VM, VM),
        scratch_shapes=[
            pltpu.VMEM((6, chans, lats), BF16),
            pltpu.VMEM((7 * 3 * chans, lats), BF16),
            pltpu.VMEM((2, fluxes, lats), F32),
            pltpu.SemaphoreType.DMA((4,)),
        ],
        cost_estimate=pl.CostEstimate(flops=10**9, bytes_accessed=10**6, transcendentals=3 * 10**5),
        name="edge",
    )(x, west, east, flux_in, w1, w2, fwt)


def list_tiles(mask, chosen, count):
    for k in range(MAXACT):
        chosen[k] = count - 1
    for k in range(FOLDB):
        chosen[k] = count - FOLDB + k
    found = FOLDB
    for t in range(count - FOLDB):
        water = mask[t] == 1

        @pl.when(jnp.logical_and(water, found < MAXACT))
        def _():
            chosen[found] = t

        found = found + water.astype(jnp.int32)
    return found


def early_kernel(
    hid_in, edges, pair, mask, tiles, ocean_hbm, regrid_hbm, ow_hbm, cw_hbm, mw_hbm,
    hid_out, blocks, sums, base, cwt, mwt,
    ocean, ow, cw, mw, chosen, sems,
):
    count = ocean_hbm.shape[0]
    columns = hid_in.shape[0]
    small = [
        pltpu.make_async_copy(ow_hbm, ow, sems.at[0]),
        pltpu.make_async_copy(cw_hbm, cw, sems.at[1]),
        pltpu.make_async_copy(mw_hbm, mw, sems.at[2]),
    ]
    out = [
        pltpu.make_async_copy(edges.at[0], hid_out.at[0], sems.at[3]),
        pltpu.make_async_copy(edges.at[1], hid_out.at[columns - 1], sems.at[4]),
    ]
    for c in small:
        c.start()
    list_tiles(mask, chosen, count)
    loads = []
    for k in range(MAXACT):
        t = chosen[k]
        loads.append(
            (
                pltpu.make_async_copy(ocean_hbm.at[t], ocean.at[k], sems.at[5 + 2 * k]),
                pltpu.make_async_copy(regrid_hbm.at[t], blocks.at[k], sems.at[6 + 2 * k]),
            )
        )
        for c in loads[-1]:
            c.start()
    for c in out:
        c.start()
    for c in small:
        c.wait()
    cwt[...] = cw[...].astype(F32).T.astype(BF16)
    mwt[...] = mw[...].astype(F32).T.astype(BF16)
    owt = ow[...].astype(F32).T.astype(BF16)
    ones = jnp.ones(tiles.shape[1:], BF16)
    for k in range(MAXACT):
        for c in loads[k]:
            c.wait()
        mine = jnp.concatenate([tiles[pair[chosen[k], 1]], ones], 0)
        sums[k] = dot_t(mine, blocks[k, 1])
        base[k] = dot(owt, ocean[k])
    for c in out:
        c.wait()


def early(hid, edges, pair, mask, tiles, ocean, regrid, ow, cw, mw):
    count, chans, cells = ocean.shape
    width = mw.shape[0]
    fluxes = cw.shape[0]
    pairs = regrid.shape[1]
    return pl.pallas_call(
        early_kernel,
        out_shape=(
            jax.ShapeDtypeStruct(hid.shape, BF16),
            jax.ShapeDtypeStruct((MAXACT,) + regrid.shape[1:], BF16),
            jax.ShapeDtypeStruct((MAXACT, 2 * fluxes, cells), F32),
            jax.ShapeDtypeStruct((MAXACT, width, cells), F32),
            jax.ShapeDtypeStruct((width, fluxes), BF16),
            jax.ShapeDtypeStruct((width, width), BF16),
        ),
        in_specs=[ANY, VM, SM, SM, VM, ANY, ANY, ANY, ANY, ANY],
        out_specs=(ANY, VM, VM, VM, VM, VM),
        scratch_shapes=[
            pltpu.VMEM((MAXACT, chans, cells), BF16),
            pltpu.VMEM(ow.shape, BF16),
            pltpu.VMEM(cw.shape, BF16),
            pltpu.VMEM(mw.shape, BF16),
            pltpu.SMEM((MAXACT,), jnp.int32),
            pltpu.SemaphoreType.DMA((5 + 2 * MAXACT,)),
        ],
        input_output_aliases={0: 0},
        cost_estimate=pl.CostEstimate(flops=10**9, bytes_accessed=3 * 10**6, transcendentals=0),
        name="early",
    )(hid, edges, pair, mask, tiles, ocean, regrid, ow, cw, mw)


def late_kernel(
    pair, mask, west, east, fold, blocks, sums, base, cwt, mwt,
    out_hbm,
    out, zero, chosen, sems,
):
    count = out_hbm.shape[0]
    fluxes = fold.shape[0]
    zero[...] = jnp.zeros(zero.shape, BF16)
    for t in range(count - FOLDB):

        @pl.when(mask[t] != 1)
        def _():
            pltpu.make_async_copy(zero, out_hbm.at[t], sems.at[0]).start()

    found = list_tiles(mask, chosen, count)
    ones = jnp.ones(fold.shape, BF16)
    for k in range(MAXACT):
        t = chosen[k]
        total = sums[k]
        total = total + dot_t(jnp.concatenate([west[pair[t, 0]], ones], 0), blocks[k, 0])
        total = total + dot_t(jnp.concatenate([east[pair[t, 2]], ones], 0), blocks[k, 2])
        if k < FOLDB:
            total = total + dot_t(jnp.concatenate([fold[...], ones], 0), blocks[k, 3])
        regrid = (total[:fluxes] / total[fluxes : fluxes + 1]).astype(BF16)
        state = (base[k] + dot(cwt[...], regrid)).astype(BF16)
        mixed = dot(mwt[...], state)
        out[k] = (state.astype(F32) + gelu(mixed)).astype(BF16)

        @pl.when(k < found)
        def _():
            pltpu.make_async_copy(out.at[k], out_hbm.at[t], sems.at[1]).start()

    for t in range(count - FOLDB):

        @pl.when(mask[t] != 1)
        def _():
            pltpu.make_async_copy(zero, out_hbm.at[t], sems.at[0]).wait()

    for k in range(MAXACT):

        @pl.when(k < found)
        def _():
            pltpu.make_async_copy(out.at[k], out_hbm.at[0], sems.at[1]).wait()


def late(pair, mask, west, east, fold, blocks, sums, base, cwt, mwt):
    count = mask.shape[0]
    width, cells = base.shape[1:]
    return pl.pallas_call(
        late_kernel,
        out_shape=jax.ShapeDtypeStruct((count, width, cells), BF16),
        in_specs=[SM, SM, VM, VM, VM, VM, VM, VM, VM, VM],
        out_specs=ANY,
        scratch_shapes=[
            pltpu.VMEM((MAXACT, width, cells), BF16),
            pltpu.VMEM((width, cells), BF16),
            pltpu.SMEM((MAXACT,), jnp.int32),
            pltpu.SemaphoreType.DMA((2,)),
        ],
        cost_estimate=pl.CostEstimate(flops=10**9, bytes_accessed=10**6, transcendentals=3 * 10**5),
        name="late",
    )(pair, mask, west, east, fold, blocks, sums, base, cwt, mwt)


def per_device(
    atm_in,
    ocean_in,
    lift_weight,
    conv_weight,
    flux_weight,
    ocean_weight,
    couple_weight,
    mix_weight,
    regrid_weight,
    pair_tile,
    ocean_mask,
):
    columns = atm_in.shape[0]
    strips = lax.axis_size("lon")
    forward = [(i, (i + 1) % strips) for i in range(strips)]
    backward = [((i + 1) % strips, i) for i in range(strips)]
    mirror = [(i, strips - 1 - i) for i in range(strips)]
    west = lax.ppermute(atm_in[columns - 1 :], "lon", forward)
    east = lax.ppermute(atm_in[:1], "lon", backward)
    hid, flux, w1, w2, fwt = interior(atm_in, lift_weight, conv_weight, flux_weight)
    edges, tiles, north = edge(atm_in, west, east, flux, w1, w2, fwt)
    tiles_west = lax.ppermute(tiles, "lon", forward)
    tiles_east = lax.ppermute(tiles, "lon", backward)
    fold = lax.ppermute(north, "lon", mirror)
    atm_hidden, blocks, sums, base, cwt, mwt = early(
        hid, edges, pair_tile, ocean_mask, tiles, ocean_in, regrid_weight,
        ocean_weight, couple_weight, mix_weight,
    )
    ocean_hidden = late(
        pair_tile, ocean_mask, tiles_west, tiles_east, fold, blocks, sums, base, cwt, mwt
    )
    return (atm_hidden, ocean_hidden)


def solution(mesh):
    in_specs = (
        P(("groups", "lon"), None, None),
        P(("groups", "lon"), None, None),
        P(),
        P(),
        P(),
        P(),
        P(),
        P(),
        P("lon", None, None, None),
        P("lon", None),
        P("lon"),
    )
    out_specs = (P(("groups", "lon"), None, None), P(("groups", "lon"), None, None))
    return jax.shard_map(
        per_device, mesh=mesh, in_specs=in_specs, out_specs=out_specs, check_vma=False
    )
```

time: 97.8 us -> 41.8 us (0.43)
  matrix products: 57.3 us -> 0 us
  Pallas kernels: 0 us -> 24.8 us
  waiting for transfers between devices: 14.4 us -> 0.63 us
  starting transfers between devices: 14 us -> 10.1 us
  other arithmetic: 3.18 us -> 0 us
  local copies, waits for them, and re-layouts: 7.75 us -> 5.17 us
    dot_general x14 -> x0, matrix products: 57.3 us -> none  [the longest x9 44.4 us: per_device(): jnp.einsum('xcy,co->xoy', padded[shift_x:shift_x + columns, :, shift_y:sh...]
    pallas_call x0 -> x4, Pallas kernels: none -> 24.8 us  [the longest x1 9.92 us: interior(): pl.pallas_call(inner_kernel, out_shape=(jax.ShapeDtypeStruct((columns, wi...]
    ppermute x8 -> x5, waiting for transfers between devices: 14.4 us -> 0.63 us  [the longest x1 0.62 us: per_device(): fold = lax.ppermute(north, 'lon', mirror)]
    ppermute x8 -> x5, starting transfers between devices: 14 us -> 10.1 us  [the longest x1 5.05 us: per_device(): east = lax.ppermute(atm_in[:1], 'lon', backward)]
    unnamed x26 -> x17, local copies, waits for them, and re-layouts: 1.08 us -> 4.29 us
    concatenate x3 -> x0, other arithmetic: 2.73 us -> none  [the longest x2 2.68 us: with_halo(): block = jnp.concatenate([low, block, high], axis=dim)]
    ppermute x2 -> x0, local copies, waits for them, and re-layouts: 2.54 us -> none  [the longest x1 1.27 us: with_halo(): lax.ppermute(lax.slice_in_dim(block, 0, width, axis=dim), axis, backward)]
    transpose x1 -> x0, local copies, waits for them, and re-layouts: 1.8 us -> none  [per_device(): tiles = flux.reshape(columns, flux_count, tiles_lat, TLAT).transpose(2, 1...]
  transfers between devices with their start and end apart: 8 -> 5, of which waited for: 3 -> 1; matrix products, arithmetic and copies ran while one was open for 11% -> 7% of each run, Pallas kernels for 0% -> 37%
where the time goes in v1:
time: 41.8 us; the launch traced here: 41.5 us
  Pallas kernels  24.8 us (59%)
  starting transfers between devices  10.1 us (24%)
  local copies, waits for them, and re-layouts  5.17 us (12%)
  between operations  0.73 us (2%)
  waiting for transfers between devices  0.63 us (2%)
    pallas_call x1, Pallas kernels, interior(): pl.pallas_call(inner_kernel, out_shape=(jax.ShapeDtypeStruct((columns, wi...  9.92 us
    pallas_call x1, Pallas kernels, early(): pl.pallas_call(early_kernel, out_shape=(jax.ShapeDtypeStruct(hid.shape, B...  5.31 us
    pallas_call x1, Pallas kernels, edge(): pl.pallas_call(edge_kernel, out_shape=(jax.ShapeDtypeStruct((2, width, la...  5.29 us
    ppermute x1, starting transfers between devices, per_device(): east = lax.ppermute(atm_in[:1], 'lon', backward)  5.05 us
    ppermute x1, starting transfers between devices, per_device(): tiles_east = lax.ppermute(tiles, 'lon', backward)  4.43 us
    pallas_call x1, Pallas kernels, late(): pl.pallas_call(late_kernel, out_shape=jax.ShapeDtypeStruct((count, width,...  4.33 us
    unnamed x17, local copies, waits for them, and re-layouts  4.29 us
    slice x1, local copies, waits for them, and re-layouts, per_device(): east = lax.ppermute(atm_in[:1], 'lon', backward)  0.87 us
  transfers between devices with their start and end apart: 5, of which 1 were waited for; matrix products, arithmetic and copies ran while one was open for 7% of the time, Pallas kernels for 37%

profile of v1, /device:TPU:0, one launch (start us, length us, event | category | flops | bytes accessed | tf_op | source)
XLA Modules:
  0.0 41.5 jit_solution(675284545695220126)
XLA Ops:
  0.6 0.9 %fusion = (bf16[1,48,640]{2,1,0:T(8,128)(2,1)S(1)}, bf16[1,48,640]{2,1,0:T(8,128)(2,1)S(1)}) fusion(bf16[8,48,640]{2,1,0:T(8,128)(2,1)} %x_hbm.3), kind=kLoop, calls=%fused_computation | loop fusion | bytes 245760 | tf_op jit(solution)/shard_map/slice | solution.py:415
  1.5 0.5 %collective-permute-start = (bf16[1,48,640]{2,1,0:T(8,128)(2,1)S(1)}, bf16[1,48,640]{2,1,0:T(8,128)(2,1)S(1)}, u32[]{:S(2)}, u32[]{:S(2)}) collective-permute-start(bf16[1,48,640]{2,1,0:T(8,128)(2,1)S(1)} %get-tuple-element.31), channel_id=1, source_target_pairs={{0,1},{1,2},{2,3},{3,4},{4,5},{5,6},{6,7},{7,8},{8,9},{9,10},{10,1... | collective-permute-start | bytes 184328 | tf_op jit(solution)/shard_map/ppermute | solution.py:414
  2.0 5.0 %collective-permute-start.1 = (bf16[1,48,640]{2,1,0:T(8,128)(2,1)S(1)}, bf16[1,48,640]{2,1,0:T(8,128)(2,1)S(1)}, u32[]{:S(2)}, u32[]{:S(2)}) collective-permute-start(bf16[1,48,640]{2,1,0:T(8,128)(2,1)S(1)} %get-tuple-element.30), channel_id=1, source_target_pairs={{1,0},{2,1},{3,2},{4,3},{5,4},{6,5},{7,6},{8,7},{9,8},{10,9},{11,1... | collective-permute-start | bytes 184328 | tf_op jit(solution)/shard_map/ppermute | solution.py:415
  7.1 1.4 %copy.14.fw_hbm = bf16[256,16]{1,0:T(8,128)(2,1)} copy(bf16[256,16]{0,1:T(8,128)(2,1)} %param.15) | data formatting | bytes 16384 | tf_op args[4]
  8.5 9.9 %interior.1 = (bf16[8,256,640]{2,1,0:T(8,128)(2,1)}, f32[8,16,640]{2,1,0:T(8,128)}, bf16[512,256]{1,0:T(8,128)(2,1)}, bf16[256,256]{1,0:T(8,128)(2,1)}, bf16[16,256]{1,0:T(8,128)(2,1)}) custom-call(bf16[8,48,640]{2,1,0:T(8,128)(2,1)} %x_hbm.3, bf16[48,256]{1,0:T(8,128)(2,1)} %lift_hbm.1, bf16[3,3,256,256]{3,2,1,0:T(8,128)(2,1)} %conv_hbm.1, ...), custom_call_target="tpu_custom_call" | custom-call | flops 4000000000 | bytes 4000000 | tf_op jit(solution)/shard_map/interior/pallas_call | solution.py:131
  18.5 0.0 copy-start.4
  18.5 0.0 copy-start
  18.5 0.0 collective-permute-done.west_hbm
  18.5 0.0 copy-start.5
  18.5 0.0 collective-permute-done.1.east_hbm
  18.5 0.0 copy-start.6
  18.5 0.6 %copy-done.5 = bf16[1,48,640]{2,1,0:T(8,128)(2,1)} copy-done((bf16[1,48,640]{2,1,0:T(8,128)(2,1)}, bf16[1,48,640]{2,1,0:T(8,128)(2,1)S(1)}, u32[]{:S(2)}) %copy-start.5) | copy-done | bytes 61464
  19.1 0.0 copy-done.6
  19.1 5.3 %edge.1 = (bf16[2,256,640]{2,1,0:T(8,128)(2,1)}, bf16[40,16,128]{2,1,0:T(8,128)(2,1)}, bf16[16,128]{1,0:T(8,128)(2,1)}) custom-call(bf16[8,48,640]{2,1,0:T(8,128)(2,1)} %x_hbm.3, bf16[1,48,640]{2,1,0:T(8,128)(2,1)} %copy-done.5, bf16[1,48,640]{2,1,0:T(8,128)(2,1)} %copy-done.6, f32[8,16,640]{2,1,0:T(8,128)} %get-tuple-element.17.flux_in, ...), custom_call_target="tpu_custom_call" | custom-call | flops 1000000000 | bytes 1000000 | tf_op jit(solution)/shard_map/edge/pallas_call | solution.py:216
  24.4 0.1 collective-permute-start.2
  24.5 4.4 %collective-permute-start.3 = (bf16[40,16,128]{2,1,0:T(8,128)(2,1)}, bf16[40,16,128]{2,1,0:T(8,128)(2,1)S(1)}, u32[]{:S(2)}, u32[]{:S(2)}) collective-permute-start(bf16[40,16,128]{2,1,0:T(8,128)(2,1)} %get-tuple-element.22.tiles), channel_id=1, source_target_pairs={{1,0},{2,1},{3,2},{4,3},{5,4},{6,5},{7,6},{8,7},{9,8},{10,9},{11,1... | collective-permute-start | bytes 491528 | tf_op jit(solution)/shard_map/ppermute | solution.py:419
  28.9 0.0 copy-done.4
  28.9 0.7 %copy.15.pair = s32[16,3]{1,0:T(8,128)} copy(s32[16,3]{0,1:T(4,128)S(1)} %copy-done.4) | data formatting | bytes 384 | tf_op args[9]
  29.6 0.0 copy-done
  29.6 0.8 %copy.16.ocean_hbm = bf16[16,95,128]{2,1,0:T(8,128)(2,1)} copy(bf16[16,95,128]{2,0,1:T(8,128)(2,1)S(1)} %copy-done) | data formatting | bytes 778240 | tf_op args[1]
  30.5 0.0 collective-permute-start.4
  30.5 5.3 %early.1 = (bf16[8,256,640]{2,1,0:T(8,128)(2,1)}, bf16[8,4,128,128]{3,2,1,0:T(8,128)(2,1)}, f32[8,32,128]{2,1,0:T(8,128)}, f32[8,256,128]{2,1,0:T(8,128)}, bf16[...) custom-call(bf16[8,256,640]{2,1,0:T(8,128)(2,1)} %get-tuple-element.16.hid_in, ...), custom_call_target="tpu_custom_call", output_to_operand_aliasing={{0}: (0, {})} | custom-call | flops 1000000000 | bytes 3000000 | tf_op jit(solution)/shard_map/early/pallas_call | solution.py:306
  35.8 0.6 %collective-permute-done.4.fold = bf16[16,128]{1,0:T(8,128)(2,1)S(1)} collective-permute-done((bf16[16,128]{1,0:T(8,128)(2,1)}, bf16[16,128]{1,0:T(8,128)(2,1)S(1)}, u32[]{:S(2)}, u32[]{:S(2)}) %collective-permute-start.4) | collective-permute-done | bytes 4128 | tf_op jit(solution)/shard_map/ppermute | solution.py:420
  36.4 0.0 copy-start.3
  36.4 0.0 collective-permute-done.2.west
  36.4 0.0 copy-start.1
  36.4 0.0 collective-permute-done.3.east
  36.4 0.0 copy-start.2
  36.4 0.6 %copy-done.3 = bf16[16,128]{1,0:T(8,128)(2,1)} copy-done((bf16[16,128]{1,0:T(8,128)(2,1)}, bf16[16,128]{1,0:T(8,128)(2,1)S(1)}, u32[]{:S(2)}) %copy-start.3) | copy-done | bytes 4120
  37.0 0.1 copy-done.1
  37.1 0.1 copy-done.2
  37.1 4.3 %late.1 = bf16[16,256,128]{2,1,0:T(8,128)(2,1)} custom-call(s32[16,3]{1,0:T(8,128)} %copy.15.pair, s32[16]{0:T(128)} %mask.3, bf16[40,16,128]{2,1,0:T(8,128)(2,1)} %copy-done.1, bf16[40,16,128]{2,1,0:T(8,128)(2,1)} %copy-done.2, bf16[16,128]{1,0:T(8,128)(2,1)} %copy-done.3, bf16[8,4,128,128]{3,2,1,0:T(8,128)(2,1)} %get-tuple-element.25.blocks, ...), custom_call_target="tpu_custom_call" | custom-call | flops 1000000000 | bytes 1000000 | tf_op jit(solution)/shard_map/late/pallas_call | solution.py:380
Async XLA Ops:
  1.5 17.0 %collective-permute-start = (bf16[1,48,640]{2,1,0:T(8,128)(2,1)S(1)}, bf16[1,48,640]{2,1,0:T(8,128)(2,1)S(1)}, u32[]{:S(2)}, u32[]{:S(2)}) collective-permute-start(bf16[1,48,640]{2,1,0:T(8,128)(2,1)S(1)} %get-tuple-element.31), channel_id=1, source_target_pairs={{0,1},{1,2},{2,3},{3,4},{4,5},{5,6},{6,7},{7,8},{8,9},{9,10},{10,1... | collective-permute-start | bytes 184328 | tf_op jit(solution)/shard_map/ppermute | solution.py:414
  2.0 16.5 %collective-permute-start.1 = (bf16[1,48,640]{2,1,0:T(8,128)(2,1)S(1)}, bf16[1,48,640]{2,1,0:T(8,128)(2,1)S(1)}, u32[]{:S(2)}, u32[]{:S(2)}) collective-permute-start(bf16[1,48,640]{2,1,0:T(8,128)(2,1)S(1)} %get-tuple-element.30), channel_id=1, source_target_pairs={{1,0},{2,1},{3,2},{4,3},{5,4},{6,5},{7,6},{8,7},{9,8},{10,9},{11,1... | collective-permute-start | bytes 184328 | tf_op jit(solution)/shard_map/ppermute | solution.py:415
  18.5 10.5 %copy-start.4 = (s32[16,3]{0,1:T(4,128)S(1)}, s32[16,3]{0,1:T(4,128)}, u32[]{:S(2)}) copy-start(s32[16,3]{0,1:T(4,128)} %param.20) | copy-start | bytes 580
  18.5 11.1 %copy-start = (bf16[16,95,128]{2,0,1:T(8,128)(2,1)S(1)}, bf16[16,95,128]{2,0,1:T(8,128)(2,1)}, u32[]{:S(2)}) copy-start(bf16[16,95,128]{2,0,1:T(8,128)(2,1)} %param.12) | copy-start | bytes 1167364
  18.5 0.6 %copy-start.5 = (bf16[1,48,640]{2,1,0:T(8,128)(2,1)}, bf16[1,48,640]{2,1,0:T(8,128)(2,1)S(1)}, u32[]{:S(2)}) copy-start(bf16[1,48,640]{2,1,0:T(8,128)(2,1)S(1)} %collective-permute-done.west_hbm) | copy-start | bytes 184324
  18.5 0.6 %copy-start.6 = (bf16[1,48,640]{2,1,0:T(8,128)(2,1)}, bf16[1,48,640]{2,1,0:T(8,128)(2,1)S(1)}, u32[]{:S(2)}) copy-start(bf16[1,48,640]{2,1,0:T(8,128)(2,1)S(1)} %collective-permute-done.1.east_hbm) | copy-start | bytes 184324
  24.4 12.0 %collective-permute-start.2 = (bf16[40,16,128]{2,1,0:T(8,128)(2,1)}, bf16[40,16,128]{2,1,0:T(8,128)(2,1)S(1)}, u32[]{:S(2)}, u32[]{:S(2)}) collective-permute-start(bf16[40,16,128]{2,1,0:T(8,128)(2,1)} %get-tuple-element.22.tiles), channel_id=1, source_target_pairs={{0,1},{1,2},{2,3},{3,4},{4,5},{5,6},{6,7},{7,8},{8,9},{9,10},{10,1... | collective-permute-start | bytes 491528 | tf_op jit(solution)/shard_map/ppermute | solution.py:418
  24.5 11.9 %collective-permute-start.3 = (bf16[40,16,128]{2,1,0:T(8,128)(2,1)}, bf16[40,16,128]{2,1,0:T(8,128)(2,1)S(1)}, u32[]{:S(2)}, u32[]{:S(2)}) collective-permute-start(bf16[40,16,128]{2,1,0:T(8,128)(2,1)} %get-tuple-element.22.tiles), channel_id=1, source_target_pairs={{1,0},{2,1},{3,2},{4,3},{5,4},{6,5},{7,6},{8,7},{9,8},{10,9},{11,1... | collective-permute-start | bytes 491528 | tf_op jit(solution)/shard_map/ppermute | solution.py:419
  30.5 5.9 %collective-permute-start.4 = (bf16[16,128]{1,0:T(8,128)(2,1)}, bf16[16,128]{1,0:T(8,128)(2,1)S(1)}, u32[]{:S(2)}, u32[]{:S(2)}) collective-permute-start(bf16[16,128]{1,0:T(8,128)(2,1)} %get-tuple-element.24), channel_id=1, source_target_pairs={{0,15},{1,14},{2,13},{3,12},{4,11},{5,10},{6,9},{7,8},{8,7},{9,6},... | collective-permute-start | bytes 12296 | tf_op jit(solution)/shard_map/ppermute | solution.py:420
  36.4 0.6 %copy-start.3 = (bf16[16,128]{1,0:T(8,128)(2,1)}, bf16[16,128]{1,0:T(8,128)(2,1)S(1)}, u32[]{:S(2)}) copy-start(bf16[16,128]{1,0:T(8,128)(2,1)S(1)} %collective-permute-done.4.fold) | copy-start | bytes 12292
  36.4 0.7 %copy-start.1 = (bf16[40,16,128]{2,1,0:T(8,128)(2,1)}, bf16[40,16,128]{2,1,0:T(8,128)(2,1)S(1)}, u32[]{:S(2)}) copy-start(bf16[40,16,128]{2,1,0:T(8,128)(2,1)S(1)} %collective-permute-done.2.west) | copy-start | bytes 491524
  36.4 0.7 %copy-start.2 = (bf16[40,16,128]{2,1,0:T(8,128)(2,1)}, bf16[40,16,128]{2,1,0:T(8,128)(2,1)S(1)}, u32[]{:S(2)}) copy-start(bf16[40,16,128]{2,1,0:T(8,128)(2,1)S(1)} %collective-permute-done.3.east) | copy-start | bytes 491524

commit v2 on v1

v2 whole, which is shorter than its diff:
```python
import functools

import jax
import jax.numpy as jnp
from jax import lax
from jax.experimental import pallas as pl
from jax.experimental.pallas import tpu as pltpu
from jax.sharding import PartitionSpec as P

TLAT = 16
MAXACT = 8
FOLDB = 2
F32 = jnp.float32
BF16 = jnp.bfloat16
ROOT = 0.7978845608028654
CUBIC = ROOT * 0.044715

CHUNK = 256
STRIP = 32

HBM = pl.BlockSpec(memory_space=pltpu.HBM)
VM = pl.BlockSpec(memory_space=pltpu.VMEM)
SM = pl.BlockSpec(memory_space=pltpu.SMEM)


def dot(a, b):
    return lax.dot_general(a, b, (((1,), (0,)), ((), ())), preferred_element_type=F32)


def dot_t(a, b):
    return lax.dot_general(a, b, (((1,), (1,)), ((), ())), preferred_element_type=F32)


def gelu(x):
    half = 0.5 * x
    return half + half * jnp.tanh(x * (ROOT + CUBIC * (x * x)))


def put_shifts(taps, at, column):
    chans, lats = column.shape
    wide = column.astype(F32)
    lane = lax.broadcasted_iota(jnp.int32, wide.shape, 1)
    south = jnp.where(lane == 0, 0.0, pltpu.roll(wide, 1, 1))
    north = jnp.where(lane == lats - 1, 0.0, pltpu.roll(wide, lats - 1, 1))
    taps[:chans, at : at + lats] = south.astype(BF16)
    taps[chans : 2 * chans, at : at + lats] = column
    taps[2 * chans :, at : at + lats] = north.astype(BF16)


def join(parts, axis):
    return parts[0] if len(parts) == 1 else jnp.concatenate(parts, axis)


def multiply(segments, wc, lt, conv, lifted):
    chans = lt.shape[1]
    rows = 3 * chans
    parts = []
    for a in range(3):
        parts.append(join([seg[a][0][:, pl.ds(seg[a][1], seg[3])] for seg in segments], 1))
    parts.append(jnp.zeros((wc.shape[1] - 3 * rows, parts[0].shape[1]), BF16))
    own = join([seg[1][0][chans : 2 * chans, pl.ds(seg[1][1], seg[3])] for seg in segments], 1)
    conv[...] = dot(wc[...], jnp.concatenate(parts, 0))
    lifted[...] = dot(lt[...], own).astype(BF16)


def activate(conv, lifted, out, stores):
    for r in range(0, conv.shape[0], STRIP):
        at = slice(r, r + STRIP)
        fresh = (lifted[at, :].astype(F32) + gelu(conv[at, :])).astype(BF16)
        out[at, :] = fresh
        for ref, first, lo, hi in stores:
            ref[at, pl.ds(first, hi - lo)] = fresh[:, lo:hi]


def inner_kernel(
    x_hbm, lift_hbm, conv_hbm, fwt_hbm,
    hid_hbm, flux, taps, wc, lt,
    x, lift, conv, fwt, hid, comp, ca, cb, la, lb, oa, ob, sems,
):
    columns, chans, lats = x.shape
    width = lift.shape[1]
    copies = [
        pltpu.make_async_copy(x_hbm, x, sems.at[0]),
        pltpu.make_async_copy(lift_hbm, lift, sems.at[1]),
        pltpu.make_async_copy(fwt_hbm, fwt, sems.at[2]),
    ]
    for a in range(3):
        copies.append(pltpu.make_async_copy(conv_hbm.at[a], conv.at[a], sems.at[3 + a]))
    for c in copies:
        c.start()
    comp[pl.ds(9 * chans, 2 * width - 9 * chans), :] = jnp.zeros((2 * width - 9 * chans, width), F32)
    copies[0].wait()
    for i in range(columns):
        put_shifts(taps, i * lats, x[i])
    copies[1].wait()
    lt[...] = lift[...].astype(F32).T.astype(BF16)
    for a in range(3):
        copies[3 + a].wait()
        for b in range(3):
            comp[pl.ds((3 * a + b) * chans, chans), :] = dot(lift[...], conv[a, b])
    wc[...] = comp[...].T.astype(BF16)
    copies[2].wait()

    def feed(j, conv_to, lifted_to):
        at = [pl.multiple_of(j * CHUNK + a * lats, 128) for a in range(3)]
        multiply([[(taps, p) for p in at] + [CHUNK]], wc, lt, conv_to, lifted_to)

    def finish(j, conv_of, lifted_of, out):
        activate(conv_of, lifted_of, out, [(hid, pl.multiple_of(j * CHUNK, 128), 0, CHUNK)])

    def head(j, out):
        flux[:, pl.ds(pl.multiple_of(j * CHUNK, 128), CHUNK)] = dot(fwt[...], out[...])

    def send(column):
        return pltpu.make_async_copy(
            hid.at[:, pl.ds(pl.multiple_of(column * lats, 128), lats)], hid_hbm.at[column + 1], sems.at[0]
        )

    chunks = (columns - 2) * lats // CHUNK
    feed(0, ca, la)

    def two(i, _):
        j = 2 * i
        feed(j + 1, cb, lb)
        finish(j, ca, la, oa)
        head(jnp.maximum(j - 1, 0), ob)
        feed(jnp.minimum(j + 2, chunks - 1), ca, la)
        finish(j + 1, cb, lb, ob)
        head(j, oa)
        before = j * CHUNK // lats

        @pl.when((j + 2) * CHUNK // lats > before)
        def _():
            send(before).start()

        return 0

    lax.fori_loop(0, chunks // 2, two, 0)
    head(chunks // 2 * 2 - 1, ob)
    if chunks % 2:
        finish(chunks - 1, ca, la, oa)
        head(chunks - 1, oa)
        send(columns - 3).start()
    for i in range(columns - 2):
        send(i).wait()


def interior(x, lift, conv, fwt):
    columns, chans, lats = x.shape
    width = lift.shape[1]
    fluxes = fwt.shape[0]
    inner = (columns - 2) * lats
    x, lift, conv, fwt = [
        pltpu.with_memory_space_constraint(v, pltpu.HBM) for v in (x, lift, conv, fwt)
    ]
    return pl.pallas_call(
        inner_kernel,
        out_shape=(
            jax.ShapeDtypeStruct((columns, width, lats), BF16),
            jax.ShapeDtypeStruct((fluxes, inner), F32),
            jax.ShapeDtypeStruct((3 * chans, columns * lats), BF16),
            jax.ShapeDtypeStruct((width, 2 * width), BF16),
            jax.ShapeDtypeStruct((width, chans), BF16),
        ),
        in_specs=[HBM] * 4,
        out_specs=(HBM, VM, VM, VM, VM),
        scratch_shapes=[
            pltpu.VMEM((columns, chans, lats), BF16),
            pltpu.VMEM((chans, width), BF16),
            pltpu.VMEM((3, 3, width, width), BF16),
            pltpu.VMEM((fluxes, width), BF16),
            pltpu.VMEM((width, inner), BF16),
            pltpu.VMEM((2 * width, width), F32),
            pltpu.VMEM((width, CHUNK), F32),
            pltpu.VMEM((width, CHUNK), F32),
            pltpu.VMEM((width, CHUNK), BF16),
            pltpu.VMEM((width, CHUNK), BF16),
            pltpu.VMEM((width, CHUNK), BF16),
            pltpu.VMEM((width, CHUNK), BF16),
            pltpu.SemaphoreType.DMA((6,)),
        ],
        compiler_params=pltpu.CompilerParams(vmem_limit_bytes=16 * 2**20),
        cost_estimate=pl.CostEstimate(flops=4 * 10**9, bytes_accessed=4 * 10**6, transcendentals=10**6),
        name="interior",
    )(x, lift, conv, fwt)


def swap_blocks(values, lanes):
    count = len(values)
    lane = lax.broadcasted_iota(jnp.int32, values[0].shape, 1)
    step = count // 2
    while step:
        shift = step * TLAT
        upper = (lane & shift) != 0
        fresh = list(values)
        for i in range(count):
            if i & step:
                continue
            low, high = values[i], values[i + step]
            fresh[i] = jnp.where(upper, pltpu.roll(high, shift, 1), low)
            fresh[i + step] = jnp.where(upper, high, pltpu.roll(low, lanes - shift, 1))
        values = fresh
        step //= 2
    return values


def edge_kernel(
    west, east, flux_in, taps, wc, lt, fwt,
    edges, tiles, north,
    halo, flux, ca, cb, la, lb, oa, ob,
):
    lats = west.shape[2]
    columns = taps.shape[1] // lats
    put_shifts(halo, 0, west[0])
    put_shifts(halo, lats, east[0])
    sides = [
        [(halo, 0), (taps, 0), (taps, lats)],
        [(taps, (columns - 2) * lats), (taps, (columns - 1) * lats), (halo, lats)],
    ]
    work = []
    full = lats // CHUNK * CHUNK
    for side in range(2):
        for lo in range(0, full, CHUNK):
            work.append([(side, lo, CHUNK)])
    if full < lats:
        work.append([(0, full, lats - full), (1, full, lats - full)])
    bufs = [(ca, la, oa), (cb, lb, ob)]

    def feed(j):
        segments = []
        for side, lo, size in work[j]:
            segments.append([(ref, at + lo) for ref, at in sides[side]] + [size])
        multiply(segments, wc, lt, bufs[j % 2][0], bufs[j % 2][1])

    def finish(j):
        stores = []
        at = 0
        for side, lo, size in work[j]:
            stores.append((edges.at[side], lo, at, at + size))
            at += size
        activate(bufs[j % 2][0], bufs[j % 2][1], bufs[j % 2][2], stores)

    def head(j):
        got = dot(fwt[...], bufs[j % 2][2][...])
        at = 0
        for side, lo, size in work[j]:
            flux[side, :, lo : lo + size] = got[:, at : at + size]
            at += size

    feed(0)
    for j in range(len(work)):
        if j + 1 < len(work):
            feed(j + 1)
        finish(j)
        if j:
            head(j - 1)
    head(len(work) - 1)
    group = 128 // TLAT
    for g in range(lats // 128):
        at = slice(g * 128, g * 128 + 128)
        values = [flux[0, :, at]]
        for i in range(columns - 2):
            values.append(flux_in[:, i * lats + g * 128 : i * lats + g * 128 + 128])
        values.append(flux[1, :, at])
        for a, v in enumerate(swap_blocks(values, 128)):
            tiles[g * group + a] = v.astype(BF16)
            if g == lats // 128 - 1 and a == group - 1:
                north[...] = v.astype(BF16)


def edge(west, east, flux_in, taps, wc, lt, fwt):
    lats = west.shape[2]
    columns = taps.shape[1] // lats
    width, chans = lt.shape
    fluxes = fwt.shape[0]
    cells = columns * TLAT
    return pl.pallas_call(
        edge_kernel,
        out_shape=(
            jax.ShapeDtypeStruct((2, width, lats), BF16),
            jax.ShapeDtypeStruct((lats // TLAT, fluxes, cells), BF16),
            jax.ShapeDtypeStruct((fluxes, cells), BF16),
        ),
        in_specs=[VM] * 7,
        out_specs=(VM, VM, VM),
        scratch_shapes=[
            pltpu.VMEM((3 * chans, 2 * lats), BF16),
            pltpu.VMEM((2, fluxes, lats), F32),
            pltpu.VMEM((width, CHUNK), F32),
            pltpu.VMEM((width, CHUNK), F32),
            pltpu.VMEM((width, CHUNK), BF16),
            pltpu.VMEM((width, CHUNK), BF16),
            pltpu.VMEM((width, CHUNK), BF16),
            pltpu.VMEM((width, CHUNK), BF16),
        ],
        compiler_params=pltpu.CompilerParams(vmem_limit_bytes=12 * 2**20),
        cost_estimate=pl.CostEstimate(flops=10**9, bytes_accessed=10**6, transcendentals=3 * 10**5),
        name="edge",
    )(west, east, flux_in, taps, wc, lt, fwt)


def list_tiles(mask, chosen, count):
    for k in range(MAXACT):
        chosen[k] = count - 1
    for k in range(FOLDB):
        chosen[k] = count - FOLDB + k
    found = FOLDB
    for t in range(count - FOLDB):
        water = mask[t] == 1

        @pl.when(jnp.logical_and(water, found < MAXACT))
        def _():
            chosen[found] = t

        found = found + water.astype(jnp.int32)
    return found


def early_kernel(
    hid_in, edges, pair, mask, tiles, ocean, regrid, ow, cw, mw,
    hid_out, sums, base, cwt, mwt,
    chosen, sems,
):
    count = ocean.shape[0]
    columns = hid_in.shape[0]
    out = [
        pltpu.make_async_copy(edges.at[0], hid_out.at[0], sems.at[0]),
        pltpu.make_async_copy(edges.at[1], hid_out.at[columns - 1], sems.at[1]),
    ]
    for c in out:
        c.start()
    list_tiles(mask, chosen, count)
    cwt[...] = cw[...].astype(F32).T.astype(BF16)
    mwt[...] = mw[...].astype(F32).T.astype(BF16)
    owt = ow[...].astype(F32).T.astype(BF16)
    ones = jnp.ones(tiles.shape[1:], BF16)
    for k in range(MAXACT):
        t = chosen[k]
        mine = jnp.concatenate([tiles[pair[1, t]], ones], 0)
        sums[k] = dot_t(mine, regrid[t, 1])
        base[k] = dot(owt, ocean[t])
    for c in out:
        c.wait()


def early(hid, edges, pair, mask, tiles, ocean, regrid, ow, cw, mw):
    cells = ocean.shape[2]
    width = mw.shape[0]
    fluxes = cw.shape[0]
    return pl.pallas_call(
        early_kernel,
        out_shape=(
            jax.ShapeDtypeStruct(hid.shape, BF16),
            jax.ShapeDtypeStruct((MAXACT, 2 * fluxes, cells), F32),
            jax.ShapeDtypeStruct((MAXACT, width, cells), F32),
            jax.ShapeDtypeStruct((width, fluxes), BF16),
            jax.ShapeDtypeStruct((width, width), BF16),
        ),
        in_specs=[HBM, VM, SM, SM, VM, VM, VM, VM, VM, VM],
        out_specs=(HBM, VM, VM, VM, VM),
        scratch_shapes=[
            pltpu.SMEM((MAXACT,), jnp.int32),
            pltpu.SemaphoreType.DMA((2,)),
        ],
        input_output_aliases={0: 0},
        compiler_params=pltpu.CompilerParams(vmem_limit_bytes=12 * 2**20),
        cost_estimate=pl.CostEstimate(flops=10**9, bytes_accessed=3 * 10**6, transcendentals=0),
        name="early",
    )(hid, edges, pair, mask, tiles, ocean, regrid, ow, cw, mw)


def late_kernel(
    pair, mask, west, east, fold, regrid_weight, sums, base, cwt, mwt,
    out_hbm,
    out, zero, chosen, sems,
):
    count = out_hbm.shape[0]
    fluxes = fold.shape[0]
    zero[...] = jnp.zeros(zero.shape, BF16)
    for t in range(count - FOLDB):

        @pl.when(mask[t] != 1)
        def _():
            pltpu.make_async_copy(zero, out_hbm.at[t], sems.at[0]).start()

    found = list_tiles(mask, chosen, count)
    ones = jnp.ones(fold.shape, BF16)
    for k in range(MAXACT):
        t = chosen[k]
        total = sums[k]
        total = total + dot_t(jnp.concatenate([west[pair[0, t]], ones], 0), regrid_weight[t, 0])
        total = total + dot_t(jnp.concatenate([east[pair[2, t]], ones], 0), regrid_weight[t, 2])
        if k < FOLDB:
            total = total + dot_t(jnp.concatenate([fold[...], ones], 0), regrid_weight[t, 3])
        regrid = (total[:fluxes] / total[fluxes : fluxes + 1]).astype(BF16)
        state = (base[k] + dot(cwt[...], regrid)).astype(BF16)
        mixed = dot(mwt[...], state)
        out[k] = (state.astype(F32) + gelu(mixed)).astype(BF16)
    for k in range(MAXACT):

        @pl.when(k < found)
        def _():
            pltpu.make_async_copy(out.at[k], out_hbm.at[chosen[k]], sems.at[1]).start()

    for t in range(count - FOLDB):

        @pl.when(mask[t] != 1)
        def _():
            pltpu.make_async_copy(zero, out_hbm.at[t], sems.at[0]).wait()

    for k in range(MAXACT):

        @pl.when(k < found)
        def _():
            pltpu.make_async_copy(out.at[k], out_hbm.at[0], sems.at[1]).wait()


def late(pair, mask, west, east, fold, regrid, sums, base, cwt, mwt):
    count = mask.shape[0]
    width, cells = base.shape[1:]
    return pl.pallas_call(
        late_kernel,
        out_shape=jax.ShapeDtypeStruct((count, width, cells), BF16),
        in_specs=[SM, SM, VM, VM, VM, VM, VM, VM, VM, VM],
        out_specs=HBM,
        scratch_shapes=[
            pltpu.VMEM((MAXACT, width, cells), BF16),
            pltpu.VMEM((width, cells), BF16),
            pltpu.SMEM((MAXACT,), jnp.int32),
            pltpu.SemaphoreType.DMA((2,)),
        ],
        compiler_params=pltpu.CompilerParams(vmem_limit_bytes=12 * 2**20),
        cost_estimate=pl.CostEstimate(flops=10**9, bytes_accessed=10**6, transcendentals=3 * 10**5),
        name="late",
    )(pair, mask, west, east, fold, regrid, sums, base, cwt, mwt)


def per_device(
    atm_in,
    ocean_in,
    lift_weight,
    conv_weight,
    flux_weight,
    ocean_weight,
    couple_weight,
    mix_weight,
    regrid_weight,
    pair_tile,
    ocean_mask,
):
    columns = atm_in.shape[0]
    strips = lax.axis_size("lon")
    forward = [(i, (i + 1) % strips) for i in range(strips)]
    backward = [((i + 1) % strips, i) for i in range(strips)]
    mirror = [(i, strips - 1 - i) for i in range(strips)]
    west = lax.ppermute(atm_in[columns - 1 :], "lon", forward)
    east = lax.ppermute(atm_in[:1], "lon", backward)
    fwt = flux_weight.T
    pair = pair_tile.T
    hid, flux, taps, wc, lt = interior(atm_in, lift_weight, conv_weight, fwt)
    edges, tiles, north = edge(west, east, flux, taps, wc, lt, fwt)
    tiles_west = lax.ppermute(tiles, "lon", forward)
    tiles_east = lax.ppermute(tiles, "lon", backward)
    fold = lax.ppermute(north, "lon", mirror)
    atm_hidden, sums, base, cwt, mwt = early(
        hid, edges, pair, ocean_mask, tiles, ocean_in, regrid_weight,
        ocean_weight, couple_weight, mix_weight,
    )
    ocean_hidden = late(
        pair, ocean_mask, tiles_west, tiles_east, fold, regrid_weight, sums, base, cwt, mwt
    )
    return (atm_hidden, ocean_hidden)


def solution(mesh):
    in_specs = (
        P(("groups", "lon"), None, None),
        P(("groups", "lon"), None, None),
        P(),
        P(),
        P(),
        P(),
        P(),
        P(),
        P("lon", None, None, None),
        P("lon", None),
        P("lon"),
    )
    out_specs = (P(("groups", "lon"), None, None), P(("groups", "lon"), None, None))
    return jax.shard_map(
        per_device, mesh=mesh, in_specs=in_specs, out_specs=out_specs, check_vma=False
    )
```

time: 41.8 us -> 29.1 us (0.70)
  Pallas kernels: 24.8 us -> 13 us
  local copies, waits for them, and re-layouts: 5.17 us -> 1.02 us
  waiting for transfers between devices: 0.63 us -> 3.91 us
    unnamed x17, local copies, waits for them, and re-layouts: 4.29 us -> 0.15 us
    pallas_call x1, Pallas kernels: 5.29 us -> 1.31 us  [edge(): pl.pallas_call(edge_kernel, out_shape=(jax.ShapeDtypeStruct((2, width, la...]
    pallas_call x1, Pallas kernels: 9.92 us -> 6.05 us  [interior(): pl.pallas_call(inner_kernel, out_shape=(jax.ShapeDtypeStruct((columns, wi...]
    pallas_call x1, Pallas kernels: 5.31 us -> 1.75 us  [early(): pl.pallas_call(early_kernel, out_shape=(jax.ShapeDtypeStruct(hid.shape, B...]
    ppermute x1, waiting for transfers between devices: 0.62 us -> 3.9 us  [per_device(): fold = lax.ppermute(north, 'lon', mirror)]
    pallas_call x1, Pallas kernels: 4.33 us -> 3.89 us  [late(): pl.pallas_call(late_kernel, out_shape=jax.ShapeDtypeStruct((count, width,...]
  transfers between devices with their start and end apart: 5 -> 5, of which waited for: 1 -> 1; matrix products, arithmetic and copies ran while one was open for 7% -> 0% of each run, Pallas kernels for 37% -> 27%
where the time goes in v2:
time: 29.1 us; the launch traced here: 28.9 us
  Pallas kernels  13 us (45%)
  starting transfers between devices  10.1 us (35%)
  waiting for transfers between devices  3.91 us (13%)
  local copies, waits for them, and re-layouts  1.02 us (4%)
  between operations  0.8 us (3%)
    pallas_call x1, Pallas kernels, interior(): pl.pallas_call(inner_kernel, out_shape=(jax.ShapeDtypeStruct((columns, wi...  6.05 us
    ppermute x1, starting transfers between devices, per_device(): east = lax.ppermute(atm_in[:1], 'lon', backward)  5.05 us
    ppermute x1, starting transfers between devices, per_device(): tiles_east = lax.ppermute(tiles, 'lon', backward)  4.43 us
    ppermute x1, waiting for transfers between devices, per_device(): fold = lax.ppermute(north, 'lon', mirror)  3.9 us
    pallas_call x1, Pallas kernels, late(): pl.pallas_call(late_kernel, out_shape=jax.ShapeDtypeStruct((count, width,...  3.89 us
    pallas_call x1, Pallas kernels, early(): pl.pallas_call(early_kernel, out_shape=(jax.ShapeDtypeStruct(hid.shape, B...  1.75 us
    pallas_call x1, Pallas kernels, edge(): pl.pallas_call(edge_kernel, out_shape=(jax.ShapeDtypeStruct((2, width, la...  1.31 us
    slice x1, local copies, waits for them, and re-layouts, per_device(): east = lax.ppermute(atm_in[:1], 'lon', backward)  0.87 us
  transfers between devices with their start and end apart: 5, of which 1 were waited for; matrix products, arithmetic and copies ran while one was open for 0% of the time, Pallas kernels for 27%

profile of v2, /device:TPU:0, one launch (start us, length us, event | category | flops | bytes accessed | tf_op | source)
XLA Modules:
  0.0 28.9 jit_solution(6817855059292502975)
XLA Ops:
  0.6 0.9 %fusion = (bf16[1,48,640]{2,1,0:T(8,128)(2,1)S(1)}, bf16[1,48,640]{2,1,0:T(8,128)(2,1)S(1)}) fusion(bf16[8,48,640]{2,1,0:T(8,128)(2,1)} %x_hbm.1), kind=kLoop, calls=%fused_computation | loop fusion | bytes 245760 | tf_op jit(solution)/shard_map/slice | solution.py:457
  1.5 0.5 %collective-permute-start = (bf16[1,48,640]{2,1,0:T(8,128)(2,1)S(1)}, bf16[1,48,640]{2,1,0:T(8,128)(2,1)S(1)}, u32[]{:S(2)}, u32[]{:S(2)}) collective-permute-start(bf16[1,48,640]{2,1,0:T(8,128)(2,1)S(1)} %get-tuple-element.29), channel_id=1, source_target_pairs={{0,1},{1,2},{2,3},{3,4},{4,5},{5,6},{6,7},{7,8},{8,9},{9,10},{10,1... | collective-permute-start | bytes 184328 | tf_op jit(solution)/shard_map/ppermute | solution.py:456
  2.0 5.0 %collective-permute-start.1 = (bf16[1,48,640]{2,1,0:T(8,128)(2,1)S(1)}, bf16[1,48,640]{2,1,0:T(8,128)(2,1)S(1)}, u32[]{:S(2)}, u32[]{:S(2)}) collective-permute-start(bf16[1,48,640]{2,1,0:T(8,128)(2,1)S(1)} %get-tuple-element.28), channel_id=1, source_target_pairs={{1,0},{2,1},{3,2},{4,3},{5,4},{6,5},{7,6},{8,7},{9,8},{10,9},{11,1... | collective-permute-start | bytes 184328 | tf_op jit(solution)/shard_map/ppermute | solution.py:457
  7.1 0.0 copy-start.6
  7.1 6.0 %interior.1 = (bf16[8,256,640]{2,1,0:T(8,128)(2,1)}, f32[16,3840]{1,0:T(8,128)S(1)}, bf16[144,5120]{1,0:T(8,128)(2,1)S(1)}, bf16[256,512]{1,0:T(8,128)(2,1)S(1)}, bf16[256,48]{1,0:T(8,128)(2,1)S(1)}) custom-call(bf16[8,48,640]{2,1,0:T(8,128)(2,1)} %x_hbm.1, bf16[48,256]{1,0:T(8,128)(2,1)} %lift_hbm.1, bf16[3,3,256,256]{3,2,1,0:T(8,128)(2,1)} %conv_hbm.1, ...), custom_call_target="tpu_custom_call" | custom-call | flops 4000000000 | bytes 4000000 | tf_op jit(solution)/shard_map/interior/pallas_call | solution.py:156
  13.2 0.0 copy-start.7
  13.2 0.0 collective-permute-done.west
  13.2 0.0 collective-permute-done.1.east
  13.2 0.0 copy-done.6
  13.2 0.0 copy-start
  13.2 0.0 copy-start.1
  13.2 0.0 copy-start.2
  13.2 0.0 copy-start.3
  13.2 0.0 copy-start.4
  13.3 0.0 copy-start.5
  13.3 1.3 %edge.1 = (bf16[2,256,640]{2,1,0:T(8,128)(2,1)S(1)}, bf16[40,16,128]{2,1,0:T(8,128)(2,1)S(1)}, bf16[16,128]{1,0:T(8,128)(2,1)S(1)}) custom-call(bf16[1,48,640]{2,1,0:T(8,128)(2,1)S(1)} %collective-permute-done.west, bf16[1,48,640]{2,1,0:T(8,128)(2,1)S(1)} %collective-permute-done.1.east, f32[16,3840]{1,0:T(8,128)S(1)} %get-tuple-element.16.flux_in, ...), custom_call_target="tpu_custom_call" | custom-call | flops 1000000000 | bytes 1000000 | tf_op jit(solution)/shard_map/edge/pallas_call | solution.py:277
  14.6 0.1 collective-permute-start.2
  14.7 4.4 %collective-permute-start.3 = (bf16[40,16,128]{2,1,0:T(8,128)(2,1)S(1)}, bf16[40,16,128]{2,1,0:T(8,128)(2,1)S(1)}, u32[]{:S(2)}, u32[]{:S(2)}) collective-permute-start(bf16[40,16,128]{2,1,0:T(8,128)(2,1)S(1)} %get-tuple-element.21.tiles), channel_id=1, source_target_pairs={{1,0},{2,1},{3,2},{4,3},{5,4},{6,5},{7,6},{8,7},{9,8},{10,9},{11,1... | collective-permute-start | bytes 491528 | tf_op jit(solution)/shard_map/ppermute | solution.py:463
  19.1 0.0 copy-done.7
  19.1 0.1 copy.14.ocean
  19.2 0.1 collective-permute-start.4
  19.3 0.0 copy-done
  19.3 0.0 copy-done.1
  19.3 0.0 copy-done.2
  19.3 0.0 copy-done.3
  19.3 0.0 copy-done.4
  19.3 0.0 copy-done.5
  19.3 1.8 %early.1 = (bf16[8,256,640]{2,1,0:T(8,128)(2,1)}, f32[8,32,128]{2,1,0:T(8,128)S(1)}, f32[8,256,128]{2,1,0:T(8,128)S(1)}, bf16[256,16]{1,0:T(8,128)(2,1)S(1)}, bf16[256,256]{1,0:T(8,128)(2,1)S(1)}) custom-call(bf16[8,256,640]{2,1,0:T(8,128)(2,1)} %get-tuple-element.15.hid_in, ...), custom_call_target="tpu_custom_call", output_to_operand_aliasing={{0}: (0, {})} | custom-call | flops 1000000000 | bytes 3000000 | tf_op jit(solution)/shard_map/early/pallas_call | solution.py:350
  21.1 3.9 %collective-permute-done.4.fold = bf16[16,128]{1,0:T(8,128)(2,1)S(1)} collective-permute-done((bf16[16,128]{1,0:T(8,128)(2,1)S(1)}, bf16[16,128]{1,0:T(8,128)(2,1)S(1)}, u32[]{:S(2)}, u32[]{:S(2)}) %collective-permute-start.4) | collective-permute-done | bytes 4128 | tf_op jit(solution)/shard_map/ppermute | solution.py:464
  25.0 0.0 collective-permute-done.2.west
  25.0 0.0 collective-permute-done.3.east
  25.0 3.9 %late.1 = bf16[16,256,128]{2,1,0:T(8,128)(2,1)} custom-call(s32[3,16]{1,0:T(4,128)S(1)} %bitcast.3, s32[16]{0:T(128)S(1)} %copy-done.5, bf16[40,16,128]{2,1,0:T(8,128)(2,1)S(1)} %collective-permute-done.2.west, bf16[40,16,128]{2,1,0:T(8,128)(2,1)S(1)} %collective-permute-done.3.east, bf16[16,128]{1,0:T(8,128)(2,1)S(1)} %collective-permute-done.4.fold, ...), custom_call_target="tpu_custom_call" | custom-call | flops 1000000000 | bytes 1000000 | tf_op jit(solution)/shard_map/late/pallas_call | solution.py:421
Async XLA Ops:
  1.5 11.7 %collective-permute-start = (bf16[1,48,640]{2,1,0:T(8,128)(2,1)S(1)}, bf16[1,48,640]{2,1,0:T(8,128)(2,1)S(1)}, u32[]{:S(2)}, u32[]{:S(2)}) collective-permute-start(bf16[1,48,640]{2,1,0:T(8,128)(2,1)S(1)} %get-tuple-element.29), channel_id=1, source_target_pairs={{0,1},{1,2},{2,3},{3,4},{4,5},{5,6},{6,7},{7,8},{8,9},{9,10},{10,1... | collective-permute-start | bytes 184328 | tf_op jit(solution)/shard_map/ppermute | solution.py:456
  2.0 11.1 %collective-permute-start.1 = (bf16[1,48,640]{2,1,0:T(8,128)(2,1)S(1)}, bf16[1,48,640]{2,1,0:T(8,128)(2,1)S(1)}, u32[]{:S(2)}, u32[]{:S(2)}) collective-permute-start(bf16[1,48,640]{2,1,0:T(8,128)(2,1)S(1)} %get-tuple-element.28), channel_id=1, source_target_pairs={{1,0},{2,1},{3,2},{4,3},{5,4},{6,5},{7,6},{8,7},{9,8},{10,9},{11,1... | collective-permute-start | bytes 184328 | tf_op jit(solution)/shard_map/ppermute | solution.py:457
  7.1 6.1 %copy-start.6 = (bf16[256,16]{0,1:T(8,128)(2,1)S(1)}, bf16[256,16]{0,1:T(8,128)(2,1)}, u32[]{:S(2)}) copy-start(bf16[256,16]{0,1:T(8,128)(2,1)} %param.15) | copy-start | bytes 24580
  13.2 5.9 %copy-start.7 = (bf16[16,95,128]{2,0,1:T(8,128)(2,1)S(1)}, bf16[16,95,128]{2,0,1:T(8,128)(2,1)}, u32[]{:S(2)}) copy-start(bf16[16,95,128]{2,0,1:T(8,128)(2,1)} %param.12) | copy-start | bytes 1167364
  13.2 6.1 %copy-start = (bf16[16,4,128,128]{3,2,1,0:T(8,128)(2,1)S(1)}, bf16[16,4,128,128]{3,2,1,0:T(8,128)(2,1)}, u32[]{:S(2)}) copy-start(bf16[16,4,128,128]{3,2,1,0:T(8,128)(2,1)} %regrid_weight.1) | copy-start | bytes 6291460
  13.2 6.1 %copy-start.1 = (bf16[256,256]{1,0:T(8,128)(2,1)S(1)}, bf16[256,256]{1,0:T(8,128)(2,1)}, u32[]{:S(2)}) copy-start(bf16[256,256]{1,0:T(8,128)(2,1)} %mw.1) | copy-start | bytes 393220
  13.2 6.1 %copy-start.2 = (bf16[95,256]{1,0:T(8,128)(2,1)S(1)}, bf16[95,256]{1,0:T(8,128)(2,1)}, u32[]{:S(2)}) copy-start(bf16[95,256]{1,0:T(8,128)(2,1)} %ow.1) | copy-start | bytes 145924
  13.2 6.1 %copy-start.3 = (bf16[16,256]{1,0:T(8,128)(2,1)S(1)}, bf16[16,256]{1,0:T(8,128)(2,1)}, u32[]{:S(2)}) copy-start(bf16[16,256]{1,0:T(8,128)(2,1)} %cw.1) | copy-start | bytes 24580
  13.2 6.1 %copy-start.4 = (s32[16,3]{0,1:T(4,128)S(1)}, s32[16,3]{0,1:T(4,128)}, u32[]{:S(2)}) copy-start(s32[16,3]{0,1:T(4,128)} %param.20) | copy-start | bytes 580
  13.3 6.1 %copy-start.5 = (s32[16]{0:T(128)S(1)}, s32[16]{0:T(128)}, u32[]{:S(2)}) copy-start(s32[16]{0:T(128)} %mask.3) | copy-start | bytes 196
  14.6 10.4 %collective-permute-start.2 = (bf16[40,16,128]{2,1,0:T(8,128)(2,1)S(1)}, bf16[40,16,128]{2,1,0:T(8,128)(2,1)S(1)}, u32[]{:S(2)}, u32[]{:S(2)}) collective-permute-start(bf16[40,16,128]{2,1,0:T(8,128)(2,1)S(1)} %get-tuple-element.21.tiles), channel_id=1, source_target_pairs={{0,1},{1,2},{2,3},{3,4},{4,5},{5,6},{6,7},{7,8},{8,9},{9,10},{10,1... | collective-permute-start | bytes 491528 | tf_op jit(solution)/shard_map/ppermute | solution.py:462
  14.7 10.3 %collective-permute-start.3 = (bf16[40,16,128]{2,1,0:T(8,128)(2,1)S(1)}, bf16[40,16,128]{2,1,0:T(8,128)(2,1)S(1)}, u32[]{:S(2)}, u32[]{:S(2)}) collective-permute-start(bf16[40,16,128]{2,1,0:T(8,128)(2,1)S(1)} %get-tuple-element.21.tiles), channel_id=1, source_target_pairs={{1,0},{2,1},{3,2},{4,3},{5,4},{6,5},{7,6},{8,7},{9,8},{10,9},{11,1... | collective-permute-start | bytes 491528 | tf_op jit(solution)/shard_map/ppermute | solution.py:463
  19.2 5.8 %collective-permute-start.4 = (bf16[16,128]{1,0:T(8,128)(2,1)S(1)}, bf16[16,128]{1,0:T(8,128)(2,1)S(1)}, u32[]{:S(2)}, u32[]{:S(2)}) collective-permute-start(bf16[16,128]{1,0:T(8,128)(2,1)S(1)} %get-tuple-element.23), channel_id=1, source_target_pairs={{0,15},{1,14},{2,13},{3,12},{4,11},{5,10},{6,9},{7,8},{8,7},{9,6},... | collective-permute-start | bytes 12296 | tf_op jit(solution)/shard_map/ppermute | solution.py:464

commit v3 on v2

v3 whole, which is shorter than its diff:
```python
import functools

import jax
import jax.numpy as jnp
from jax import lax
from jax.experimental import pallas as pl
from jax.experimental.pallas import tpu as pltpu
from jax.sharding import PartitionSpec as P

TLAT = 16
MAXACT = 8
FOLDB = 2
F32 = jnp.float32
BF16 = jnp.bfloat16
ROOT = 0.7978845608028654
CUBIC = ROOT * 0.044715

CHUNK = 256
STRIP = 32

HBM = pl.BlockSpec(memory_space=pltpu.HBM)
VM = pl.BlockSpec(memory_space=pltpu.VMEM)
SM = pl.BlockSpec(memory_space=pltpu.SMEM)


def dot(a, b):
    return lax.dot_general(a, b, (((1,), (0,)), ((), ())), preferred_element_type=F32)


def dot_t(a, b):
    return lax.dot_general(a, b, (((1,), (1,)), ((), ())), preferred_element_type=F32)


def gelu_of_half(half):
    return half + half * jnp.tanh(half * (2.0 * ROOT + 8.0 * CUBIC * (half * half)))


def put_shifts(taps, at, column):
    chans, lats = column.shape
    wide = column.astype(F32)
    lane = lax.broadcasted_iota(jnp.int32, wide.shape, 1)
    south = jnp.where(lane == 0, 0.0, pltpu.roll(wide, 1, 1))
    north = jnp.where(lane == lats - 1, 0.0, pltpu.roll(wide, lats - 1, 1))
    taps[:chans, pl.ds(at, lats)] = south.astype(BF16)
    taps[chans : 2 * chans, pl.ds(at, lats)] = column
    taps[2 * chans :, pl.ds(at, lats)] = north.astype(BF16)


def join(parts, axis):
    return parts[0] if len(parts) == 1 else jnp.concatenate(parts, axis)


def multiply(segments, wc, lt, conv, lifted):
    chans = lt.shape[1]
    rows = 3 * chans
    parts = []
    for a in range(3):
        parts.append(join([seg[a][0][:, pl.ds(seg[a][1], seg[3])] for seg in segments], 1))
    parts.append(jnp.zeros((wc.shape[1] - 3 * rows, parts[0].shape[1]), BF16))
    own = join([seg[1][0][chans : 2 * chans, pl.ds(seg[1][1], seg[3])] for seg in segments], 1)
    conv[...] = dot(wc[...], jnp.concatenate(parts, 0))
    lifted[...] = dot(lt[...], own).astype(BF16)


def activate(conv, lifted, out, stores):
    for r in range(0, conv.shape[0], STRIP):
        at = slice(r, r + STRIP)
        fresh = (lifted[at, :].astype(F32) + gelu_of_half(conv[at, :])).astype(BF16)
        out[at, :] = fresh
        for ref, first, lo, hi in stores:
            ref[at, pl.ds(first, hi - lo)] = fresh[:, lo:hi]


def parity():
    return lax.rem(lax.axis_index("lon"), 2)


def first_kernel(x_hbm, lift_hbm, conv_hbm, fwt_hbm, one, two, x, lift, conv, fwt, sems):
    odd = parity()
    last = x.shape[0] - 1
    copies = [
        pltpu.make_async_copy(x_hbm.at[pl.ds(last * (1 - odd), 1)], one, sems.at[0]),
        pltpu.make_async_copy(x_hbm.at[pl.ds(last * odd, 1)], two, sems.at[1]),
        pltpu.make_async_copy(x_hbm, x, sems.at[2]),
        pltpu.make_async_copy(lift_hbm, lift, sems.at[3]),
        pltpu.make_async_copy(conv_hbm, conv, sems.at[4]),
        pltpu.make_async_copy(fwt_hbm, fwt, sems.at[5]),
    ]
    for c in copies:
        c.start()
    for c in copies:
        c.wait()


def first(x, lift, conv, fwt):
    column = jax.ShapeDtypeStruct((1,) + x.shape[1:], BF16)
    given = [pltpu.with_memory_space_constraint(v, pltpu.HBM) for v in (x, lift, conv, fwt)]
    return pl.pallas_call(
        first_kernel,
        out_shape=(column, column) + tuple(jax.ShapeDtypeStruct(v.shape, BF16) for v in (x, lift, conv, fwt)),
        in_specs=[HBM] * 4,
        out_specs=(VM,) * 6,
        scratch_shapes=[pltpu.SemaphoreType.DMA((6,))],
        compiler_params=pltpu.CompilerParams(vmem_limit_bytes=4 * 2**20),
        cost_estimate=pl.CostEstimate(flops=0, bytes_accessed=3 * 10**6, transcendentals=0),
        name="first",
    )(*given)


def inner_kernel(
    x, lift, conv, fwt,
    hid, flux, taps, wc, lt,
    comp, ca, cb, la, lb, oa, ob,
):
    columns, chans, lats = x.shape
    width = lift.shape[1]
    comp[pl.ds(9 * chans, 2 * width - 9 * chans), :] = jnp.zeros((2 * width - 9 * chans, width), F32)
    half = 0.5 * lift[...]
    for a in range(3):
        for b in range(3):
            comp[pl.ds((3 * a + b) * chans, chans), :] = dot(half, conv[a, b])
    wc[...] = comp[...].T.astype(BF16)
    lt[...] = lift[...].astype(F32).T.astype(BF16)
    for i in range(columns):
        put_shifts(taps, i * lats, x[i])

    def feed(j, conv_to, lifted_to):
        at = [pl.multiple_of(j * CHUNK + a * lats, 128) for a in range(3)]
        multiply([[(taps, p) for p in at] + [CHUNK]], wc, lt, conv_to, lifted_to)

    def finish(j, conv_of, lifted_of, out):
        activate(conv_of, lifted_of, out, [(hid, pl.multiple_of(j * CHUNK, 128), 0, CHUNK)])

    def head(j, out):
        flux[:, pl.ds(pl.multiple_of(j * CHUNK, 128), CHUNK)] = dot(fwt[...], out[...])

    chunks = (columns - 2) * lats // CHUNK
    feed(0, ca, la)

    def two(i, _):
        j = 2 * i
        feed(j + 1, cb, lb)
        finish(j, ca, la, oa)
        head(jnp.maximum(j - 1, 0), ob)

        feed(jnp.minimum(j + 2, chunks - 1), ca, la)
        finish(j + 1, cb, lb, ob)
        head(j, oa)
        return 0

    lax.fori_loop(0, chunks // 2, two, 0)
    head(chunks // 2 * 2 - 1, ob)
    if chunks % 2:
        finish(chunks - 1, ca, la, oa)
        head(chunks - 1, oa)


def interior(x, lift, conv, fwt):
    columns, chans, lats = x.shape
    width = lift.shape[1]
    fluxes = fwt.shape[0]
    inner = (columns - 2) * lats
    return pl.pallas_call(
        inner_kernel,
        out_shape=(
            jax.ShapeDtypeStruct((width, inner), BF16),
            jax.ShapeDtypeStruct((fluxes, inner), F32),
            jax.ShapeDtypeStruct((3 * chans, columns * lats), BF16),
            jax.ShapeDtypeStruct((width, 2 * width), BF16),
            jax.ShapeDtypeStruct((width, chans), BF16),
        ),
        in_specs=[VM] * 4,
        out_specs=(VM,) * 5,
        scratch_shapes=[
            pltpu.VMEM((2 * width, width), F32),
            pltpu.VMEM((width, CHUNK), F32),
            pltpu.VMEM((width, CHUNK), F32),
            pltpu.VMEM((width, CHUNK), BF16),
            pltpu.VMEM((width, CHUNK), BF16),
            pltpu.VMEM((width, CHUNK), BF16),
            pltpu.VMEM((width, CHUNK), BF16),
        ],
        compiler_params=pltpu.CompilerParams(vmem_limit_bytes=12 * 2**20),
        cost_estimate=pl.CostEstimate(flops=4 * 10**9, bytes_accessed=4 * 10**6, transcendentals=10**6),
        name="interior",
    )(x, lift, conv, fwt)


def swap_blocks(values, lanes):
    count = len(values)
    lane = lax.broadcasted_iota(jnp.int32, values[0].shape, 1)
    step = count // 2
    while step:
        shift = step * TLAT
        upper = (lane & shift) != 0
        fresh = list(values)
        for i in range(count):
            if i & step:
                continue
            low, high = values[i], values[i + step]
            fresh[i] = jnp.where(upper, pltpu.roll(high, shift, 1), low)
            fresh[i + step] = jnp.where(upper, high, pltpu.roll(low, lanes - shift, 1))
        values = fresh
        step //= 2
    return values


def edge_kernel(
    one, two, flux_in, taps, wc, lt, fwt,
    edges, tiles, north,
    halo, flux, ca, cb, la, lb, oa, ob,
):
    lats = one.shape[2]
    columns = taps.shape[1] // lats
    odd = parity()
    put_shifts(halo, pl.multiple_of(lats * (1 - odd), 128), one[0])
    put_shifts(halo, pl.multiple_of(lats * odd, 128), two[0])
    sides = [
        [(halo, 0), (taps, 0), (taps, lats)],
        [(taps, (columns - 2) * lats), (taps, (columns - 1) * lats), (halo, lats)],
    ]
    work = []
    full = lats // CHUNK * CHUNK
    for side in range(2):
        for lo in range(0, full, CHUNK):
            work.append([(side, lo, CHUNK)])
    if full < lats:
        work.append([(0, full, lats - full), (1, full, lats - full)])
    bufs = [(ca, la, oa), (cb, lb, ob)]

    def feed(j):
        segments = []
        for side, lo, size in work[j]:
            segments.append([(ref, at + lo) for ref, at in sides[side]] + [size])
        multiply(segments, wc, lt, bufs[j % 2][0], bufs[j % 2][1])

    def finish(j):
        stores = []
        at = 0
        for side, lo, size in work[j]:
            stores.append((edges.at[side], lo, at, at + size))
            at += size
        activate(bufs[j % 2][0], bufs[j % 2][1], bufs[j % 2][2], stores)

    def head(j):
        got = dot(fwt[...], bufs[j % 2][2][...])
        at = 0
        for side, lo, size in work[j]:
            flux[side, :, lo : lo + size] = got[:, at : at + size]
            at += size

    feed(0)
    for j in range(len(work)):
        if j + 1 < len(work):
            feed(j + 1)
        finish(j)
        if j:
            head(j - 1)
    head(len(work) - 1)
    group = 128 // TLAT
    for g in range(lats // 128):
        at = slice(g * 128, g * 128 + 128)
        values = [flux[0, :, at]]
        for i in range(columns - 2):
            values.append(flux_in[:, i * lats + g * 128 : i * lats + g * 128 + 128])
        values.append(flux[1, :, at])
        for a, v in enumerate(swap_blocks(values, 128)):
            tiles[g * group + a] = v.astype(BF16)
            if g == lats // 128 - 1 and a == group - 1:
                north[...] = v.astype(BF16)


def edge(one, two, flux_in, taps, wc, lt, fwt):
    lats = one.shape[2]
    columns = taps.shape[1] // lats
    width, chans = lt.shape
    fluxes = fwt.shape[0]
    cells = columns * TLAT
    return pl.pallas_call(
        edge_kernel,
        out_shape=(
            jax.ShapeDtypeStruct((2, width, lats), BF16),
            jax.ShapeDtypeStruct((lats // TLAT, fluxes, cells), BF16),
            jax.ShapeDtypeStruct((fluxes, cells), BF16),
        ),
        in_specs=[VM] * 7,
        out_specs=(VM, VM, VM),
        scratch_shapes=[
            pltpu.VMEM((3 * chans, 2 * lats), BF16),
            pltpu.VMEM((2, fluxes, lats), F32),
            pltpu.VMEM((width, CHUNK), F32),
            pltpu.VMEM((width, CHUNK), F32),
            pltpu.VMEM((width, CHUNK), BF16),
            pltpu.VMEM((width, CHUNK), BF16),
            pltpu.VMEM((width, CHUNK), BF16),
            pltpu.VMEM((width, CHUNK), BF16),
        ],
        compiler_params=pltpu.CompilerParams(vmem_limit_bytes=12 * 2**20),
        cost_estimate=pl.CostEstimate(flops=10**9, bytes_accessed=10**6, transcendentals=3 * 10**5),
        name="edge",
    )(one, two, flux_in, taps, wc, lt, fwt)


def list_tiles(mask, chosen, count):
    for k in range(MAXACT):
        chosen[k] = count - 1
    for k in range(FOLDB):
        chosen[k] = count - FOLDB + k
    found = FOLDB
    for t in range(count - FOLDB):
        water = mask[t] == 1

        @pl.when(jnp.logical_and(water, found < MAXACT))
        def _():
            chosen[found] = t

        found = found + water.astype(jnp.int32)
    return found


def early_kernel(
    hid, edges, pair, mask, tiles, ocean, regrid, ow, cw, mw,
    hid_out, out_hbm, sums, base, cwt, mwt,
    zero, chosen, sems,
):
    count = ocean.shape[0]
    cells = ocean.shape[2]
    columns, _, lats = hid_out.shape
    zero[...] = jnp.zeros(zero.shape, BF16)
    out = [
        pltpu.make_async_copy(edges.at[0], hid_out.at[0], sems.at[0]),
        pltpu.make_async_copy(edges.at[1], hid_out.at[columns - 1], sems.at[1]),
    ]
    for i in range(columns - 2):
        out.append(
            pltpu.make_async_copy(hid.at[:, pl.ds(i * lats, lats)], hid_out.at[i + 1], sems.at[2 + i])
        )
    for c in out:
        c.start()
    list_tiles(mask, chosen, count)
    for t in range(count - FOLDB):

        @pl.when(mask[t] != 1)
        def _():
            pltpu.make_async_copy(zero, out_hbm.at[t], sems.at[columns]).start()

    cwt[...] = cw[...].astype(F32).T.astype(BF16)
    mwt[...] = (0.5 * mw[...].astype(F32)).T.astype(BF16)
    owt = ow[...].astype(F32).T.astype(BF16)
    ones = jnp.ones(tiles.shape[1:], BF16)
    for k in range(MAXACT):
        t = chosen[k]
        at = slice(k * cells, k * cells + cells)
        mine = jnp.concatenate([tiles[pair[1, t]], ones], 0)
        sums[:, at] = dot_t(mine, regrid[t, 1])
        base[:, at] = dot(owt, ocean[t])
    for t in range(count - FOLDB):

        @pl.when(mask[t] != 1)
        def _():
            pltpu.make_async_copy(zero, out_hbm.at[t], sems.at[columns]).wait()

    for c in out:
        c.wait()


def early(hid, edges, pair, mask, tiles, ocean, regrid, ow, cw, mw):
    count, _, cells = ocean.shape
    width = mw.shape[0]
    fluxes = cw.shape[0]
    lats = edges.shape[2]
    columns = hid.shape[1] // lats + 2
    return pl.pallas_call(
        early_kernel,
        out_shape=(
            jax.ShapeDtypeStruct((columns, width, lats), BF16),
            jax.ShapeDtypeStruct((count, width, cells), BF16),
            jax.ShapeDtypeStruct((2 * fluxes, MAXACT * cells), F32),
            jax.ShapeDtypeStruct((width, MAXACT * cells), F32),
            jax.ShapeDtypeStruct((width, fluxes), BF16),
            jax.ShapeDtypeStruct((width, width), BF16),
        ),
        in_specs=[VM, VM, SM, SM, VM, VM, VM, VM, VM, VM],
        out_specs=(HBM, HBM, VM, VM, VM, VM),
        scratch_shapes=[
            pltpu.VMEM((width, cells), BF16),
            pltpu.SMEM((MAXACT,), jnp.int32),
            pltpu.SemaphoreType.DMA((columns + 1,)),
        ],
        compiler_params=pltpu.CompilerParams(vmem_limit_bytes=12 * 2**20),
        cost_estimate=pl.CostEstimate(flops=10**9, bytes_accessed=6 * 10**6, transcendentals=0),
        name="early",
    )(hid, edges, pair, mask, tiles, ocean, regrid, ow, cw, mw)


def late_kernel(
    pair, mask, one, two, fold, regrid_weight, sums, base, cwt, mwt, given_hbm,
    out_hbm,
    state, mixed, out, chosen, sems,
):
    count = out_hbm.shape[0]
    fluxes = fold.shape[0]
    cells = out.shape[2]
    found = list_tiles(mask, chosen, count)
    odd = parity() == 1
    ones = jnp.ones(fold.shape, BF16)
    wide = 2 * cells
    totals = []
    for k in range(MAXACT):
        t = chosen[k]
        pw, pe = pair[0, t], pair[2, t]
        west = jnp.where(odd, one[pw], two[pw])
        east = jnp.where(odd, two[pe], one[pe])
        got = jnp.concatenate([jnp.concatenate([west, ones], 0), jnp.concatenate([east, ones], 0)], 1)
        weights = jnp.concatenate([regrid_weight[t, 0], regrid_weight[t, 2]], 1)
        total = sums[:, k * cells : (k + 1) * cells] + dot_t(got, weights)
        if k < FOLDB:
            total = total + dot_t(jnp.concatenate([fold[...], ones], 0), regrid_weight[t, 3])
        totals.append(total)
    for p in range(MAXACT // 2):
        at = slice(p * wide, p * wide + wide)
        total = jnp.concatenate(totals[2 * p : 2 * p + 2], 1)
        regrid = (total[:fluxes] / total[fluxes : fluxes + 1]).astype(BF16)
        state[:, at] = (base[:, at] + dot(cwt[...], regrid)).astype(BF16)

    def mix(p):
        mixed[p % 2][...] = dot(mwt[...], state[:, p * wide : p * wide + wide])

    mix(0)
    for p in range(MAXACT // 2):
        if p + 1 < MAXACT // 2:
            mix(p + 1)
        for r in range(0, state.shape[0], STRIP):
            at = slice(r, r + STRIP)
            for side in range(2):
                k = 2 * p + side
                own = state[at, k * cells : (k + 1) * cells].astype(F32)
                half = mixed[p % 2][at, side * cells : (side + 1) * cells]
                out[k, at, :] = (own + gelu_of_half(half)).astype(BF16)
        for side in range(2):
            k = 2 * p + side

            @pl.when(k < found)
            def _():
                pltpu.make_async_copy(out.at[k], out_hbm.at[chosen[k]], sems.at[k]).start()

    for k in range(MAXACT):

        @pl.when(k < found)
        def _():
            pltpu.make_async_copy(out.at[k], out_hbm.at[0], sems.at[k]).wait()


def late(pair, mask, one, two, fold, regrid, sums, base, cwt, mwt, given):
    count, width, cells = given.shape

    def body(*refs):
        head, (state, ma, mb, out, chosen, sems) = refs[:12], refs[12:]
        late_kernel(*head, state, (ma, mb), out, chosen, sems)

    return pl.pallas_call(
        body,
        out_shape=jax.ShapeDtypeStruct((count, width, cells), BF16),
        in_specs=[SM, SM, VM, VM, VM, VM, VM, VM, VM, VM, HBM],
        out_specs=HBM,
        scratch_shapes=[
            pltpu.VMEM((width, MAXACT * cells), BF16),
            pltpu.VMEM((width, 2 * cells), F32),
            pltpu.VMEM((width, 2 * cells), F32),
            pltpu.VMEM((MAXACT, width, cells), BF16),
            pltpu.SMEM((MAXACT,), jnp.int32),
            pltpu.SemaphoreType.DMA((MAXACT,)),
        ],
        input_output_aliases={10: 0},
        compiler_params=pltpu.CompilerParams(vmem_limit_bytes=12 * 2**20),
        cost_estimate=pl.CostEstimate(flops=10**9, bytes_accessed=10**6, transcendentals=3 * 10**5),
        name="late",
    )(pair, mask, one, two, fold, regrid, sums, base, cwt, mwt, given)


def per_device(
    atm_in,
    ocean_in,
    lift_weight,
    conv_weight,
    flux_weight,
    ocean_weight,
    couple_weight,
    mix_weight,
    regrid_weight,
    pair_tile,
    ocean_mask,
):
    strips = lax.axis_size("lon")
    inward = [(i, i ^ 1) for i in range(strips)]
    outward = [(i, (i + 1 if i % 2 else i - 1) % strips) for i in range(strips)]
    mirror = [(i, strips - 1 - i) for i in range(strips)]
    fwt = flux_weight.T
    pair = pair_tile.T
    send_one, send_two, x, lift, conv, fwt = first(atm_in, lift_weight, conv_weight, fwt)
    one = lax.ppermute(send_one, "lon", inward)
    two = lax.ppermute(send_two, "lon", outward)
    hid, flux, taps, wc, lt = interior(x, lift, conv, fwt)
    edges, tiles, north = edge(one, two, flux, taps, wc, lt, fwt)
    tiles_one = lax.ppermute(tiles, "lon", inward)
    tiles_two = lax.ppermute(tiles, "lon", outward)
    fold = lax.ppermute(north, "lon", mirror)
    atm_hidden, given, sums, base, cwt, mwt = early(
        hid, edges, pair, ocean_mask, tiles, ocean_in, regrid_weight,
        ocean_weight, couple_weight, mix_weight,
    )
    ocean_hidden = late(
        pair, ocean_mask, tiles_one, tiles_two, fold, regrid_weight, sums, base, cwt, mwt, given
    )
    return (atm_hidden, ocean_hidden)


def solution(mesh):
    in_specs = (
        P(("groups", "lon"), None, None),
        P(("groups", "lon"), None, None),
        P(),
        P(),
        P(),
        P(),
        P(),
        P(),
        P("lon", None, None, None),
        P("lon", None),
        P("lon"),
    )
    out_specs = (P(("groups", "lon"), None, None), P(("groups", "lon"), None, None))
    return jax.shard_map(
        per_device, mesh=mesh, in_specs=in_specs, out_specs=out_specs, check_vma=False
    )
```

time: 29.1 us -> 24.4 us (0.84)
  waiting for transfers between devices: 3.91 us -> 1.4 us
  Pallas kernels: 13 us -> 11.1 us
  local copies, waits for them, and re-layouts: 1.02 us -> 0.14 us
  starting transfers between devices: 10.1 us -> 10.9 us
    ppermute x1, waiting for transfers between devices: 3.9 us -> 1.39 us  [per_device(): fold = lax.ppermute(north, 'lon', mirror)]
    pallas_call x3 -> x4, Pallas kernels: 11.7 us -> 9.82 us  [the longest x1 3.55 us: interior(): pl.pallas_call(inner_kernel, out_shape=(jax.ShapeDtypeStruct((width, inne...]
    ppermute x1, starting transfers between devices: 0.07 us -> 1.78 us  [per_device(): fold = lax.ppermute(north, 'lon', mirror)]
    ppermute x4, starting transfers between devices: 10.1 us -> 9.08 us  [the longest x1 5.66 us: per_device(): two = lax.ppermute(send_two, 'lon', outward)]
    slice x1 -> x0, local copies, waits for them, and re-layouts: 0.87 us -> none  [per_device(): east = lax.ppermute(atm_in[:1], 'lon', backward)]
  transfers between devices with their start and end apart: 5 -> 5, of which waited for: 1 -> 1; matrix products, arithmetic and copies ran while one was open for 0% -> 0% of each run, Pallas kernels for 27% -> 25%
where the time goes in v3:
time: 24.4 us; the launch traced here: 24.3 us
  Pallas kernels  11.1 us (45%)
  starting transfers between devices  10.9 us (45%)
  waiting for transfers between devices  1.4 us (6%)
  between operations  0.75 us (3%)
    ppermute x1, starting transfers between devices, per_device(): two = lax.ppermute(send_two, 'lon', outward)  5.66 us
    pallas_call x1, Pallas kernels, interior(): pl.pallas_call(inner_kernel, out_shape=(jax.ShapeDtypeStruct((width, inne...  3.55 us
    ppermute x1, starting transfers between devices, per_device(): tiles_two = lax.ppermute(tiles, 'lon', outward)  2.79 us
    pallas_call x1, Pallas kernels, early(): pl.pallas_call(early_kernel, out_shape=(jax.ShapeDtypeStruct((columns, wi...  2.59 us
    pallas_call x1, Pallas kernels, late(): pl.pallas_call(body, out_shape=jax.ShapeDtypeStruct((count, width, cells)...  2.1 us
    ppermute x1, starting transfers between devices, per_device(): fold = lax.ppermute(north, 'lon', mirror)  1.78 us
    pallas_call x1, Pallas kernels, first(): pl.pallas_call(first_kernel, out_shape=(column, column) + tuple((jax.Shap...  1.57 us
    ppermute x1, waiting for transfers between devices, per_device(): fold = lax.ppermute(north, 'lon', mirror)  1.39 us
  transfers between devices with their start and end apart: 5, of which 1 were waited for; matrix products, arithmetic and copies ran while one was open for 0% of the time, Pallas kernels for 25%

profile of v3, /device:TPU:0, one launch (start us, length us, event | category | flops | bytes accessed | tf_op | source)
XLA Modules:
  0.0 24.3 jit_solution(17654262824532289227)
XLA Ops:
  0.6 1.6 %first.1 = (bf16[1,48,640]{2,1,0:T(8,128)(2,1)S(1)}, bf16[1,48,640]{2,1,0:T(8,128)(2,1)S(1)}, bf16[8,48,640]{2,1,0:T(8,128)(2,1)S(1)}, bf16[48,256]{1,0:T(8,128)...) custom-call(bf16[8,48,640]{2,1,0:T(8,128)(2,1)} %x_hbm.1, bf16[48,256]{1,0:T(8,128)(2,1)} %lift_hbm.1, ...), custom_call_target="tpu_custom_call" | custom-call | bytes 3000000 | tf_op jit(solution)/shard_map/first/pallas_call | solution.py:98
  2.2 0.6 %collective-permute-start = (bf16[1,48,640]{2,1,0:T(8,128)(2,1)S(1)}, bf16[1,48,640]{2,1,0:T(8,128)(2,1)S(1)}, u32[]{:S(2)}, u32[]{:S(2)}) collective-permute-start(bf16[1,48,640]{2,1,0:T(8,128)(2,1)S(1)} %get-tuple-element.27), channel_id=1, source_target_pairs={{0,1},{1,0},{2,3},{3,2},{4,5},{5,4},{6,7},{7,6},{8,9},{9,8},{10,11... | collective-permute-start | bytes 184328 | tf_op jit(solution)/shard_map/ppermute | solution.py:501
  2.8 5.7 %collective-permute-start.1 = (bf16[1,48,640]{2,1,0:T(8,128)(2,1)S(1)}, bf16[1,48,640]{2,1,0:T(8,128)(2,1)S(1)}, u32[]{:S(2)}, u32[]{:S(2)}) collective-permute-start(bf16[1,48,640]{2,1,0:T(8,128)(2,1)S(1)} %get-tuple-element.28), channel_id=1, source_target_pairs={{0,15},{1,2},{2,1},{3,4},{4,3},{5,6},{6,5},{7,8},{8,7},{9,10},{10,... | collective-permute-start | bytes 184328 | tf_op jit(solution)/shard_map/ppermute | solution.py:502
  8.4 3.6 %interior.1 = (bf16[256,3840]{1,0:T(8,128)(2,1)S(1)}, f32[16,3840]{1,0:T(8,128)S(1)}, bf16[144,5120]{1,0:T(8,128)(2,1)S(1)}, bf16[256,512]{1,0:T(8,128)(2,1)S(1)}, bf16[256,48]{1,0:T(8,128)(2,1)S(1)}) custom-call(bf16[8,48,640]{2,1,0:T(8,128)(2,1)S(1)} %get-tuple-element.22.x, bf16[48,256]{1,0:T(8,128)(2,1)S(1)} %get-tuple-element.23.lift, ...), custom_call_target="tpu_custom_call" | custom-call | flops 4000000000 | bytes 4000000 | tf_op jit(solution)/shard_map/interior/pallas_call | solution.py:163
  12.0 0.0 copy-start.6
  12.0 0.0 collective-permute-done.one
  12.0 0.0 collective-permute-done.1.two
  12.0 0.0 copy-start
  12.0 0.0 copy-start.1
  12.0 0.0 copy-start.2
  12.0 0.0 copy-start.3
  12.0 0.0 copy-start.4
  12.1 0.0 copy-start.5
  12.1 1.3 %edge.1 = (bf16[2,256,640]{2,1,0:T(8,128)(2,1)S(1)}, bf16[40,16,128]{2,1,0:T(8,128)(2,1)S(1)}, bf16[16,128]{1,0:T(8,128)(2,1)S(1)}) custom-call(bf16[1,48,640]{2,1,0:T(8,128)(2,1)S(1)} %collective-permute-done.one, bf16[1,48,640]{2,1,0:T(8,128)(2,1)S(1)} %collective-permute-done.1.two, f32[16,3840]{1,0:T(8,128)S(1)} %get-tuple-element.29.flux_in, ...), custom_call_target="tpu_custom_call" | custom-call | flops 1000000000 | bytes 1000000 | tf_op jit(solution)/shard_map/edge/pallas_call | solution.py:279
  13.4 0.1 collective-permute-start.2
  13.5 2.8 %collective-permute-start.3 = (bf16[40,16,128]{2,1,0:T(8,128)(2,1)S(1)}, bf16[40,16,128]{2,1,0:T(8,128)(2,1)S(1)}, u32[]{:S(2)}, u32[]{:S(2)}) collective-permute-start(bf16[40,16,128]{2,1,0:T(8,128)(2,1)S(1)} %get-tuple-element.34.tiles), channel_id=1, source_target_pairs={{0,15},{1,2},{2,1},{3,4},{4,3},{5,6},{6,5},{7,8},{8,7},{9,10},{10,... | collective-permute-start | bytes 491528 | tf_op jit(solution)/shard_map/ppermute | solution.py:506
  16.3 0.0 copy-done.6
  16.3 0.1 copy.14.ocean
  16.4 1.8 %collective-permute-start.4 = (bf16[16,128]{1,0:T(8,128)(2,1)S(1)}, bf16[16,128]{1,0:T(8,128)(2,1)S(1)}, u32[]{:S(2)}, u32[]{:S(2)}) collective-permute-start(bf16[16,128]{1,0:T(8,128)(2,1)S(1)} %get-tuple-element.36), channel_id=1, source_target_pairs={{0,15},{1,14},{2,13},{3,12},{4,11},{5,10},{6,9},{7,8},{8,7},{9,6},... | collective-permute-start | bytes 12296 | tf_op jit(solution)/shard_map/ppermute | solution.py:507
  18.1 0.0 copy-done
  18.2 0.0 copy-done.1
  18.2 0.0 copy-done.2
  18.2 0.0 copy-done.3
  18.2 0.0 copy-done.4
  18.2 0.0 copy-done.5
  18.2 2.6 %early.1 = (bf16[8,256,640]{2,1,0:T(8,128)(2,1)}, bf16[16,256,128]{2,1,0:T(8,128)(2,1)}, f32[32,1024]{1,0:T(8,128)S(1)}, f32[256,1024]{1,0:T(8,128)S(1)}, bf16[2...) custom-call(bf16[256,3840]{1,0:T(8,128)(2,1)S(1)} %get-tuple-element.26.hid, ...), custom_call_target="tpu_custom_call" | custom-call | flops 1000000000 | bytes 6000000 | tf_op jit(solution)/shard_map/early/pallas_call | solution.py:373
  20.8 1.4 %collective-permute-done.4.refs_4_ = bf16[16,128]{1,0:T(8,128)(2,1)S(1)} collective-permute-done((bf16[16,128]{1,0:T(8,128)(2,1)S(1)}, bf16[16,128]{1,0:T(8,128)(2,1)S(1)}, u32[]{:S(2)}, u32[]{:S(2)}) %collective-permute-start.4) | collective-permute-done | bytes 4128 | tf_op jit(solution)/shard_map/ppermute | solution.py:507
  22.2 0.0 collective-permute-done.2.refs_2_
  22.2 0.0 collective-permute-done.3.refs_3_
  22.2 2.1 %late.1 = bf16[16,256,128]{2,1,0:T(8,128)(2,1)} custom-call(s32[3,16]{1,0:T(4,128)S(1)} %bitcast.3, s32[16]{0:T(128)S(1)} %copy-done.5, bf16[40,16,128]{2,1,0:T(8,128)(2,1)S(1)} %collective-permute-done.2.refs_2_, bf16[40,16,128]{2,1,0:T(8,128)(2,1)S(1)} %collective-permute-done.3.refs_3_, ...), custom_call_target="tpu_custom_call", output_to_operand_aliasing={{}: (10, {})} | custom-call | flops 1000000000 | bytes 1000000 | tf_op jit(solution)/shard_map/late/pallas_call | solution.py:461
Async XLA Ops:
  2.2 9.8 %collective-permute-start = (bf16[1,48,640]{2,1,0:T(8,128)(2,1)S(1)}, bf16[1,48,640]{2,1,0:T(8,128)(2,1)S(1)}, u32[]{:S(2)}, u32[]{:S(2)}) collective-permute-start(bf16[1,48,640]{2,1,0:T(8,128)(2,1)S(1)} %get-tuple-element.27), channel_id=1, source_target_pairs={{0,1},{1,0},{2,3},{3,2},{4,5},{5,4},{6,7},{7,6},{8,9},{9,8},{10,11... | collective-permute-start | bytes 184328 | tf_op jit(solution)/shard_map/ppermute | solution.py:501
  2.8 9.2 %collective-permute-start.1 = (bf16[1,48,640]{2,1,0:T(8,128)(2,1)S(1)}, bf16[1,48,640]{2,1,0:T(8,128)(2,1)S(1)}, u32[]{:S(2)}, u32[]{:S(2)}) collective-permute-start(bf16[1,48,640]{2,1,0:T(8,128)(2,1)S(1)} %get-tuple-element.28), channel_id=1, source_target_pairs={{0,15},{1,2},{2,1},{3,4},{4,3},{5,6},{6,5},{7,8},{8,7},{9,10},{10,... | collective-permute-start | bytes 184328 | tf_op jit(solution)/shard_map/ppermute | solution.py:502
  12.0 4.3 %copy-start.6 = (bf16[16,95,128]{2,0,1:T(8,128)(2,1)S(1)}, bf16[16,95,128]{2,0,1:T(8,128)(2,1)}, u32[]{:S(2)}) copy-start(bf16[16,95,128]{2,0,1:T(8,128)(2,1)} %param.12) | copy-start | bytes 1167364
  12.0 6.2 %copy-start = (bf16[16,4,128,128]{3,2,1,0:T(8,128)(2,1)S(1)}, bf16[16,4,128,128]{3,2,1,0:T(8,128)(2,1)}, u32[]{:S(2)}) copy-start(bf16[16,4,128,128]{3,2,1,0:T(8,128)(2,1)} %refs_5_.1) | copy-start | bytes 6291460
  12.0 6.1 %copy-start.1 = (bf16[256,256]{1,0:T(8,128)(2,1)S(1)}, bf16[256,256]{1,0:T(8,128)(2,1)}, u32[]{:S(2)}) copy-start(bf16[256,256]{1,0:T(8,128)(2,1)} %mw.1) | copy-start | bytes 393220
  12.0 6.1 %copy-start.2 = (bf16[95,256]{1,0:T(8,128)(2,1)S(1)}, bf16[95,256]{1,0:T(8,128)(2,1)}, u32[]{:S(2)}) copy-start(bf16[95,256]{1,0:T(8,128)(2,1)} %ow.1) | copy-start | bytes 145924
  12.0 6.1 %copy-start.3 = (s32[16,3]{0,1:T(4,128)S(1)}, s32[16,3]{0,1:T(4,128)}, u32[]{:S(2)}) copy-start(s32[16,3]{0,1:T(4,128)} %param.20) | copy-start | bytes 580
  12.0 6.1 %copy-start.4 = (bf16[16,256]{1,0:T(8,128)(2,1)S(1)}, bf16[16,256]{1,0:T(8,128)(2,1)}, u32[]{:S(2)}) copy-start(bf16[16,256]{1,0:T(8,128)(2,1)} %cw.1) | copy-start | bytes 24580
  12.1 6.1 %copy-start.5 = (s32[16]{0:T(128)S(1)}, s32[16]{0:T(128)}, u32[]{:S(2)}) copy-start(s32[16]{0:T(128)} %refs_1_.1) | copy-start | bytes 196
  13.4 8.8 %collective-permute-start.2 = (bf16[40,16,128]{2,1,0:T(8,128)(2,1)S(1)}, bf16[40,16,128]{2,1,0:T(8,128)(2,1)S(1)}, u32[]{:S(2)}, u32[]{:S(2)}) collective-permute-start(bf16[40,16,128]{2,1,0:T(8,128)(2,1)S(1)} %get-tuple-element.34.tiles), channel_id=1, source_target_pairs={{0,1},{1,0},{2,3},{3,2},{4,5},{5,4},{6,7},{7,6},{8,9},{9,8},{10,11... | collective-permute-start | bytes 491528 | tf_op jit(solution)/shard_map/ppermute | solution.py:505
  13.5 8.7 %collective-permute-start.3 = (bf16[40,16,128]{2,1,0:T(8,128)(2,1)S(1)}, bf16[40,16,128]{2,1,0:T(8,128)(2,1)S(1)}, u32[]{:S(2)}, u32[]{:S(2)}) collective-permute-start(bf16[40,16,128]{2,1,0:T(8,128)(2,1)S(1)} %get-tuple-element.34.tiles), channel_id=1, source_target_pairs={{0,15},{1,2},{2,1},{3,4},{4,3},{5,6},{6,5},{7,8},{8,7},{9,10},{10,... | collective-permute-start | bytes 491528 | tf_op jit(solution)/shard_map/ppermute | solution.py:506
  16.4 5.8 %collective-permute-start.4 = (bf16[16,128]{1,0:T(8,128)(2,1)S(1)}, bf16[16,128]{1,0:T(8,128)(2,1)S(1)}, u32[]{:S(2)}, u32[]{:S(2)}) collective-permute-start(bf16[16,128]{1,0:T(8,128)(2,1)S(1)} %get-tuple-element.36), channel_id=1, source_target_pairs={{0,15},{1,14},{2,13},{3,12},{4,11},{5,10},{6,9},{7,8},{8,7},{9,6},... | collective-permute-start | bytes 12296 | tf_op jit(solution)/shard_map/ppermute | solution.py:507

commit v4 on v3

--- a/solution.py
+++ b/solution.py
@@ -17,6 +17,7 @@
 
 CHUNK = 256
 STRIP = 32
+ASK = 16
 
 HBM = pl.BlockSpec(memory_space=pltpu.HBM)
 VM = pl.BlockSpec(memory_space=pltpu.VMEM)
@@ -75,34 +76,60 @@
     return lax.rem(lax.axis_index("lon"), 2)
 
 
-def first_kernel(x_hbm, lift_hbm, conv_hbm, fwt_hbm, one, two, x, lift, conv, fwt, sems):
+def list_tiles(mask, chosen, count):
+    for k in range(FOLDB):
+        chosen[k] = count - FOLDB + k
+    for k in range(FOLDB, MAXACT + 1):
+        chosen[k] = count - 1
+    found = jnp.int32(FOLDB)
+    for t in range(count - FOLDB):
+        chosen[jnp.minimum(found, MAXACT)] = t
+        found = found + jnp.where(mask[t] == 1, 1, 0)
+    return jnp.minimum(found, MAXACT)
+
+
+def first_kernel(x_hbm, pair_hbm, mask_hbm, one, two, pair, mask, chosen, sems):
     odd = parity()
-    last = x.shape[0] - 1
+    last = x_hbm.shape[0] - 1
+    chans = x_hbm.shape[1]
     copies = [
-        pltpu.make_async_copy(x_hbm.at[pl.ds(last * (1 - odd), 1)], one, sems.at[0]),
-        pltpu.make_async_copy(x_hbm.at[pl.ds(last * odd, 1)], two, sems.at[1]),
-        pltpu.make_async_copy(x_hbm, x, sems.at[2]),
-        pltpu.make_async_copy(lift_hbm, lift, sems.at[3]),
-        pltpu.make_async_copy(conv_hbm, conv, sems.at[4]),
-        pltpu.make_async_copy(fwt_hbm, fwt, sems.at[5]),
+        pltpu.make_async_copy(mask_hbm, mask, sems.at[0]),
+        pltpu.make_async_copy(pair_hbm, pair, sems.at[1]),
+        pltpu.make_async_copy(x_hbm.at[last * (1 - odd)], one.at[pl.ds(0, chans)], sems.at[2]),
+        pltpu.make_async_copy(x_hbm.at[last * odd], two.at[pl.ds(0, chans)], sems.at[3]),
     ]
     for c in copies:
         c.start()
-    for c in copies:
-        c.wait()
-
-
-def first(x, lift, conv, fwt):
-    column = jax.ShapeDtypeStruct((1,) + x.shape[1:], BF16)
-    given = [pltpu.with_memory_space_constraint(v, pltpu.HBM) for v in (x, lift, conv, fwt)]
+    copies[0].wait()
+    list_tiles(mask, chosen, mask.shape[0])
+    copies[1].wait()
+    lane = lax.broadcasted_iota(jnp.int32, (ASK, 128), 1)
+    for ref, side in ((one, 2 - 2 * odd), (two, 2 * odd)):
+        asked = jnp.zeros((ASK, 128), jnp.int32)
+        for k in range(MAXACT):
+            asked = jnp.where(lane == k, pair[side, chosen[k]], asked)
+        ref[pl.ds(chans, ASK), :128] = asked.astype(F32).astype(BF16)
+        ref[pl.ds(chans, ASK), 128:] = jnp.zeros((ASK, ref.shape[1] - 128), BF16)
+    copies[2].wait()
+    copies[3].wait()
+
+
+def first(x, pair, mask):
+    column = jax.ShapeDtypeStruct((x.shape[1] + ASK, x.shape[2]), BF16)
+    given = [pltpu.with_memory_space_constraint(v, pltpu.HBM) for v in (x, pair, mask)]
     return pl.pallas_call(
         first_kernel,
-        out_shape=(column, column) + tuple(jax.ShapeDtypeStruct(v.shape, BF16) for v in (x, lift, conv, fwt)),
-        in_specs=[HBM] * 4,
-        out_specs=(VM,) * 6,
-        scratch_shapes=[pltpu.SemaphoreType.DMA((6,))],
+        out_shape=(column, column),
+        in_specs=[HBM] * 3,
+        out_specs=(VM, VM),
+        scratch_shapes=[
+            pltpu.SMEM(pair.shape, jnp.int32),
+            pltpu.SMEM(mask.shape, jnp.int32),
+            pltpu.SMEM((MAXACT + 1,), jnp.int32),
+            pltpu.SemaphoreType.DMA((4,)),
+        ],
         compiler_params=pltpu.CompilerParams(vmem_limit_bytes=4 * 2**20),
-        cost_estimate=pl.CostEstimate(flops=0, bytes_accessed=3 * 10**6, transcendentals=0),
+        cost_estimate=pl.CostEstimate(flops=4 * 10**9, bytes_accessed=10**6, transcendentals=0),
         name="first",
     )(*given)
 
@@ -207,14 +234,21 @@
 
 def edge_kernel(
     one, two, flux_in, taps, wc, lt, fwt,
-    edges, tiles, north,
-    halo, flux, ca, cb, la, lb, oa, ob,
+    edges, tiles, north, send_one, send_two,
+    halo, flux, ca, cb, la, lb, oa, ob, asked, ask_one, ask_two, sems,
 ):
-    lats = one.shape[2]
+    lats = one.shape[1]
+    chans = lt.shape[1]
     columns = taps.shape[1] // lats
+    lists = []
+    for i, (ref, to) in enumerate(((one, ask_one), (two, ask_two))):
+        wanted = ref[pl.ds(chans, ASK), :128].astype(F32).astype(jnp.int32)
+        asked[pl.ds(i * ASK, ASK), :] = jnp.clip(wanted, 0, lats // TLAT - 1)
+        lists.append(pltpu.make_async_copy(asked.at[pl.ds(i * ASK, 8)], to, sems.at[i]))
+        lists[-1].start()
     odd = parity()
-    put_shifts(halo, pl.multiple_of(lats * (1 - odd), 128), one[0])
-    put_shifts(halo, pl.multiple_of(lats * odd, 128), two[0])
+    put_shifts(halo, pl.multiple_of(lats * (1 - odd), 128), one[pl.ds(0, chans), :])
+    put_shifts(halo, pl.multiple_of(lats * odd, 128), two[pl.ds(0, chans), :])
     sides = [
         [(halo, 0), (taps, 0), (taps, lats)],
         [(taps, (columns - 2) * lats), (taps, (columns - 1) * lats), (halo, lats)],
@@ -268,10 +302,17 @@
             tiles[g * group + a] = v.astype(BF16)
             if g == lats // 128 - 1 and a == group - 1:
                 north[...] = v.astype(BF16)
+                send_one[MAXACT] = v.astype(BF16)
+                send_two[MAXACT] = v.astype(BF16)
+    for c in lists:
+        c.wait()
+    for k in range(MAXACT):
+        send_one[k] = tiles[ask_one[0, k]]
+        send_two[k] = tiles[ask_two[0, k]]
 
 
 def edge(one, two, flux_in, taps, wc, lt, fwt):
-    lats = one.shape[2]
+    lats = one.shape[1]
     columns = taps.shape[1] // lats
     width, chans = lt.shape
     fluxes = fwt.shape[0]
@@ -282,9 +323,11 @@
             jax.ShapeDtypeStruct((2, width, lats), BF16),
             jax.ShapeDtypeStruct((lats // TLAT, fluxes, cells), BF16),
             jax.ShapeDtypeStruct((fluxes, cells), BF16),
+            jax.ShapeDtypeStruct((MAXACT + 1, fluxes, cells), BF16),
+            jax.ShapeDtypeStruct((MAXACT + 1, fluxes, cells), BF16),
         ),
         in_specs=[VM] * 7,
-        out_specs=(VM, VM, VM),
+        out_specs=(VM,) * 5,
         scratch_shapes=[
             pltpu.VMEM((3 * chans, 2 * lats), BF16),
             pltpu.VMEM((2, fluxes, lats), F32),
@@ -294,28 +337,15 @@
             pltpu.VMEM((width, CHUNK), BF16),
             pltpu.VMEM((width, CHUNK), BF16),
             pltpu.VMEM((width, CHUNK), BF16),
+            pltpu.VMEM((2 * ASK, 128), jnp.int32),
+            pltpu.SMEM((8, 128), jnp.int32),
+            pltpu.SMEM((8, 128), jnp.int32),
+            pltpu.SemaphoreType.DMA((2,)),
         ],
         compiler_params=pltpu.CompilerParams(vmem_limit_bytes=12 * 2**20),
         cost_estimate=pl.CostEstimate(flops=10**9, bytes_accessed=10**6, transcendentals=3 * 10**5),
         name="edge",
     )(one, two, flux_in, taps, wc, lt, fwt)
-
-
-def list_tiles(mask, chosen, count):
-    for k in range(MAXACT):
-        chosen[k] = count - 1
-    for k in range(FOLDB):
-        chosen[k] = count - FOLDB + k
-    found = FOLDB
-    for t in range(count - FOLDB):
-        water = mask[t] == 1
-
-        @pl.when(jnp.logical_and(water, found < MAXACT))
-        def _():
-            chosen[found] = t
-
-        found = found + water.astype(jnp.int32)
-    return found
 
 
 def early_kernel(
@@ -384,7 +414,7 @@
         out_specs=(HBM, HBM, VM, VM, VM, VM),
         scratch_shapes=[
             pltpu.VMEM((width, cells), BF16),
-            pltpu.SMEM((MAXACT,), jnp.int32),
+            pltpu.SMEM((MAXACT + 1,), jnp.int32),
             pltpu.SemaphoreType.DMA((columns + 1,)),
         ],
         compiler_params=pltpu.CompilerParams(vmem_limit_bytes=12 * 2**20),
@@ -394,7 +424,7 @@
 
 
 def late_kernel(
-    pair, mask, one, two, fold, regrid_weight, sums, base, cwt, mwt, given_hbm,
+    mask, one, two, fold, regrid_weight, sums, base, cwt, mwt, given_hbm,
     out_hbm,
     state, mixed, out, chosen, sems,
 ):
@@ -402,20 +432,23 @@
     fluxes = fold.shape[0]
     cells = out.shape[2]
     found = list_tiles(mask, chosen, count)
-    odd = parity() == 1
+    strip, strips = lax.axis_index("lon"), lax.axis_size("lon")
+    odd = lax.rem(strip, 2)
+    met = lax.rem(strip + 2 * odd - 1 + strips, strips) == strips - 1 - strip
+    odd = odd == 1
+    partner = jnp.where(met, two[MAXACT], fold[...])
     ones = jnp.ones(fold.shape, BF16)
     wide = 2 * cells
     totals = []
     for k in range(MAXACT):
         t = chosen[k]
-        pw, pe = pair[0, t], pair[2, t]
-        west = jnp.where(odd, one[pw], two[pw])
-        east = jnp.where(odd, two[pe], one[pe])
+        west = jnp.where(odd, one[k], two[k])
+        east = jnp.where(odd, two[k], one[k])
         got = jnp.concatenate([jnp.concatenate([west, ones], 0), jnp.concatenate([east, ones], 0)], 1)
         weights = jnp.concatenate([regrid_weight[t, 0], regrid_weight[t, 2]], 1)
         total = sums[:, k * cells : (k + 1) * cells] + dot_t(got, weights)
         if k < FOLDB:
-            total = total + dot_t(jnp.concatenate([fold[...], ones], 0), regrid_weight[t, 3])
+            total = total + dot_t(jnp.concatenate([partner, ones], 0), regrid_weight[t, 3])
         totals.append(total)
     for p in range(MAXACT // 2):
         at = slice(p * wide, p * wide + wide)
@@ -451,31 +484,31 @@
             pltpu.make_async_copy(out.at[k], out_hbm.at[0], sems.at[k]).wait()
 
 
-def late(pair, mask, one, two, fold, regrid, sums, base, cwt, mwt, given):
+def late(mask, one, two, fold, regrid, sums, base, cwt, mwt, given):
     count, width, cells = given.shape
 
     def body(*refs):
-        head, (state, ma, mb, out, chosen, sems) = refs[:12], refs[12:]
+        head, (state, ma, mb, out, chosen, sems) = refs[:11], refs[11:]
         late_kernel(*head, state, (ma, mb), out, chosen, sems)
 
     return pl.pallas_call(
         body,
         out_shape=jax.ShapeDtypeStruct((count, width, cells), BF16),
-        in_specs=[SM, SM, VM, VM, VM, VM, VM, VM, VM, VM, HBM],
+        in_specs=[SM, VM, VM, VM, VM, VM, VM, VM, VM, HBM],
         out_specs=HBM,
         scratch_shapes=[
             pltpu.VMEM((width, MAXACT * cells), BF16),
             pltpu.VMEM((width, 2 * cells), F32),
             pltpu.VMEM((width, 2 * cells), F32),
             pltpu.VMEM((MAXACT, width, cells), BF16),
-            pltpu.SMEM((MAXACT,), jnp.int32),
+            pltpu.SMEM((MAXACT + 1,), jnp.int32),
             pltpu.SemaphoreType.DMA((MAXACT,)),
         ],
-        input_output_aliases={10: 0},
+        input_output_aliases={9: 0},
         compiler_params=pltpu.CompilerParams(vmem_limit_bytes=12 * 2**20),
         cost_estimate=pl.CostEstimate(flops=10**9, bytes_accessed=10**6, transcendentals=3 * 10**5),
         name="late",
-    )(pair, mask, one, two, fold, regrid, sums, base, cwt, mwt, given)
+    )(mask, one, two, fold, regrid, sums, base, cwt, mwt, given)
 
 
 def per_device(
@@ -494,24 +527,23 @@
     strips = lax.axis_size("lon")
     inward = [(i, i ^ 1) for i in range(strips)]
     outward = [(i, (i + 1 if i % 2 else i - 1) % strips) for i in range(strips)]
-    mirror = [(i, strips - 1 - i) for i in range(strips)]
+    met = dict(outward)
+    mirror = [(i, strips - 1 - i) for i in range(strips) if met[i] != strips - 1 - i]
     fwt = flux_weight.T
     pair = pair_tile.T
-    send_one, send_two, x, lift, conv, fwt = first(atm_in, lift_weight, conv_weight, fwt)
+    send_one, send_two = first(atm_in, pair, ocean_mask)
+    two = lax.ppermute(send_two, "lon", outward)
+    one = lax.ppermute(send_one, "lon", inward)
+    hid, flux, taps, wc, lt = interior(atm_in, lift_weight, conv_weight, fwt)
+    edges, tiles, north, send_one, send_two = edge(one, two, flux, taps, wc, lt, fwt)
     one = lax.ppermute(send_one, "lon", inward)
     two = lax.ppermute(send_two, "lon", outward)
-    hid, flux, taps, wc, lt = interior(x, lift, conv, fwt)
-    edges, tiles, north = edge(one, two, flux, taps, wc, lt, fwt)
-    tiles_one = lax.ppermute(tiles, "lon", inward)
-    tiles_two = lax.ppermute(tiles, "lon", outward)
     fold = lax.ppermute(north, "lon", mirror)
     atm_hidden, given, sums, base, cwt, mwt = early(
         hid, edges, pair, ocean_mask, tiles, ocean_in, regrid_weight,
         ocean_weight, couple_weight, mix_weight,
     )
-    ocean_hidden = late(
-        pair, ocean_mask, tiles_one, tiles_two, fold, regrid_weight, sums, base, cwt, mwt, given
-    )
+    ocean_hidden = late(ocean_mask, one, two, fold, regrid_weight, sums, base, cwt, mwt, given)
     return (atm_hidden, ocean_hidden)
 
 

time: 24.4 us -> 24.5 us (level)
  starting transfers between devices: 10.9 us -> 9.78 us
  waiting for transfers between devices: 1.4 us -> 2.39 us
    ppermute x2 -> x0, starting transfers between devices: 2.86 us -> none  [the longest x1 2.79 us: per_device(): tiles_two = lax.ppermute(tiles, 'lon', outward)]
    ppermute x1 -> x2, waiting for transfers between devices: 0.01 us -> 2.38 us  [per_device(): two = lax.ppermute(send_two, 'lon', outward)]
    ppermute x1 -> x2, starting transfers between devices: 0.56 us -> 2.49 us  [per_device(): one = lax.ppermute(send_one, 'lon', inward)]
    ppermute x1, waiting for transfers between devices: 1.39 us -> 0.01 us  [per_device(): fold = lax.ppermute(north, 'lon', mirror)]
    ppermute x1, starting transfers between devices: 1.78 us -> 0.66 us  [per_device(): fold = lax.ppermute(north, 'lon', mirror)]
    ppermute x1 -> x2, starting transfers between devices: 5.66 us -> 6.62 us  [per_device(): two = lax.ppermute(send_two, 'lon', outward)]
    pallas_call x1, Pallas kernels: 1.31 us -> 1.95 us  [edge(): pl.pallas_call(edge_kernel, out_shape=(jax.ShapeDtypeStruct((2, width, la...]
    pallas_call x1, Pallas kernels: 1.57 us -> 1.02 us  [first(): pl.pallas_call(first_kernel, out_shape=(column, column), in_specs=[HBM] *...]
  transfers between devices with their start and end apart: 5 -> 5, of which waited for: 1 -> 1; matrix products, arithmetic and copies ran while one was open for 0% -> 0% of each run, Pallas kernels for 25% -> 26%
where the time goes in v4:
time: 24.5 us; the launch traced here: 24.3 us
  Pallas kernels  11.2 us (46%)
  starting transfers between devices  9.78 us (40%)
  waiting for transfers between devices  2.39 us (10%)
  between operations  0.82 us (3%)
    ppermute x2, starting transfers between devices, per_device(): two = lax.ppermute(send_two, 'lon', outward)  6.62 us
    pallas_call x1, Pallas kernels, interior(): pl.pallas_call(inner_kernel, out_shape=(jax.ShapeDtypeStruct((width, inne...  3.56 us
    pallas_call x1, Pallas kernels, early(): pl.pallas_call(early_kernel, out_shape=(jax.ShapeDtypeStruct((columns, wi...  2.67 us
    ppermute x2, starting transfers between devices, per_device(): one = lax.ppermute(send_one, 'lon', inward)  2.49 us
    ppermute x2, waiting for transfers between devices, per_device(): two = lax.ppermute(send_two, 'lon', outward)  2.38 us
    pallas_call x1, Pallas kernels, late(): pl.pallas_call(body, out_shape=jax.ShapeDtypeStruct((count, width, cells)...  1.96 us
    pallas_call x1, Pallas kernels, edge(): pl.pallas_call(edge_kernel, out_shape=(jax.ShapeDtypeStruct((2, width, la...  1.95 us
    pallas_call x1, Pallas kernels, first(): pl.pallas_call(first_kernel, out_shape=(column, column), in_specs=[HBM] *...  1.02 us
  transfers between devices with their start and end apart: 5, of which 1 were waited for; matrix products, arithmetic and copies ran while one was open for 0% of the time, Pallas kernels for 26%

profile of v4, /device:TPU:0, one launch (start us, length us, event | category | flops | bytes accessed | tf_op | source)
XLA Modules:
  0.0 24.3 jit_solution(147551144344576964)
XLA Ops:
  0.6 0.0 copy-start.6
  0.6 0.0 copy-start.7
  0.7 0.0 copy-start.8
  0.7 0.0 copy-start.9
  0.7 1.0 %first.1 = (bf16[64,640]{1,0:T(8,128)(2,1)S(1)}, bf16[64,640]{1,0:T(8,128)(2,1)S(1)}) custom-call(bf16[8,48,640]{2,1,0:T(8,128)(2,1)} %x_hbm.1, s32[3,16]{1,0:T(4,128)} %bitcast.2, s32[16]{0:T(128)} %refs_0_.1), custom_call_target="tpu_custom_call" | custom-call | flops 4000000000 | bytes 1000000 | tf_op jit(solution)/shard_map/first/pallas_call | solution.py:120
  1.7 0.6 %collective-permute-start = (bf16[64,640]{1,0:T(8,128)(2,1)S(1)}, bf16[64,640]{1,0:T(8,128)(2,1)S(1)}, u32[]{:S(2)}, u32[]{:S(2)}) collective-permute-start(bf16[64,640]{1,0:T(8,128)(2,1)S(1)} %get-tuple-element.21), channel_id=1, source_target_pairs={{0,1},{1,0},{2,3},{3,2},{4,5},{5,4},{6,7},{7,6},{8,9},{9,8},{10,11... | collective-permute-start | bytes 245768 | tf_op jit(solution)/shard_map/ppermute | solution.py:536
  2.3 5.7 %collective-permute-start.1 = (bf16[64,640]{1,0:T(8,128)(2,1)S(1)}, bf16[64,640]{1,0:T(8,128)(2,1)S(1)}, u32[]{:S(2)}, u32[]{:S(2)}) collective-permute-start(bf16[64,640]{1,0:T(8,128)(2,1)S(1)} %get-tuple-element.22), channel_id=1, source_target_pairs={{0,15},{1,2},{2,1},{3,4},{4,3},{5,6},{6,5},{7,8},{8,7},{9,10},{10,... | collective-permute-start | bytes 245768 | tf_op jit(solution)/shard_map/ppermute | solution.py:535
  7.9 0.0 copy-done.6
  7.9 0.0 copy-done.7
  7.9 0.0 copy-done.8
  7.9 0.0 copy-done.9
  7.9 0.0 copy-start.10
  7.9 3.6 %interior.1 = (bf16[256,3840]{1,0:T(8,128)(2,1)S(1)}, f32[16,3840]{1,0:T(8,128)S(1)}, bf16[144,5120]{1,0:T(8,128)(2,1)S(1)}, bf16[256,512]{1,0:T(8,128)(2,1)S(1)}, bf16[256,48]{1,0:T(8,128)(2,1)S(1)}) custom-call(bf16[8,48,640]{2,1,0:T(8,128)(2,1)S(1)} %copy-done.7, bf16[48,256]{1,0:T(8,128)(2,1)S(1)} %copy-done.8, bf16[3,3,256,256]{3,2,1,0:T(8,128)(2,1)S(1)} %copy-done.6, ...), custom_call_target="tpu_custom_call" | custom-call | flops 4000000000 | bytes 4000000 | tf_op jit(solution)/shard_map/interior/pallas_call | solution.py:190
  11.5 0.0 copy-done.10
  11.5 0.1 copy.14.ocean
  11.6 0.0 copy-start
  11.6 0.0 copy-start.1
  11.6 0.0 copy-start.2
  11.7 0.0 copy-start.3
  11.7 0.0 copy-start.4
  11.7 0.0 copy-start.5
  11.7 0.0 collective-permute-done.one
  11.7 0.0 collective-permute-done.1.two
  11.7 1.9 %edge.1 = (bf16[2,256,640]{2,1,0:T(8,128)(2,1)S(1)}, bf16[40,16,128]{2,1,0:T(8,128)(2,1)S(1)}, bf16[16,128]{1,0:T(8,128)(2,1)S(1)}, bf16[9,16,128]{2,1,0:T(8,128)(2,1)S(1)}, bf16[9,16,128]{2,1,0:T(8,128)(2,1)S(1)}) custom-call(bf16[64,640]{1,0:T(8,128)(2,1)S(1)} %collective-permute-done.one, bf16[64,640]{1,0:T(8,128)(2,1)S(1)} %collective-permute-done.1.two, ...), custom_call_target="tpu_custom_call" | custom-call | flops 1000000000 | bytes 1000000 | tf_op jit(solution)/shard_map/edge/pallas_call | solution.py:320
  13.7 0.7 %collective-permute-start.4 = (bf16[16,128]{1,0:T(8,128)(2,1)S(1)}, bf16[16,128]{1,0:T(8,128)(2,1)S(1)}, u32[]{:S(2)}, u32[]{:S(2)}) collective-permute-start(bf16[16,128]{1,0:T(8,128)(2,1)S(1)} %get-tuple-element.32), channel_id=1, source_target_pairs={{1,14},{2,13},{3,12},{4,11},{5,10},{6,9},{9,6},{10,5},{11,4},{12,3... | collective-permute-start | bytes 12296 | tf_op jit(solution)/shard_map/ppermute | solution.py:541
  14.3 1.9 %collective-permute-start.2 = (bf16[9,16,128]{2,1,0:T(8,128)(2,1)S(1)}, bf16[9,16,128]{2,1,0:T(8,128)(2,1)S(1)}, u32[]{:S(2)}, u32[]{:S(2)}) collective-permute-start(bf16[9,16,128]{2,1,0:T(8,128)(2,1)S(1)} %get-tuple-element.30), channel_id=1, source_target_pairs={{0,1},{1,0},{2,3},{3,2},{4,5},{5,4},{6,7},{7,6},{8,9},{9,8},{10,11... | collective-permute-start | bytes 110600 | tf_op jit(solution)/shard_map/ppermute | solution.py:539
  16.3 1.0 %collective-permute-start.3 = (bf16[9,16,128]{2,1,0:T(8,128)(2,1)S(1)}, bf16[9,16,128]{2,1,0:T(8,128)(2,1)S(1)}, u32[]{:S(2)}, u32[]{:S(2)}) collective-permute-start(bf16[9,16,128]{2,1,0:T(8,128)(2,1)S(1)} %get-tuple-element.31), channel_id=1, source_target_pairs={{0,15},{1,2},{2,1},{3,4},{4,3},{5,6},{6,5},{7,8},{8,7},{9,10},{10,... | collective-permute-start | bytes 110600 | tf_op jit(solution)/shard_map/ppermute | solution.py:540
  17.2 0.0 copy-done
  17.2 0.0 copy-done.1
  17.2 0.0 copy-done.2
  17.2 0.0 copy-done.3
  17.3 0.0 copy-done.4
  17.3 0.0 copy-done.5
  17.3 2.7 %early.1 = (bf16[8,256,640]{2,1,0:T(8,128)(2,1)}, bf16[16,256,128]{2,1,0:T(8,128)(2,1)}, f32[32,1024]{1,0:T(8,128)S(1)}, f32[256,1024]{1,0:T(8,128)S(1)}, bf16[2...) custom-call(bf16[256,3840]{1,0:T(8,128)(2,1)S(1)} %get-tuple-element.20.hid, ...), custom_call_target="tpu_custom_call" | custom-call | flops 1000000000 | bytes 6000000 | tf_op jit(solution)/shard_map/early/pallas_call | solution.py:403
  20.0 0.0 collective-permute-done.4.refs_3_
  20.0 0.0 collective-permute-done.2.refs_1_
  20.0 2.4 %collective-permute-done.3.refs_2_ = bf16[9,16,128]{2,1,0:T(8,128)(2,1)S(1)} collective-permute-done((bf16[9,16,128]{2,1,0:T(8,128)(2,1)S(1)}, bf16[9,16,128]{2,1,0:T(8,128)(2,1)S(1)}, u32[]{:S(2)}, u32[]{:S(2)}) %collective-permute-start.3) | collective-permute-done | bytes 36896 | tf_op jit(solution)/shard_map/ppermute | solution.py:540
  22.4 2.0 %late.1 = bf16[16,256,128]{2,1,0:T(8,128)(2,1)} custom-call(s32[16]{0:T(128)S(1)} %copy-done.5, bf16[9,16,128]{2,1,0:T(8,128)(2,1)S(1)} %collective-permute-done.2.refs_1_, bf16[9,16,128]{2,1,0:T(8,128)(2,1)S(1)} %collective-permute-done.3.refs_2_, bf16[16,128]{1,0:T(8,128)(2,1)S(1)} %collective-permute-done.4.refs_3_, ...), custom_call_target="tpu_custom_call", output_to_operand_aliasing={{}: (9, {})} | custom-call | flops 1000000000 | bytes 1000000 | tf_op jit(solution)/shard_map/late/pallas_call | solution.py:494
Async XLA Ops:
  0.6 7.3 %copy-start.6 = (bf16[3,3,256,256]{3,2,1,0:T(8,128)(2,1)S(1)}, bf16[3,3,256,256]{3,2,1,0:T(8,128)(2,1)}, u32[]{:S(2)}) copy-start(bf16[3,3,256,256]{3,2,1,0:T(8,128)(2,1)} %conv.1) | copy-start | bytes 3538948
  0.6 7.3 %copy-start.7 = (bf16[8,48,640]{2,1,0:T(8,128)(2,1)S(1)}, bf16[8,48,640]{2,1,0:T(8,128)(2,1)}, u32[]{:S(2)}) copy-start(bf16[8,48,640]{2,1,0:T(8,128)(2,1)} %x_hbm.1) | copy-start | bytes 1474564
  0.7 7.3 %copy-start.8 = (bf16[48,256]{1,0:T(8,128)(2,1)S(1)}, bf16[48,256]{1,0:T(8,128)(2,1)}, u32[]{:S(2)}) copy-start(bf16[48,256]{1,0:T(8,128)(2,1)} %lift.1) | copy-start | bytes 73732
  0.7 7.3 %copy-start.9 = (bf16[256,16]{0,1:T(8,128)(2,1)S(1)}, bf16[256,16]{0,1:T(8,128)(2,1)}, u32[]{:S(2)}) copy-start(bf16[256,16]{0,1:T(8,128)(2,1)} %param.15) | copy-start | bytes 24580
  1.7 10.0 %collective-permute-start = (bf16[64,640]{1,0:T(8,128)(2,1)S(1)}, bf16[64,640]{1,0:T(8,128)(2,1)S(1)}, u32[]{:S(2)}, u32[]{:S(2)}) collective-permute-start(bf16[64,640]{1,0:T(8,128)(2,1)S(1)} %get-tuple-element.21), channel_id=1, source_target_pairs={{0,1},{1,0},{2,3},{3,2},{4,5},{5,4},{6,7},{7,6},{8,9},{9,8},{10,11... | collective-permute-start | bytes 245768 | tf_op jit(solution)/shard_map/ppermute | solution.py:536
  2.3 9.4 %collective-permute-start.1 = (bf16[64,640]{1,0:T(8,128)(2,1)S(1)}, bf16[64,640]{1,0:T(8,128)(2,1)S(1)}, u32[]{:S(2)}, u32[]{:S(2)}) collective-permute-start(bf16[64,640]{1,0:T(8,128)(2,1)S(1)} %get-tuple-element.22), channel_id=1, source_target_pairs={{0,15},{1,2},{2,1},{3,4},{4,3},{5,6},{6,5},{7,8},{8,7},{9,10},{10,... | collective-permute-start | bytes 245768 | tf_op jit(solution)/shard_map/ppermute | solution.py:535
  7.9 3.6 %copy-start.10 = (bf16[16,95,128]{2,0,1:T(8,128)(2,1)S(1)}, bf16[16,95,128]{2,0,1:T(8,128)(2,1)}, u32[]{:S(2)}) copy-start(bf16[16,95,128]{2,0,1:T(8,128)(2,1)} %param.12) | copy-start | bytes 1167364
  11.6 5.6 %copy-start = (bf16[16,4,128,128]{3,2,1,0:T(8,128)(2,1)S(1)}, bf16[16,4,128,128]{3,2,1,0:T(8,128)(2,1)}, u32[]{:S(2)}) copy-start(bf16[16,4,128,128]{3,2,1,0:T(8,128)(2,1)} %refs_4_.1) | copy-start | bytes 6291460
  11.6 5.6 %copy-start.1 = (bf16[256,256]{1,0:T(8,128)(2,1)S(1)}, bf16[256,256]{1,0:T(8,128)(2,1)}, u32[]{:S(2)}) copy-start(bf16[256,256]{1,0:T(8,128)(2,1)} %mw.1) | copy-start | bytes 393220
  11.6 5.6 %copy-start.2 = (bf16[95,256]{1,0:T(8,128)(2,1)S(1)}, bf16[95,256]{1,0:T(8,128)(2,1)}, u32[]{:S(2)}) copy-start(bf16[95,256]{1,0:T(8,128)(2,1)} %ow.1) | copy-start | bytes 145924
  11.7 5.6 %copy-start.3 = (bf16[16,256]{1,0:T(8,128)(2,1)S(1)}, bf16[16,256]{1,0:T(8,128)(2,1)}, u32[]{:S(2)}) copy-start(bf16[16,256]{1,0:T(8,128)(2,1)} %cw.1) | copy-start | bytes 24580
  11.7 5.6 %copy-start.4 = (s32[16,3]{0,1:T(4,128)S(1)}, s32[16,3]{0,1:T(4,128)}, u32[]{:S(2)}) copy-start(s32[16,3]{0,1:T(4,128)} %param.20) | copy-start | bytes 580
  11.7 5.6 %copy-start.5 = (s32[16]{0:T(128)S(1)}, s32[16]{0:T(128)}, u32[]{:S(2)}) copy-start(s32[16]{0:T(128)} %refs_0_.1) | copy-start | bytes 196
  13.7 6.3 %collective-permute-start.4 = (bf16[16,128]{1,0:T(8,128)(2,1)S(1)}, bf16[16,128]{1,0:T(8,128)(2,1)S(1)}, u32[]{:S(2)}, u32[]{:S(2)}) collective-permute-start(bf16[16,128]{1,0:T(8,128)(2,1)S(1)} %get-tuple-element.32), channel_id=1, source_target_pairs={{1,14},{2,13},{3,12},{4,11},{5,10},{6,9},{9,6},{10,5},{11,4},{12,3... | collective-permute-start | bytes 12296 | tf_op jit(solution)/shard_map/ppermute | solution.py:541
  14.3 5.6 %collective-permute-start.2 = (bf16[9,16,128]{2,1,0:T(8,128)(2,1)S(1)}, bf16[9,16,128]{2,1,0:T(8,128)(2,1)S(1)}, u32[]{:S(2)}, u32[]{:S(2)}) collective-permute-start(bf16[9,16,128]{2,1,0:T(8,128)(2,1)S(1)} %get-tuple-element.30), channel_id=1, source_target_pairs={{0,1},{1,0},{2,3},{3,2},{4,5},{5,4},{6,7},{7,6},{8,9},{9,8},{10,11... | collective-permute-start | bytes 110600 | tf_op jit(solution)/shard_map/ppermute | solution.py:539
  16.3 6.1 %collective-permute-start.3 = (bf16[9,16,128]{2,1,0:T(8,128)(2,1)S(1)}, bf16[9,16,128]{2,1,0:T(8,128)(2,1)S(1)}, u32[]{:S(2)}, u32[]{:S(2)}) collective-permute-start(bf16[9,16,128]{2,1,0:T(8,128)(2,1)S(1)} %get-tuple-element.31), channel_id=1, source_target_pairs={{0,15},{1,2},{2,1},{3,4},{4,3},{5,6},{6,5},{7,8},{8,7},{9,10},{10,... | collective-permute-start | bytes 110600 | tf_op jit(solution)/shard_map/ppermute | solution.py:540

commit v5 on v4

--- a/solution.py
+++ b/solution.py
@@ -1,11 +1,10 @@
-import functools
-
 import jax
 import jax.numpy as jnp
 from jax import lax
 from jax.experimental import pallas as pl
 from jax.experimental.pallas import tpu as pltpu
 from jax.sharding import PartitionSpec as P
+
 
 TLAT = 16
 MAXACT = 8
@@ -244,7 +243,7 @@
     for i, (ref, to) in enumerate(((one, ask_one), (two, ask_two))):
         wanted = ref[pl.ds(chans, ASK), :128].astype(F32).astype(jnp.int32)
         asked[pl.ds(i * ASK, ASK), :] = jnp.clip(wanted, 0, lats // TLAT - 1)
-        lists.append(pltpu.make_async_copy(asked.at[pl.ds(i * ASK, 8)], to, sems.at[i]))
+        lists.append(pltpu.make_async_copy(asked.at[pl.ds(i * ASK, 1)], to, sems.at[i]))
         lists[-1].start()
     odd = parity()
     put_shifts(halo, pl.multiple_of(lats * (1 - odd), 128), one[pl.ds(0, chans), :])
@@ -338,8 +337,8 @@
             pltpu.VMEM((width, CHUNK), BF16),
             pltpu.VMEM((width, CHUNK), BF16),
             pltpu.VMEM((2 * ASK, 128), jnp.int32),
-            pltpu.SMEM((8, 128), jnp.int32),
-            pltpu.SMEM((8, 128), jnp.int32),
+            pltpu.SMEM((1, 128), jnp.int32),
+            pltpu.SMEM((1, 128), jnp.int32),
             pltpu.SemaphoreType.DMA((2,)),
         ],
         compiler_params=pltpu.CompilerParams(vmem_limit_bytes=12 * 2**20),
@@ -562,6 +561,7 @@
         P("lon"),
     )
     out_specs = (P(("groups", "lon"), None, None), P(("groups", "lon"), None, None))
+
     return jax.shard_map(
         per_device, mesh=mesh, in_specs=in_specs, out_specs=out_specs, check_vma=False
     )

time: 24.5 us -> 24.5 us (level)
  transfers between devices with their start and end apart: 5 -> 5, of which waited for: 1 -> 1; matrix products, arithmetic and copies ran while one was open for 0% -> 0% of each run, Pallas kernels for 26% -> 25%
where the time goes in v5:
time: 24.5 us; the launch traced here: 24.4 us
  Pallas kernels  11.1 us (45%)
  starting transfers between devices  9.78 us (40%)
  waiting for transfers between devices  2.52 us (10%)
  between operations  0.82 us (3%)
    ppermute x2, starting transfers between devices, per_device(): two = lax.ppermute(send_two, 'lon', outward)  6.62 us
    pallas_call x1, Pallas kernels, interior(): pl.pallas_call(inner_kernel, out_shape=(jax.ShapeDtypeStruct((width, inne...  3.56 us
    pallas_call x1, Pallas kernels, early(): pl.pallas_call(early_kernel, out_shape=(jax.ShapeDtypeStruct((columns, wi...  2.55 us
    ppermute x2, waiting for transfers between devices, per_device(): two = lax.ppermute(send_two, 'lon', outward)  2.51 us
    ppermute x2, starting transfers between devices, per_device(): one = lax.ppermute(send_one, 'lon', inward)  2.49 us
    pallas_call x1, Pallas kernels, late(): pl.pallas_call(body, out_shape=jax.ShapeDtypeStruct((count, width, cells)...  2.14 us
    pallas_call x1, Pallas kernels, edge(): pl.pallas_call(edge_kernel, out_shape=(jax.ShapeDtypeStruct((2, width, la...  1.84 us
    pallas_call x1, Pallas kernels, first(): pl.pallas_call(first_kernel, out_shape=(column, column), in_specs=[HBM] *...  1.02 us
  transfers between devices with their start and end apart: 5, of which 1 were waited for; matrix products, arithmetic and copies ran while one was open for 0% of the time, Pallas kernels for 25%

profile of v5, /device:TPU:0, one launch (start us, length us, event | category | flops | bytes accessed | tf_op | source)
XLA Modules:
  0.0 24.4 jit_solution(8545872674776475486)
XLA Ops:
  0.6 0.0 copy-start.6
  0.6 0.0 copy-start.7
  0.7 0.0 copy-start.8
  0.7 0.0 copy-start.9
  0.7 1.0 %first.1 = (bf16[64,640]{1,0:T(8,128)(2,1)S(1)}, bf16[64,640]{1,0:T(8,128)(2,1)S(1)}) custom-call(bf16[8,48,640]{2,1,0:T(8,128)(2,1)} %x_hbm.1, s32[3,16]{1,0:T(4,128)} %bitcast.2, s32[16]{0:T(128)} %refs_0_.1), custom_call_target="tpu_custom_call" | custom-call | flops 4000000000 | bytes 1000000 | tf_op jit(solution)/shard_map/first/pallas_call | solution.py:119
  1.7 0.6 %collective-permute-start = (bf16[64,640]{1,0:T(8,128)(2,1)S(1)}, bf16[64,640]{1,0:T(8,128)(2,1)S(1)}, u32[]{:S(2)}, u32[]{:S(2)}) collective-permute-start(bf16[64,640]{1,0:T(8,128)(2,1)S(1)} %get-tuple-element.21), channel_id=1, source_target_pairs={{0,1},{1,0},{2,3},{3,2},{4,5},{5,4},{6,7},{7,6},{8,9},{9,8},{10,11... | collective-permute-start | bytes 245768 | tf_op jit(solution)/shard_map/ppermute | solution.py:535
  2.3 5.7 %collective-permute-start.1 = (bf16[64,640]{1,0:T(8,128)(2,1)S(1)}, bf16[64,640]{1,0:T(8,128)(2,1)S(1)}, u32[]{:S(2)}, u32[]{:S(2)}) collective-permute-start(bf16[64,640]{1,0:T(8,128)(2,1)S(1)} %get-tuple-element.22), channel_id=1, source_target_pairs={{0,15},{1,2},{2,1},{3,4},{4,3},{5,6},{6,5},{7,8},{8,7},{9,10},{10,... | collective-permute-start | bytes 245768 | tf_op jit(solution)/shard_map/ppermute | solution.py:534
  7.9 0.0 copy-done.6
  7.9 0.0 copy-done.7
  7.9 0.0 copy-done.8
  7.9 0.0 copy-done.9
  7.9 0.0 copy-start.10
  7.9 3.6 %interior.1 = (bf16[256,3840]{1,0:T(8,128)(2,1)S(1)}, f32[16,3840]{1,0:T(8,128)S(1)}, bf16[144,5120]{1,0:T(8,128)(2,1)S(1)}, bf16[256,512]{1,0:T(8,128)(2,1)S(1)}, bf16[256,48]{1,0:T(8,128)(2,1)S(1)}) custom-call(bf16[8,48,640]{2,1,0:T(8,128)(2,1)S(1)} %copy-done.7, bf16[48,256]{1,0:T(8,128)(2,1)S(1)} %copy-done.8, bf16[3,3,256,256]{3,2,1,0:T(8,128)(2,1)S(1)} %copy-done.6, ...), custom_call_target="tpu_custom_call" | custom-call | flops 4000000000 | bytes 4000000 | tf_op jit(solution)/shard_map/interior/pallas_call | solution.py:189
  11.5 0.0 copy-done.10
  11.5 0.1 copy.14.ocean
  11.6 0.0 copy-start
  11.6 0.0 copy-start.1
  11.6 0.0 copy-start.2
  11.7 0.0 copy-start.3
  11.7 0.0 copy-start.4
  11.7 0.0 copy-start.5
  11.7 0.0 collective-permute-done.one
  11.7 0.0 collective-permute-done.1.two
  11.7 1.8 %edge.1 = (bf16[2,256,640]{2,1,0:T(8,128)(2,1)S(1)}, bf16[40,16,128]{2,1,0:T(8,128)(2,1)S(1)}, bf16[16,128]{1,0:T(8,128)(2,1)S(1)}, bf16[9,16,128]{2,1,0:T(8,128)(2,1)S(1)}, bf16[9,16,128]{2,1,0:T(8,128)(2,1)S(1)}) custom-call(bf16[64,640]{1,0:T(8,128)(2,1)S(1)} %collective-permute-done.one, bf16[64,640]{1,0:T(8,128)(2,1)S(1)} %collective-permute-done.1.two, ...), custom_call_target="tpu_custom_call" | custom-call | flops 1000000000 | bytes 1000000 | tf_op jit(solution)/shard_map/edge/pallas_call | solution.py:319
  13.6 0.7 %collective-permute-start.4 = (bf16[16,128]{1,0:T(8,128)(2,1)S(1)}, bf16[16,128]{1,0:T(8,128)(2,1)S(1)}, u32[]{:S(2)}, u32[]{:S(2)}) collective-permute-start(bf16[16,128]{1,0:T(8,128)(2,1)S(1)} %get-tuple-element.32), channel_id=1, source_target_pairs={{1,14},{2,13},{3,12},{4,11},{5,10},{6,9},{9,6},{10,5},{11,4},{12,3... | collective-permute-start | bytes 12296 | tf_op jit(solution)/shard_map/ppermute | solution.py:540
  14.2 1.9 %collective-permute-start.2 = (bf16[9,16,128]{2,1,0:T(8,128)(2,1)S(1)}, bf16[9,16,128]{2,1,0:T(8,128)(2,1)S(1)}, u32[]{:S(2)}, u32[]{:S(2)}) collective-permute-start(bf16[9,16,128]{2,1,0:T(8,128)(2,1)S(1)} %get-tuple-element.30), channel_id=1, source_target_pairs={{0,1},{1,0},{2,3},{3,2},{4,5},{5,4},{6,7},{7,6},{8,9},{9,8},{10,11... | collective-permute-start | bytes 110600 | tf_op jit(solution)/shard_map/ppermute | solution.py:538
  16.2 1.0 %collective-permute-start.3 = (bf16[9,16,128]{2,1,0:T(8,128)(2,1)S(1)}, bf16[9,16,128]{2,1,0:T(8,128)(2,1)S(1)}, u32[]{:S(2)}, u32[]{:S(2)}) collective-permute-start(bf16[9,16,128]{2,1,0:T(8,128)(2,1)S(1)} %get-tuple-element.31), channel_id=1, source_target_pairs={{0,15},{1,2},{2,1},{3,4},{4,3},{5,6},{6,5},{7,8},{8,7},{9,10},{10,... | collective-permute-start | bytes 110600 | tf_op jit(solution)/shard_map/ppermute | solution.py:539
  17.1 0.0 copy-done
  17.1 0.0 copy-done.1
  17.1 0.0 copy-done.2
  17.1 0.0 copy-done.3
  17.1 0.0 copy-done.4
  17.2 0.0 copy-done.5
  17.2 2.5 %early.1 = (bf16[8,256,640]{2,1,0:T(8,128)(2,1)}, bf16[16,256,128]{2,1,0:T(8,128)(2,1)}, f32[32,1024]{1,0:T(8,128)S(1)}, f32[256,1024]{1,0:T(8,128)S(1)}, bf16[2...) custom-call(bf16[256,3840]{1,0:T(8,128)(2,1)S(1)} %get-tuple-element.20.hid, ...), custom_call_target="tpu_custom_call" | custom-call | flops 1000000000 | bytes 6000000 | tf_op jit(solution)/shard_map/early/pallas_call | solution.py:402
  19.7 0.0 collective-permute-done.4.refs_3_
  19.7 0.0 collective-permute-done.2.refs_1_
  19.7 2.5 %collective-permute-done.3.refs_2_ = bf16[9,16,128]{2,1,0:T(8,128)(2,1)S(1)} collective-permute-done((bf16[9,16,128]{2,1,0:T(8,128)(2,1)S(1)}, bf16[9,16,128]{2,1,0:T(8,128)(2,1)S(1)}, u32[]{:S(2)}, u32[]{:S(2)}) %collective-permute-start.3) | collective-permute-done | bytes 36896 | tf_op jit(solution)/shard_map/ppermute | solution.py:539
  22.2 2.1 %late.1 = bf16[16,256,128]{2,1,0:T(8,128)(2,1)} custom-call(s32[16]{0:T(128)S(1)} %copy-done.5, bf16[9,16,128]{2,1,0:T(8,128)(2,1)S(1)} %collective-permute-done.2.refs_1_, bf16[9,16,128]{2,1,0:T(8,128)(2,1)S(1)} %collective-permute-done.3.refs_2_, bf16[16,128]{1,0:T(8,128)(2,1)S(1)} %collective-permute-done.4.refs_3_, ...), custom_call_target="tpu_custom_call", output_to_operand_aliasing={{}: (9, {})} | custom-call | flops 1000000000 | bytes 1000000 | tf_op jit(solution)/shard_map/late/pallas_call | solution.py:493
Async XLA Ops:
  0.6 7.3 %copy-start.6 = (bf16[3,3,256,256]{3,2,1,0:T(8,128)(2,1)S(1)}, bf16[3,3,256,256]{3,2,1,0:T(8,128)(2,1)}, u32[]{:S(2)}) copy-start(bf16[3,3,256,256]{3,2,1,0:T(8,128)(2,1)} %conv.1) | copy-start | bytes 3538948
  0.6 7.3 %copy-start.7 = (bf16[8,48,640]{2,1,0:T(8,128)(2,1)S(1)}, bf16[8,48,640]{2,1,0:T(8,128)(2,1)}, u32[]{:S(2)}) copy-start(bf16[8,48,640]{2,1,0:T(8,128)(2,1)} %x_hbm.1) | copy-start | bytes 1474564
  0.7 7.3 %copy-start.8 = (bf16[48,256]{1,0:T(8,128)(2,1)S(1)}, bf16[48,256]{1,0:T(8,128)(2,1)}, u32[]{:S(2)}) copy-start(bf16[48,256]{1,0:T(8,128)(2,1)} %lift.1) | copy-start | bytes 73732
  0.7 7.3 %copy-start.9 = (bf16[256,16]{0,1:T(8,128)(2,1)S(1)}, bf16[256,16]{0,1:T(8,128)(2,1)}, u32[]{:S(2)}) copy-start(bf16[256,16]{0,1:T(8,128)(2,1)} %param.15) | copy-start | bytes 24580
  1.7 10.0 %collective-permute-start = (bf16[64,640]{1,0:T(8,128)(2,1)S(1)}, bf16[64,640]{1,0:T(8,128)(2,1)S(1)}, u32[]{:S(2)}, u32[]{:S(2)}) collective-permute-start(bf16[64,640]{1,0:T(8,128)(2,1)S(1)} %get-tuple-element.21), channel_id=1, source_target_pairs={{0,1},{1,0},{2,3},{3,2},{4,5},{5,4},{6,7},{7,6},{8,9},{9,8},{10,11... | collective-permute-start | bytes 245768 | tf_op jit(solution)/shard_map/ppermute | solution.py:535
  2.3 9.4 %collective-permute-start.1 = (bf16[64,640]{1,0:T(8,128)(2,1)S(1)}, bf16[64,640]{1,0:T(8,128)(2,1)S(1)}, u32[]{:S(2)}, u32[]{:S(2)}) collective-permute-start(bf16[64,640]{1,0:T(8,128)(2,1)S(1)} %get-tuple-element.22), channel_id=1, source_target_pairs={{0,15},{1,2},{2,1},{3,4},{4,3},{5,6},{6,5},{7,8},{8,7},{9,10},{10,... | collective-permute-start | bytes 245768 | tf_op jit(solution)/shard_map/ppermute | solution.py:534
  7.9 3.6 %copy-start.10 = (bf16[16,95,128]{2,0,1:T(8,128)(2,1)S(1)}, bf16[16,95,128]{2,0,1:T(8,128)(2,1)}, u32[]{:S(2)}) copy-start(bf16[16,95,128]{2,0,1:T(8,128)(2,1)} %param.12) | copy-start | bytes 1167364
  11.6 5.5 %copy-start = (bf16[16,4,128,128]{3,2,1,0:T(8,128)(2,1)S(1)}, bf16[16,4,128,128]{3,2,1,0:T(8,128)(2,1)}, u32[]{:S(2)}) copy-start(bf16[16,4,128,128]{3,2,1,0:T(8,128)(2,1)} %refs_4_.1) | copy-start | bytes 6291460
  11.6 5.5 %copy-start.1 = (bf16[256,256]{1,0:T(8,128)(2,1)S(1)}, bf16[256,256]{1,0:T(8,128)(2,1)}, u32[]{:S(2)}) copy-start(bf16[256,256]{1,0:T(8,128)(2,1)} %mw.1) | copy-start | bytes 393220
  11.6 5.5 %copy-start.2 = (bf16[95,256]{1,0:T(8,128)(2,1)S(1)}, bf16[95,256]{1,0:T(8,128)(2,1)}, u32[]{:S(2)}) copy-start(bf16[95,256]{1,0:T(8,128)(2,1)} %ow.1) | copy-start | bytes 145924
  11.7 5.5 %copy-start.3 = (bf16[16,256]{1,0:T(8,128)(2,1)S(1)}, bf16[16,256]{1,0:T(8,128)(2,1)}, u32[]{:S(2)}) copy-start(bf16[16,256]{1,0:T(8,128)(2,1)} %cw.1) | copy-start | bytes 24580
  11.7 5.5 %copy-start.4 = (s32[16,3]{0,1:T(4,128)S(1)}, s32[16,3]{0,1:T(4,128)}, u32[]{:S(2)}) copy-start(s32[16,3]{0,1:T(4,128)} %param.20) | copy-start | bytes 580
  11.7 5.5 %copy-start.5 = (s32[16]{0:T(128)S(1)}, s32[16]{0:T(128)}, u32[]{:S(2)}) copy-start(s32[16]{0:T(128)} %refs_0_.1) | copy-start | bytes 196
  13.6 6.2 %collective-permute-start.4 = (bf16[16,128]{1,0:T(8,128)(2,1)S(1)}, bf16[16,128]{1,0:T(8,128)(2,1)S(1)}, u32[]{:S(2)}, u32[]{:S(2)}) collective-permute-start(bf16[16,128]{1,0:T(8,128)(2,1)S(1)} %get-tuple-element.32), channel_id=1, source_target_pairs={{1,14},{2,13},{3,12},{4,11},{5,10},{6,9},{9,6},{10,5},{11,4},{12,3... | collective-permute-start | bytes 12296 | tf_op jit(solution)/shard_map/ppermute | solution.py:540
  14.2 5.5 %collective-permute-start.2 = (bf16[9,16,128]{2,1,0:T(8,128)(2,1)S(1)}, bf16[9,16,128]{2,1,0:T(8,128)(2,1)S(1)}, u32[]{:S(2)}, u32[]{:S(2)}) collective-permute-start(bf16[9,16,128]{2,1,0:T(8,128)(2,1)S(1)} %get-tuple-element.30), channel_id=1, source_target_pairs={{0,1},{1,0},{2,3},{3,2},{4,5},{5,4},{6,7},{7,6},{8,9},{9,8},{10,11... | collective-permute-start | bytes 110600 | tf_op jit(solution)/shard_map/ppermute | solution.py:538
  16.2 6.1 %collective-permute-start.3 = (bf16[9,16,128]{2,1,0:T(8,128)(2,1)S(1)}, bf16[9,16,128]{2,1,0:T(8,128)(2,1)S(1)}, u32[]{:S(2)}, u32[]{:S(2)}) collective-permute-start(bf16[9,16,128]{2,1,0:T(8,128)(2,1)S(1)} %get-tuple-element.31), channel_id=1, source_target_pairs={{0,15},{1,2},{2,1},{3,4},{4,3},{5,6},{6,5},{7,8},{8,7},{9,10},{10,... | collective-permute-start | bytes 110600 | tf_op jit(solution)/shard_map/ppermute | solution.py:539

commit v6 on v5

--- a/solution.py
+++ b/solution.py
@@ -234,17 +234,16 @@
 def edge_kernel(
     one, two, flux_in, taps, wc, lt, fwt,
     edges, tiles, north, send_one, send_two,
-    halo, flux, ca, cb, la, lb, oa, ob, asked, ask_one, ask_two, sems,
+    halo, flux, ca, cb, la, lb, oa, ob,
 ):
     lats = one.shape[1]
     chans = lt.shape[1]
     columns = taps.shape[1] // lats
     lists = []
-    for i, (ref, to) in enumerate(((one, ask_one), (two, ask_two))):
+    for ref in (one, two):
         wanted = ref[pl.ds(chans, ASK), :128].astype(F32).astype(jnp.int32)
-        asked[pl.ds(i * ASK, ASK), :] = jnp.clip(wanted, 0, lats // TLAT - 1)
-        lists.append(pltpu.make_async_copy(asked.at[pl.ds(i * ASK, 1)], to, sems.at[i]))
-        lists[-1].start()
+        wanted = jnp.clip(wanted, 0, lats // TLAT - 1)
+        lists.append([wanted[0, k] for k in range(MAXACT)])
     odd = parity()
     put_shifts(halo, pl.multiple_of(lats * (1 - odd), 128), one[pl.ds(0, chans), :])
     put_shifts(halo, pl.multiple_of(lats * odd, 128), two[pl.ds(0, chans), :])
@@ -303,11 +302,9 @@
                 north[...] = v.astype(BF16)
                 send_one[MAXACT] = v.astype(BF16)
                 send_two[MAXACT] = v.astype(BF16)
-    for c in lists:
-        c.wait()
     for k in range(MAXACT):
-        send_one[k] = tiles[ask_one[0, k]]
-        send_two[k] = tiles[ask_two[0, k]]
+        send_one[k] = tiles[lists[0][k]]
+        send_two[k] = tiles[lists[1][k]]
 
 
 def edge(one, two, flux_in, taps, wc, lt, fwt):
@@ -336,10 +333,6 @@
             pltpu.VMEM((width, CHUNK), BF16),
             pltpu.VMEM((width, CHUNK), BF16),
             pltpu.VMEM((width, CHUNK), BF16),
-            pltpu.VMEM((2 * ASK, 128), jnp.int32),
-            pltpu.SMEM((1, 128), jnp.int32),
-            pltpu.SMEM((1, 128), jnp.int32),
-            pltpu.SemaphoreType.DMA((2,)),
         ],
         compiler_params=pltpu.CompilerParams(vmem_limit_bytes=12 * 2**20),
         cost_estimate=pl.CostEstimate(flops=10**9, bytes_accessed=10**6, transcendentals=3 * 10**5),
@@ -527,7 +520,10 @@
     inward = [(i, i ^ 1) for i in range(strips)]
     outward = [(i, (i + 1 if i % 2 else i - 1) % strips) for i in range(strips)]
     met = dict(outward)
-    mirror = [(i, strips - 1 - i) for i in range(strips) if met[i] != strips - 1 - i]
+    mirror = [
+        (i, (i + strips // 2) % strips if met[i] == strips - 1 - i else strips - 1 - i)
+        for i in range(strips)
+    ]
     fwt = flux_weight.T
     pair = pair_tile.T
     send_one, send_two = first(atm_in, pair, ocean_mask)

time: 24.5 us -> 22.1 us (0.902)
  waiting for transfers between devices: 2.52 us -> 1.19 us
  starting transfers between devices: 9.78 us -> 9.19 us
  Pallas kernels: 11.1 us -> 10.6 us
    ppermute x2, starting transfers between devices: 6.62 us -> 7.95 us  [per_device(): two = lax.ppermute(send_two, 'lon', outward)]
    ppermute x2, waiting for transfers between devices: 2.51 us -> 1.18 us  [per_device(): two = lax.ppermute(send_two, 'lon', outward)]
    ppermute x2, starting transfers between devices: 2.49 us -> 1.17 us  [per_device(): one = lax.ppermute(send_one, 'lon', inward)]
    ppermute x1, starting transfers between devices: 0.66 us -> 0.07 us  [per_device(): fold = lax.ppermute(north, 'lon', mirror)]
    pallas_call x1, Pallas kernels: 1.84 us -> 1.32 us  [edge(): pl.pallas_call(edge_kernel, out_shape=(jax.ShapeDtypeStruct((2, width, la...]
  transfers between devices with their start and end apart: 5 -> 5, of which waited for: 1 -> 1; matrix products, arithmetic and copies ran while one was open for 0% -> 0% of each run, Pallas kernels for 25% -> 28%
where the time goes in v6:
time: 22.1 us; the launch traced here: 21.9 us
  Pallas kernels  10.6 us (48%)
  starting transfers between devices  9.19 us (42%)
  waiting for transfers between devices  1.19 us (5%)
  between operations  0.82 us (4%)
    ppermute x2, starting transfers between devices, per_device(): two = lax.ppermute(send_two, 'lon', outward)  7.95 us
    pallas_call x1, Pallas kernels, interior(): pl.pallas_call(inner_kernel, out_shape=(jax.ShapeDtypeStruct((width, inne...  3.56 us
    pallas_call x1, Pallas kernels, early(): pl.pallas_call(early_kernel, out_shape=(jax.ShapeDtypeStruct((columns, wi...  2.55 us
    pallas_call x1, Pallas kernels, late(): pl.pallas_call(body, out_shape=jax.ShapeDtypeStruct((count, width, cells)...  2.14 us
    pallas_call x1, Pallas kernels, edge(): pl.pallas_call(edge_kernel, out_shape=(jax.ShapeDtypeStruct((2, width, la...  1.32 us
    ppermute x2, waiting for transfers between devices, per_device(): two = lax.ppermute(send_two, 'lon', outward)  1.18 us
    ppermute x2, starting transfers between devices, per_device(): one = lax.ppermute(send_one, 'lon', inward)  1.17 us
    pallas_call x1, Pallas kernels, first(): pl.pallas_call(first_kernel, out_shape=(column, column), in_specs=[HBM] *...  1.02 us
  transfers between devices with their start and end apart: 5, of which 1 were waited for; matrix products, arithmetic and copies ran while one was open for 0% of the time, Pallas kernels for 28%

profile of v6, /device:TPU:0, one launch (start us, length us, event | category | flops | bytes accessed | tf_op | source)
XLA Modules:
  0.0 21.9 jit_solution(15431658704430708844)
XLA Ops:
  0.6 0.0 copy-start.6
  0.6 0.0 copy-start.7
  0.7 0.0 copy-start.8
  0.7 0.0 copy-start.9
  0.7 1.0 %first.1 = (bf16[64,640]{1,0:T(8,128)(2,1)S(1)}, bf16[64,640]{1,0:T(8,128)(2,1)S(1)}) custom-call(bf16[8,48,640]{2,1,0:T(8,128)(2,1)} %x_hbm.1, s32[3,16]{1,0:T(4,128)} %bitcast.2, s32[16]{0:T(128)} %refs_0_.1), custom_call_target="tpu_custom_call" | custom-call | flops 4000000000 | bytes 1000000 | tf_op jit(solution)/shard_map/first/pallas_call | solution.py:119
  1.7 0.6 %collective-permute-start = (bf16[64,640]{1,0:T(8,128)(2,1)S(1)}, bf16[64,640]{1,0:T(8,128)(2,1)S(1)}, u32[]{:S(2)}, u32[]{:S(2)}) collective-permute-start(bf16[64,640]{1,0:T(8,128)(2,1)S(1)} %get-tuple-element.21), channel_id=1, source_target_pairs={{0,1},{1,0},{2,3},{3,2},{4,5},{5,4},{6,7},{7,6},{8,9},{9,8},{10,11... | collective-permute-start | bytes 245768 | tf_op jit(solution)/shard_map/ppermute | solution.py:531
  2.3 5.7 %collective-permute-start.1 = (bf16[64,640]{1,0:T(8,128)(2,1)S(1)}, bf16[64,640]{1,0:T(8,128)(2,1)S(1)}, u32[]{:S(2)}, u32[]{:S(2)}) collective-permute-start(bf16[64,640]{1,0:T(8,128)(2,1)S(1)} %get-tuple-element.22), channel_id=1, source_target_pairs={{0,15},{1,2},{2,1},{3,4},{4,3},{5,6},{6,5},{7,8},{8,7},{9,10},{10,... | collective-permute-start | bytes 245768 | tf_op jit(solution)/shard_map/ppermute | solution.py:530
  7.9 0.0 copy-done.6
  7.9 0.0 copy-done.7
  7.9 0.0 copy-done.8
  7.9 0.0 copy-done.9
  7.9 0.0 copy-start.10
  7.9 3.6 %interior.1 = (bf16[256,3840]{1,0:T(8,128)(2,1)S(1)}, f32[16,3840]{1,0:T(8,128)S(1)}, bf16[144,5120]{1,0:T(8,128)(2,1)S(1)}, bf16[256,512]{1,0:T(8,128)(2,1)S(1)}, bf16[256,48]{1,0:T(8,128)(2,1)S(1)}) custom-call(bf16[8,48,640]{2,1,0:T(8,128)(2,1)S(1)} %copy-done.7, bf16[48,256]{1,0:T(8,128)(2,1)S(1)} %copy-done.8, bf16[3,3,256,256]{3,2,1,0:T(8,128)(2,1)S(1)} %copy-done.6, ...), custom_call_target="tpu_custom_call" | custom-call | flops 4000000000 | bytes 4000000 | tf_op jit(solution)/shard_map/interior/pallas_call | solution.py:189
  11.5 0.0 copy-done.10
  11.5 0.1 copy.14.ocean
  11.6 0.0 copy-start
  11.6 0.0 copy-start.1
  11.6 0.0 copy-start.2
  11.7 0.0 copy-start.3
  11.7 0.0 copy-start.4
  11.7 0.0 copy-start.5
  11.7 0.0 collective-permute-done.one
  11.7 0.0 collective-permute-done.1.two
  11.7 1.3 %edge.1 = (bf16[2,256,640]{2,1,0:T(8,128)(2,1)S(1)}, bf16[40,16,128]{2,1,0:T(8,128)(2,1)S(1)}, bf16[16,128]{1,0:T(8,128)(2,1)S(1)}, bf16[9,16,128]{2,1,0:T(8,128)(2,1)S(1)}, bf16[9,16,128]{2,1,0:T(8,128)(2,1)S(1)}) custom-call(bf16[64,640]{1,0:T(8,128)(2,1)S(1)} %collective-permute-done.one, bf16[64,640]{1,0:T(8,128)(2,1)S(1)} %collective-permute-done.1.two, ...), custom_call_target="tpu_custom_call" | custom-call | flops 1000000000 | bytes 1000000 | tf_op jit(solution)/shard_map/edge/pallas_call | solution.py:316
  13.0 0.1 collective-permute-start.4
  13.1 0.6 %collective-permute-start.2 = (bf16[9,16,128]{2,1,0:T(8,128)(2,1)S(1)}, bf16[9,16,128]{2,1,0:T(8,128)(2,1)S(1)}, u32[]{:S(2)}, u32[]{:S(2)}) collective-permute-start(bf16[9,16,128]{2,1,0:T(8,128)(2,1)S(1)} %get-tuple-element.30), channel_id=1, source_target_pairs={{0,1},{1,0},{2,3},{3,2},{4,5},{5,4},{6,7},{7,6},{8,9},{9,8},{10,11... | collective-permute-start | bytes 110600 | tf_op jit(solution)/shard_map/ppermute | solution.py:534
  13.7 2.3 %collective-permute-start.3 = (bf16[9,16,128]{2,1,0:T(8,128)(2,1)S(1)}, bf16[9,16,128]{2,1,0:T(8,128)(2,1)S(1)}, u32[]{:S(2)}, u32[]{:S(2)}) collective-permute-start(bf16[9,16,128]{2,1,0:T(8,128)(2,1)S(1)} %get-tuple-element.31), channel_id=1, source_target_pairs={{0,15},{1,2},{2,1},{3,4},{4,3},{5,6},{6,5},{7,8},{8,7},{9,10},{10,... | collective-permute-start | bytes 110600 | tf_op jit(solution)/shard_map/ppermute | solution.py:535
  16.0 0.0 copy-done
  16.0 0.0 copy-done.1
  16.0 0.0 copy-done.2
  16.0 0.0 copy-done.3
  16.0 0.0 copy-done.4
  16.0 0.0 copy-done.5
  16.1 2.5 %early.1 = (bf16[8,256,640]{2,1,0:T(8,128)(2,1)}, bf16[16,256,128]{2,1,0:T(8,128)(2,1)}, f32[32,1024]{1,0:T(8,128)S(1)}, f32[256,1024]{1,0:T(8,128)S(1)}, bf16[2...) custom-call(bf16[256,3840]{1,0:T(8,128)(2,1)S(1)} %get-tuple-element.20.hid, ...), custom_call_target="tpu_custom_call" | custom-call | flops 1000000000 | bytes 6000000 | tf_op jit(solution)/shard_map/early/pallas_call | solution.py:395
  18.6 0.0 collective-permute-done.4.refs_3_
  18.6 0.0 collective-permute-done.2.refs_1_
  18.6 1.2 %collective-permute-done.3.refs_2_ = bf16[9,16,128]{2,1,0:T(8,128)(2,1)S(1)} collective-permute-done((bf16[9,16,128]{2,1,0:T(8,128)(2,1)S(1)}, bf16[9,16,128]{2,1,0:T(8,128)(2,1)S(1)}, u32[]{:S(2)}, u32[]{:S(2)}) %collective-permute-start.3) | collective-permute-done | bytes 36896 | tf_op jit(solution)/shard_map/ppermute | solution.py:535
  19.8 2.1 %late.1 = bf16[16,256,128]{2,1,0:T(8,128)(2,1)} custom-call(s32[16]{0:T(128)S(1)} %copy-done.5, bf16[9,16,128]{2,1,0:T(8,128)(2,1)S(1)} %collective-permute-done.2.refs_1_, bf16[9,16,128]{2,1,0:T(8,128)(2,1)S(1)} %collective-permute-done.3.refs_2_, bf16[16,128]{1,0:T(8,128)(2,1)S(1)} %collective-permute-done.4.refs_3_, ...), custom_call_target="tpu_custom_call", output_to_operand_aliasing={{}: (9, {})} | custom-call | flops 1000000000 | bytes 1000000 | tf_op jit(solution)/shard_map/late/pallas_call | solution.py:486
Async XLA Ops:
  0.6 7.3 %copy-start.6 = (bf16[3,3,256,256]{3,2,1,0:T(8,128)(2,1)S(1)}, bf16[3,3,256,256]{3,2,1,0:T(8,128)(2,1)}, u32[]{:S(2)}) copy-start(bf16[3,3,256,256]{3,2,1,0:T(8,128)(2,1)} %conv.1) | copy-start | bytes 3538948
  0.6 7.3 %copy-start.7 = (bf16[8,48,640]{2,1,0:T(8,128)(2,1)S(1)}, bf16[8,48,640]{2,1,0:T(8,128)(2,1)}, u32[]{:S(2)}) copy-start(bf16[8,48,640]{2,1,0:T(8,128)(2,1)} %x_hbm.1) | copy-start | bytes 1474564
  0.7 7.3 %copy-start.8 = (bf16[48,256]{1,0:T(8,128)(2,1)S(1)}, bf16[48,256]{1,0:T(8,128)(2,1)}, u32[]{:S(2)}) copy-start(bf16[48,256]{1,0:T(8,128)(2,1)} %lift.1) | copy-start | bytes 73732
  0.7 7.3 %copy-start.9 = (bf16[256,16]{0,1:T(8,128)(2,1)S(1)}, bf16[256,16]{0,1:T(8,128)(2,1)}, u32[]{:S(2)}) copy-start(bf16[256,16]{0,1:T(8,128)(2,1)} %param.15) | copy-start | bytes 24580
  1.7 10.0 %collective-permute-start = (bf16[64,640]{1,0:T(8,128)(2,1)S(1)}, bf16[64,640]{1,0:T(8,128)(2,1)S(1)}, u32[]{:S(2)}, u32[]{:S(2)}) collective-permute-start(bf16[64,640]{1,0:T(8,128)(2,1)S(1)} %get-tuple-element.21), channel_id=1, source_target_pairs={{0,1},{1,0},{2,3},{3,2},{4,5},{5,4},{6,7},{7,6},{8,9},{9,8},{10,11... | collective-permute-start | bytes 245768 | tf_op jit(solution)/shard_map/ppermute | solution.py:531
  2.3 9.4 %collective-permute-start.1 = (bf16[64,640]{1,0:T(8,128)(2,1)S(1)}, bf16[64,640]{1,0:T(8,128)(2,1)S(1)}, u32[]{:S(2)}, u32[]{:S(2)}) collective-permute-start(bf16[64,640]{1,0:T(8,128)(2,1)S(1)} %get-tuple-element.22), channel_id=1, source_target_pairs={{0,15},{1,2},{2,1},{3,4},{4,3},{5,6},{6,5},{7,8},{8,7},{9,10},{10,... | collective-permute-start | bytes 245768 | tf_op jit(solution)/shard_map/ppermute | solution.py:530
  7.9 3.6 %copy-start.10 = (bf16[16,95,128]{2,0,1:T(8,128)(2,1)S(1)}, bf16[16,95,128]{2,0,1:T(8,128)(2,1)}, u32[]{:S(2)}) copy-start(bf16[16,95,128]{2,0,1:T(8,128)(2,1)} %param.12) | copy-start | bytes 1167364
  11.6 4.4 %copy-start = (bf16[16,4,128,128]{3,2,1,0:T(8,128)(2,1)S(1)}, bf16[16,4,128,128]{3,2,1,0:T(8,128)(2,1)}, u32[]{:S(2)}) copy-start(bf16[16,4,128,128]{3,2,1,0:T(8,128)(2,1)} %refs_4_.1) | copy-start | bytes 6291460
  11.6 4.4 %copy-start.1 = (bf16[256,256]{1,0:T(8,128)(2,1)S(1)}, bf16[256,256]{1,0:T(8,128)(2,1)}, u32[]{:S(2)}) copy-start(bf16[256,256]{1,0:T(8,128)(2,1)} %mw.1) | copy-start | bytes 393220
  11.6 4.4 %copy-start.2 = (bf16[95,256]{1,0:T(8,128)(2,1)S(1)}, bf16[95,256]{1,0:T(8,128)(2,1)}, u32[]{:S(2)}) copy-start(bf16[95,256]{1,0:T(8,128)(2,1)} %ow.1) | copy-start | bytes 145924
  11.7 4.4 %copy-start.3 = (bf16[16,256]{1,0:T(8,128)(2,1)S(1)}, bf16[16,256]{1,0:T(8,128)(2,1)}, u32[]{:S(2)}) copy-start(bf16[16,256]{1,0:T(8,128)(2,1)} %cw.1) | copy-start | bytes 24580
  11.7 4.4 %copy-start.4 = (s32[16,3]{0,1:T(4,128)S(1)}, s32[16,3]{0,1:T(4,128)}, u32[]{:S(2)}) copy-start(s32[16,3]{0,1:T(4,128)} %param.20) | copy-start | bytes 580
  11.7 4.4 %copy-start.5 = (s32[16]{0:T(128)S(1)}, s32[16]{0:T(128)}, u32[]{:S(2)}) copy-start(s32[16]{0:T(128)} %refs_0_.1) | copy-start | bytes 196
  13.0 5.6 %collective-permute-start.4 = (bf16[16,128]{1,0:T(8,128)(2,1)S(1)}, bf16[16,128]{1,0:T(8,128)(2,1)S(1)}, u32[]{:S(2)}, u32[]{:S(2)}) collective-permute-start(bf16[16,128]{1,0:T(8,128)(2,1)S(1)} %get-tuple-element.32), channel_id=1, source_target_pairs={{0,8},{1,14},{2,13},{3,12},{4,11},{5,10},{6,9},{7,15},{8,0},{9,6},... | collective-permute-start | bytes 12296 | tf_op jit(solution)/shard_map/ppermute | solution.py:536
  13.1 5.5 %collective-permute-start.2 = (bf16[9,16,128]{2,1,0:T(8,128)(2,1)S(1)}, bf16[9,16,128]{2,1,0:T(8,128)(2,1)S(1)}, u32[]{:S(2)}, u32[]{:S(2)}) collective-permute-start(bf16[9,16,128]{2,1,0:T(8,128)(2,1)S(1)} %get-tuple-element.30), channel_id=1, source_target_pairs={{0,1},{1,0},{2,3},{3,2},{4,5},{5,4},{6,7},{7,6},{8,9},{9,8},{10,11... | collective-permute-start | bytes 110600 | tf_op jit(solution)/shard_map/ppermute | solution.py:534
  13.7 6.1 %collective-permute-start.3 = (bf16[9,16,128]{2,1,0:T(8,128)(2,1)S(1)}, bf16[9,16,128]{2,1,0:T(8,128)(2,1)S(1)}, u32[]{:S(2)}, u32[]{:S(2)}) collective-permute-start(bf16[9,16,128]{2,1,0:T(8,128)(2,1)S(1)} %get-tuple-element.31), channel_id=1, source_target_pairs={{0,15},{1,2},{2,1},{3,4},{4,3},{5,6},{6,5},{7,8},{8,7},{9,10},{10,... | collective-permute-start | bytes 110600 | tf_op jit(solution)/shard_map/ppermute | solution.py:535

commit v7 on v6

--- a/solution.py
+++ b/solution.py
@@ -16,7 +16,7 @@
 
 CHUNK = 256
 STRIP = 32
-ASK = 16
+ASK = 8
 
 HBM = pl.BlockSpec(memory_space=pltpu.HBM)
 VM = pl.BlockSpec(memory_space=pltpu.VMEM)
@@ -51,21 +51,60 @@
 
 
 def multiply(segments, wc, lt, conv, lifted):
+    deep = wc.shape[1] // 2
     chans = lt.shape[1]
     rows = 3 * chans
-    parts = []
-    for a in range(3):
-        parts.append(join([seg[a][0][:, pl.ds(seg[a][1], seg[3])] for seg in segments], 1))
-    parts.append(jnp.zeros((wc.shape[1] - 3 * rows, parts[0].shape[1]), BF16))
-    own = join([seg[1][0][chans : 2 * chans, pl.ds(seg[1][1], seg[3])] for seg in segments], 1)
-    conv[...] = dot(wc[...], jnp.concatenate(parts, 0))
-    lifted[...] = dot(lt[...], own).astype(BF16)
-
-
-def activate(conv, lifted, out, stores):
+    width = sum(seg[3] for seg in segments)
+
+    def side(a):
+        parts = []
+        for seg in segments:
+            if seg[a] is None:
+                parts.append(jnp.zeros((rows, seg[3]), BF16))
+            else:
+                parts.append(seg[a][0][:, pl.ds(seg[a][1], seg[3])])
+        return join(parts, 1)
+
+    def blank(count):
+        return jnp.zeros((count, width), BF16)
+
+    absent = [all(seg[a] is None for seg in segments) for a in range(3)]
+    if absent[1] and absent[2]:
+        conv[...] = dot(wc[:, :deep], jnp.concatenate([side(0), blank(deep - rows)], 0))
+    elif absent[0] and absent[1]:
+        before = 2 * rows - deep
+        conv[...] = dot(
+            wc[:, deep:], jnp.concatenate([blank(before), side(2), blank(deep - before - rows)], 0)
+        )
+    else:
+        parts = [side(0), side(1), side(2), blank(2 * deep - 3 * rows)]
+        conv[...] = dot(wc[...], jnp.concatenate(parts, 0))
+    if lifted is not None:
+        own = join([seg[1][0][chans : 2 * chans, pl.ds(seg[1][1], seg[3])] for seg in segments], 1)
+        lifted[...] = dot(lt[...], own).astype(BF16)
+
+
+def edge_lanes(lats):
+    half = -(-lats // CHUNK)
+    return half, 2 * half * CHUNK - lats
+
+
+def edge_work(lats):
+    work = []
+    full = lats // CHUNK * CHUNK
+    for lo in range(0, full, CHUNK):
+        for side in range(2):
+            work.append([(side, lo, CHUNK)])
+    if full < lats:
+        work.append([(0, full, lats - full), (1, full, lats - full)])
+    return work
+
+
+def activate(conv, lifted, out, stores, rest=None):
     for r in range(0, conv.shape[0], STRIP):
         at = slice(r, r + STRIP)
-        fresh = (lifted[at, :].astype(F32) + gelu_of_half(conv[at, :])).astype(BF16)
+        half = conv[at, :] if rest is None else conv[at, :] + rest(at)
+        fresh = (lifted(at).astype(F32) + gelu_of_half(half)).astype(BF16)
         out[at, :] = fresh
         for ref, first, lo, hi in stores:
             ref[at, pl.ds(first, hi - lo)] = fresh[:, lo:hi]
@@ -135,8 +174,8 @@
 
 def inner_kernel(
     x, lift, conv, fwt,
-    hid, flux, taps, wc, lt,
-    comp, ca, cb, la, lb, oa, ob,
+    hid, flux, wc, rest, lifted,
+    taps, lt, comp, ca, cb, la, lb, oa, ob,
 ):
     columns, chans, lats = x.shape
     width = lift.shape[1]
@@ -147,15 +186,28 @@
             comp[pl.ds((3 * a + b) * chans, chans), :] = dot(half, conv[a, b])
     wc[...] = comp[...].T.astype(BF16)
     lt[...] = lift[...].astype(F32).T.astype(BF16)
+    for i in (0, columns + 1):
+        taps[:, i * lats : (i + 1) * lats] = jnp.zeros((3 * chans, lats), BF16)
     for i in range(columns):
-        put_shifts(taps, i * lats, x[i])
+        put_shifts(taps, (i + 1) * lats, x[i])
+
+    def window(first, conv_to, lifted_to):
+        at = [pl.multiple_of(first + a * lats, 128) for a in range(3)]
+        multiply([[(taps, p) for p in at] + [CHUNK]], wc, lt, conv_to, lifted_to)
 
     def feed(j, conv_to, lifted_to):
-        at = [pl.multiple_of(j * CHUNK + a * lats, 128) for a in range(3)]
-        multiply([[(taps, p) for p in at] + [CHUNK]], wc, lt, conv_to, lifted_to)
+        window(lats + j * CHUNK, conv_to, lifted_to)
 
     def finish(j, conv_of, lifted_of, out):
-        activate(conv_of, lifted_of, out, [(hid, pl.multiple_of(j * CHUNK, 128), 0, CHUNK)])
+        store = (hid, pl.multiple_of(j * CHUNK, 128), 0, CHUNK)
+        activate(conv_of, lambda at: lifted_of[at, :], out, [store])
+
+    def near_edge(k):
+        half, _ = edge_lanes(lats)
+        k = jnp.minimum(k, 2 * half - 1)
+        first = jnp.where(k < half, k * CHUNK, columns * lats + (k - 2 * half) * CHUNK)
+        to = pl.ds(pl.multiple_of(k * CHUNK, 128), CHUNK)
+        window(first, rest.at[:, to], lifted.at[:, to])
 
     def head(j, out):
         flux[:, pl.ds(pl.multiple_of(j * CHUNK, 128), CHUNK)] = dot(fwt[...], out[...])
@@ -166,6 +218,7 @@
     def two(i, _):
         j = 2 * i
         feed(j + 1, cb, lb)
+        near_edge(i)
         finish(j, ca, la, oa)
         head(jnp.maximum(j - 1, 0), ob)
 
@@ -179,6 +232,8 @@
     if chunks % 2:
         finish(chunks - 1, ca, la, oa)
         head(chunks - 1, oa)
+    for k in range(chunks // 2, 2 * edge_lanes(lats)[0]):
+        near_edge(k)
 
 
 def interior(x, lift, conv, fwt):
@@ -186,18 +241,21 @@
     width = lift.shape[1]
     fluxes = fwt.shape[0]
     inner = (columns - 2) * lats
+    pieces = 2 * edge_lanes(lats)[0] * CHUNK
     return pl.pallas_call(
         inner_kernel,
         out_shape=(
             jax.ShapeDtypeStruct((width, inner), BF16),
             jax.ShapeDtypeStruct((fluxes, inner), F32),
-            jax.ShapeDtypeStruct((3 * chans, columns * lats), BF16),
             jax.ShapeDtypeStruct((width, 2 * width), BF16),
-            jax.ShapeDtypeStruct((width, chans), BF16),
+            jax.ShapeDtypeStruct((width, pieces), F32),
+            jax.ShapeDtypeStruct((width, pieces), BF16),
         ),
         in_specs=[VM] * 4,
         out_specs=(VM,) * 5,
         scratch_shapes=[
+            pltpu.VMEM((3 * chans, (columns + 2) * lats), BF16),
+            pltpu.VMEM((width, chans), BF16),
             pltpu.VMEM((2 * width, width), F32),
             pltpu.VMEM((width, CHUNK), F32),
             pltpu.VMEM((width, CHUNK), F32),
@@ -232,13 +290,13 @@
 
 
 def edge_kernel(
-    one, two, flux_in, taps, wc, lt, fwt,
+    one, two, flux_in, wc, rest, lifted, fwt,
     edges, tiles, north, send_one, send_two,
-    halo, flux, ca, cb, la, lb, oa, ob,
+    halo, flux, ca, cb, oa, ob,
 ):
     lats = one.shape[1]
-    chans = lt.shape[1]
-    columns = taps.shape[1] // lats
+    chans = one.shape[0] - ASK
+    columns = flux_in.shape[1] // lats + 2
     lists = []
     for ref in (one, two):
         wanted = ref[pl.ds(chans, ASK), :128].astype(F32).astype(jnp.int32)
@@ -247,50 +305,41 @@
     odd = parity()
     put_shifts(halo, pl.multiple_of(lats * (1 - odd), 128), one[pl.ds(0, chans), :])
     put_shifts(halo, pl.multiple_of(lats * odd, 128), two[pl.ds(0, chans), :])
-    sides = [
-        [(halo, 0), (taps, 0), (taps, lats)],
-        [(taps, (columns - 2) * lats), (taps, (columns - 1) * lats), (halo, lats)],
-    ]
-    work = []
-    full = lats // CHUNK * CHUNK
-    for side in range(2):
-        for lo in range(0, full, CHUNK):
-            work.append([(side, lo, CHUNK)])
-    if full < lats:
-        work.append([(0, full, lats - full), (1, full, lats - full)])
-    bufs = [(ca, la, oa), (cb, lb, ob)]
+    sides = [[(halo, 0), None, None], [None, None, (halo, lats)]]
+    work = edge_work(lats)
+    bufs = [(ca, oa), (cb, ob)]
 
     def feed(j):
         segments = []
         for side, lo, size in work[j]:
-            segments.append([(ref, at + lo) for ref, at in sides[side]] + [size])
-        multiply(segments, wc, lt, bufs[j % 2][0], bufs[j % 2][1])
+            segments.append([c and (c[0], c[1] + lo) for c in sides[side]] + [size])
+        multiply(segments, wc, fwt[:, :chans], bufs[j % 2][0], None)
 
     def finish(j):
-        stores = []
+        stores, lanes = [], []
         at = 0
         for side, lo, size in work[j]:
             stores.append((edges.at[side], lo, at, at + size))
+            first = lo + side * edge_lanes(lats)[1]
+            lanes.append(slice(first, first + size))
             at += size
-        activate(bufs[j % 2][0], bufs[j % 2][1], bufs[j % 2][2], stores)
+
+        def read(ref):
+            return lambda rows: join([ref[rows, at] for at in lanes], 1)
+
+        activate(bufs[j % 2][0], read(lifted), bufs[j % 2][1], stores, read(rest))
 
     def head(j):
-        got = dot(fwt[...], bufs[j % 2][2][...])
+        got = dot(fwt[...], bufs[j % 2][1][...])
         at = 0
         for side, lo, size in work[j]:
             flux[side, :, lo : lo + size] = got[:, at : at + size]
             at += size
 
-    feed(0)
-    for j in range(len(work)):
-        if j + 1 < len(work):
-            feed(j + 1)
-        finish(j)
-        if j:
-            head(j - 1)
-    head(len(work) - 1)
     group = 128 // TLAT
-    for g in range(lats // 128):
+    north_tile = lats // TLAT - 1
+
+    def swap(g):
         at = slice(g * 128, g * 128 + 128)
         values = [flux[0, :, at]]
         for i in range(columns - 2):
@@ -298,20 +347,39 @@
         values.append(flux[1, :, at])
         for a, v in enumerate(swap_blocks(values, 128)):
             tiles[g * group + a] = v.astype(BF16)
-            if g == lats // 128 - 1 and a == group - 1:
-                north[...] = v.astype(BF16)
-                send_one[MAXACT] = v.astype(BF16)
-                send_two[MAXACT] = v.astype(BF16)
+            if g * group + a == north_tile:
+                for ref in (north, send_one.at[MAXACT], send_two.at[MAXACT]):
+                    ref[...] = v.astype(BF16)
+
+    ready, seen = [], [0, 0]
+    for pieces in work:
+        for side, lo, size in pieces:
+            seen[side] = lo + size
+        ready.append(min(seen) // 128)
+    feed(0)
+    swapped = 0
+    for j in range(len(work)):
+        if j + 1 < len(work):
+            feed(j + 1)
+        finish(j)
+        if j:
+            head(j - 1)
+            for g in range(swapped, ready[j - 1]):
+                swap(g)
+            swapped = ready[j - 1]
+    head(len(work) - 1)
+    for g in range(swapped, lats // 128):
+        swap(g)
     for k in range(MAXACT):
         send_one[k] = tiles[lists[0][k]]
         send_two[k] = tiles[lists[1][k]]
 
 
-def edge(one, two, flux_in, taps, wc, lt, fwt):
+def edge(one, two, flux_in, wc, rest, lifted, fwt):
     lats = one.shape[1]
-    columns = taps.shape[1] // lats
-    width, chans = lt.shape
-    fluxes = fwt.shape[0]
+    chans = one.shape[0] - ASK
+    columns = flux_in.shape[1] // lats + 2
+    fluxes, width = fwt.shape
     cells = columns * TLAT
     return pl.pallas_call(
         edge_kernel,
@@ -331,18 +399,16 @@
             pltpu.VMEM((width, CHUNK), F32),
             pltpu.VMEM((width, CHUNK), BF16),
             pltpu.VMEM((width, CHUNK), BF16),
-            pltpu.VMEM((width, CHUNK), BF16),
-            pltpu.VMEM((width, CHUNK), BF16),
         ],
         compiler_params=pltpu.CompilerParams(vmem_limit_bytes=12 * 2**20),
         cost_estimate=pl.CostEstimate(flops=10**9, bytes_accessed=10**6, transcendentals=3 * 10**5),
         name="edge",
-    )(one, two, flux_in, taps, wc, lt, fwt)
+    )(one, two, flux_in, wc, rest, lifted, fwt)
 
 
 def early_kernel(
     hid, edges, pair, mask, tiles, ocean, regrid, ow, cw, mw,
-    hid_out, out_hbm, sums, base, cwt, mwt,
+    hid_out, out_hbm, sums, base, cwt, mwt, blocks, folds,
     zero, chosen, sems,
 ):
     count = ocean.shape[0]
@@ -376,6 +442,10 @@
         mine = jnp.concatenate([tiles[pair[1, t]], ones], 0)
         sums[:, at] = dot_t(mine, regrid[t, 1])
         base[:, at] = dot(owt, ocean[t])
+        for side in range(2):
+            blocks[at, side * cells : (side + 1) * cells] = regrid[t, 2 * side]
+        if k < FOLDB:
+            folds[at, :] = regrid[t, 3]
     for t in range(count - FOLDB):
 
         @pl.when(mask[t] != 1)
@@ -401,9 +471,11 @@
             jax.ShapeDtypeStruct((width, MAXACT * cells), F32),
             jax.ShapeDtypeStruct((width, fluxes), BF16),
             jax.ShapeDtypeStruct((width, width), BF16),
+            jax.ShapeDtypeStruct((MAXACT * cells, 2 * cells), BF16),
+            jax.ShapeDtypeStruct((FOLDB * cells, cells), BF16),
         ),
         in_specs=[VM, VM, SM, SM, VM, VM, VM, VM, VM, VM],
-        out_specs=(HBM, HBM, VM, VM, VM, VM),
+        out_specs=(HBM, HBM) + (VM,) * 6,
         scratch_shapes=[
             pltpu.VMEM((width, cells), BF16),
             pltpu.SMEM((MAXACT + 1,), jnp.int32),
@@ -416,45 +488,46 @@
 
 
 def late_kernel(
-    mask, one, two, fold, regrid_weight, sums, base, cwt, mwt, given_hbm,
+    mask, one, two, fold, sums, base, cwt, mwt, blocks, folds, given_hbm,
     out_hbm,
-    state, mixed, out, chosen, sems,
+    state, mixed_even, mixed_odd, out, chosen, sems,
 ):
-    count = out_hbm.shape[0]
     fluxes = fold.shape[0]
     cells = out.shape[2]
-    found = list_tiles(mask, chosen, count)
+    pairs = MAXACT // 2
+    wide = 2 * cells
     strip, strips = lax.axis_index("lon"), lax.axis_size("lon")
     odd = lax.rem(strip, 2)
     met = lax.rem(strip + 2 * odd - 1 + strips, strips) == strips - 1 - strip
     odd = odd == 1
     partner = jnp.where(met, two[MAXACT], fold[...])
     ones = jnp.ones(fold.shape, BF16)
-    wide = 2 * cells
-    totals = []
-    for k in range(MAXACT):
-        t = chosen[k]
+
+    def got(k):
         west = jnp.where(odd, one[k], two[k])
         east = jnp.where(odd, two[k], one[k])
-        got = jnp.concatenate([jnp.concatenate([west, ones], 0), jnp.concatenate([east, ones], 0)], 1)
-        weights = jnp.concatenate([regrid_weight[t, 0], regrid_weight[t, 2]], 1)
-        total = sums[:, k * cells : (k + 1) * cells] + dot_t(got, weights)
-        if k < FOLDB:
-            total = total + dot_t(jnp.concatenate([partner, ones], 0), regrid_weight[t, 3])
+        return [jnp.concatenate([west, east], 1), jnp.concatenate([ones, ones], 1)]
+
+    half = 2 * fluxes
+    totals = []
+    for p in range(pairs):
+        at = slice(p * wide, p * wide + wide)
+        product = dot_t(jnp.concatenate(got(2 * p) + got(2 * p + 1), 0), blocks[at, :])
+        total = jnp.concatenate([product[:half, :cells], product[half:, cells:]], 1) + sums[:, at]
+        if 2 * p < FOLDB:
+            total = total + dot_t(jnp.concatenate([partner, ones], 0), folds[at, :])
         totals.append(total)
-    for p in range(MAXACT // 2):
+    for p in range(pairs):
         at = slice(p * wide, p * wide + wide)
-        total = jnp.concatenate(totals[2 * p : 2 * p + 2], 1)
-        regrid = (total[:fluxes] / total[fluxes : fluxes + 1]).astype(BF16)
+        regrid = (totals[p][:fluxes] / totals[p][fluxes : fluxes + 1]).astype(BF16)
         state[:, at] = (base[:, at] + dot(cwt[...], regrid)).astype(BF16)
+
+    mixed = (mixed_even, mixed_odd)
 
     def mix(p):
         mixed[p % 2][...] = dot(mwt[...], state[:, p * wide : p * wide + wide])
 
-    mix(0)
-    for p in range(MAXACT // 2):
-        if p + 1 < MAXACT // 2:
-            mix(p + 1)
+    def finish(p):
         for r in range(0, state.shape[0], STRIP):
             at = slice(r, r + STRIP)
             for side in range(2):
@@ -462,8 +535,14 @@
                 own = state[at, k * cells : (k + 1) * cells].astype(F32)
                 half = mixed[p % 2][at, side * cells : (side + 1) * cells]
                 out[k, at, :] = (own + gelu_of_half(half)).astype(BF16)
-        for side in range(2):
-            k = 2 * p + side
+
+    found = list_tiles(mask, chosen, out_hbm.shape[0])
+    mix(0)
+    for p in range(pairs):
+        if p + 1 < pairs:
+            mix(p + 1)
+        finish(p)
+        for k in (2 * p, 2 * p + 1):
 
             @pl.when(k < found)
             def _():
@@ -476,17 +555,12 @@
             pltpu.make_async_copy(out.at[k], out_hbm.at[0], sems.at[k]).wait()
 
 
-def late(mask, one, two, fold, regrid, sums, base, cwt, mwt, given):
+def late(mask, one, two, fold, sums, base, cwt, mwt, blocks, folds, given):
     count, width, cells = given.shape
-
-    def body(*refs):
-        head, (state, ma, mb, out, chosen, sems) = refs[:11], refs[11:]
-        late_kernel(*head, state, (ma, mb), out, chosen, sems)
-
     return pl.pallas_call(
-        body,
+        late_kernel,
         out_shape=jax.ShapeDtypeStruct((count, width, cells), BF16),
-        in_specs=[SM, VM, VM, VM, VM, VM, VM, VM, VM, HBM],
+        in_specs=[SM] + [VM] * 9 + [HBM],
         out_specs=HBM,
         scratch_shapes=[
             pltpu.VMEM((width, MAXACT * cells), BF16),
@@ -496,11 +570,11 @@
             pltpu.SMEM((MAXACT + 1,), jnp.int32),
             pltpu.SemaphoreType.DMA((MAXACT,)),
         ],
-        input_output_aliases={9: 0},
+        input_output_aliases={10: 0},
         compiler_params=pltpu.CompilerParams(vmem_limit_bytes=12 * 2**20),
         cost_estimate=pl.CostEstimate(flops=10**9, bytes_accessed=10**6, transcendentals=3 * 10**5),
         name="late",
-    )(mask, one, two, fold, regrid, sums, base, cwt, mwt, given)
+    )(mask, one, two, fold, sums, base, cwt, mwt, blocks, folds, given)
 
 
 def per_device(
@@ -529,16 +603,18 @@
     send_one, send_two = first(atm_in, pair, ocean_mask)
     two = lax.ppermute(send_two, "lon", outward)
     one = lax.ppermute(send_one, "lon", inward)
-    hid, flux, taps, wc, lt = interior(atm_in, lift_weight, conv_weight, fwt)
-    edges, tiles, north, send_one, send_two = edge(one, two, flux, taps, wc, lt, fwt)
+    hid, flux, wc, rest, lifted = interior(atm_in, lift_weight, conv_weight, fwt)
+    edges, tiles, north, send_one, send_two = edge(one, two, flux, wc, rest, lifted, fwt)
     one = lax.ppermute(send_one, "lon", inward)
     two = lax.ppermute(send_two, "lon", outward)
     fold = lax.ppermute(north, "lon", mirror)
-    atm_hidden, given, sums, base, cwt, mwt = early(
+    atm_hidden, given, sums, base, cwt, mwt, blocks, folds = early(
         hid, edges, pair, ocean_mask, tiles, ocean_in, regrid_weight,
         ocean_weight, couple_weight, mix_weight,
     )
-    ocean_hidden = late(ocean_mask, one, two, fold, regrid_weight, sums, base, cwt, mwt, given)
+    ocean_hidden = late(
+        ocean_mask, one, two, fold, sums, base, cwt, mwt, blocks, folds, given
+    )
     return (atm_hidden, ocean_hidden)
 
 

time: 22.1 us -> 22.8 us (1.032)
  waiting for transfers between devices: 1.19 us -> 2.18 us
  starting transfers between devices: 9.19 us -> 8.25 us
  Pallas kernels: 10.6 us -> 11.3 us
    ppermute x2, waiting for transfers between devices: 1.18 us -> 2.17 us  [per_device(): two = lax.ppermute(send_two, 'lon', outward)]
    ppermute x2, starting transfers between devices: 7.95 us -> 7.01 us  [per_device(): two = lax.ppermute(send_two, 'lon', outward)]
    pallas_call x1, Pallas kernels: 3.56 us -> 4.39 us  [interior(): pl.pallas_call(inner_kernel, out_shape=(jax.ShapeDtypeStruct((width, inne...]
  transfers between devices with their start and end apart: 5 -> 5, of which waited for: 1 -> 1; matrix products, arithmetic and copies ran while one was open for 0% -> 0% of each run, Pallas kernels for 28% -> 30%
where the time goes in v7:
time: 22.8 us; the launch traced here: 22.7 us
  Pallas kernels  11.3 us (50%)
  starting transfers between devices  8.25 us (36%)
  waiting for transfers between devices  2.18 us (10%)
  between operations  0.82 us (4%)
    ppermute x2, starting transfers between devices, per_device(): two = lax.ppermute(send_two, 'lon', outward)  7.01 us
    pallas_call x1, Pallas kernels, interior(): pl.pallas_call(inner_kernel, out_shape=(jax.ShapeDtypeStruct((width, inne...  4.39 us
    pallas_call x1, Pallas kernels, early(): pl.pallas_call(early_kernel, out_shape=(jax.ShapeDtypeStruct((columns, wi...  2.5 us
    ppermute x2, waiting for transfers between devices, per_device(): two = lax.ppermute(send_two, 'lon', outward)  2.17 us
    pallas_call x1, Pallas kernels, late(): pl.pallas_call(late_kernel, out_shape=jax.ShapeDtypeStruct((count, width,...  2.14 us
    pallas_call x1, Pallas kernels, edge(): pl.pallas_call(edge_kernel, out_shape=(jax.ShapeDtypeStruct((2, width, la...  1.23 us
    ppermute x2, starting transfers between devices, per_device(): one = lax.ppermute(send_one, 'lon', inward)  1.17 us
    pallas_call x1, Pallas kernels, first(): pl.pallas_call(first_kernel, out_shape=(column, column), in_specs=[HBM] *...  1.02 us
  transfers between devices with their start and end apart: 5, of which 1 were waited for; matrix products, arithmetic and copies ran while one was open for 0% of the time, Pallas kernels for 30%

profile of v7, /device:TPU:0, one launch (start us, length us, event | category | flops | bytes accessed | tf_op | source)
XLA Modules:
  0.0 22.7 jit_solution(14337523524409754847)
XLA Ops:
  0.6 0.0 copy-start.6
  0.6 0.0 copy-start.7
  0.7 0.0 copy-start.8
  0.7 0.0 copy-start.9
  0.7 1.0 %first.1 = (bf16[56,640]{1,0:T(8,128)(2,1)S(1)}, bf16[56,640]{1,0:T(8,128)(2,1)S(1)}) custom-call(bf16[8,48,640]{2,1,0:T(8,128)(2,1)} %x_hbm.1, s32[3,16]{1,0:T(4,128)} %bitcast.2, s32[16]{0:T(128)} %mask.3), custom_call_target="tpu_custom_call" | custom-call | flops 4000000000 | bytes 1000000 | tf_op jit(solution)/shard_map/first/pallas_call | solution.py:158
  1.7 0.6 %collective-permute-start = (bf16[56,640]{1,0:T(8,128)(2,1)S(1)}, bf16[56,640]{1,0:T(8,128)(2,1)S(1)}, u32[]{:S(2)}, u32[]{:S(2)}) collective-permute-start(bf16[56,640]{1,0:T(8,128)(2,1)S(1)} %get-tuple-element.23), channel_id=1, source_target_pairs={{0,1},{1,0},{2,3},{3,2},{4,5},{5,4},{6,7},{7,6},{8,9},{9,8},{10,11... | collective-permute-start | bytes 215048 | tf_op jit(solution)/shard_map/ppermute | solution.py:605
  2.3 5.7 %collective-permute-start.1 = (bf16[56,640]{1,0:T(8,128)(2,1)S(1)}, bf16[56,640]{1,0:T(8,128)(2,1)S(1)}, u32[]{:S(2)}, u32[]{:S(2)}) collective-permute-start(bf16[56,640]{1,0:T(8,128)(2,1)S(1)} %get-tuple-element.24), channel_id=1, source_target_pairs={{0,15},{1,2},{2,1},{3,4},{4,3},{5,6},{6,5},{7,8},{8,7},{9,10},{10,... | collective-permute-start | bytes 215048 | tf_op jit(solution)/shard_map/ppermute | solution.py:604
  7.9 0.0 copy-done.6
  7.9 0.0 copy-done.7
  7.9 0.0 copy-done.8
  7.9 0.0 copy-done.9
  7.9 0.0 copy-start.10
  7.9 4.4 %interior.1 = (bf16[256,3840]{1,0:T(8,128)(2,1)S(1)}, f32[16,3840]{1,0:T(8,128)S(1)}, bf16[256,512]{1,0:T(8,128)(2,1)S(1)}, f32[256,1536]{1,0:T(8,128)S(1)}, bf16[256,1536]{1,0:T(8,128)(2,1)S(1)}) custom-call(bf16[8,48,640]{2,1,0:T(8,128)(2,1)S(1)} %copy-done.7, bf16[48,256]{1,0:T(8,128)(2,1)S(1)} %copy-done.8, bf16[3,3,256,256]{3,2,1,0:T(8,128)(2,1)S(1)} %copy-done.6, ...), custom_call_target="tpu_custom_call" | custom-call | flops 4000000000 | bytes 4000000 | tf_op jit(solution)/shard_map/interior/pallas_call | solution.py:245
  12.3 0.0 copy-done.10
  12.3 0.1 copy.14.ocean
  12.4 0.0 copy-start
  12.5 0.0 copy-start.1
  12.5 0.0 copy-start.2
  12.5 0.0 copy-start.3
  12.5 0.0 copy-start.4
  12.5 0.0 copy-start.5
  12.5 0.0 collective-permute-done.one
  12.5 0.0 collective-permute-done.1.two
  12.5 1.2 %edge.1 = (bf16[2,256,640]{2,1,0:T(8,128)(2,1)S(1)}, bf16[40,16,128]{2,1,0:T(8,128)(2,1)S(1)}, bf16[16,128]{1,0:T(8,128)(2,1)S(1)}, bf16[9,16,128]{2,1,0:T(8,128)(2,1)S(1)}, bf16[9,16,128]{2,1,0:T(8,128)(2,1)S(1)}) custom-call(bf16[56,640]{1,0:T(8,128)(2,1)S(1)} %collective-permute-done.one, bf16[56,640]{1,0:T(8,128)(2,1)S(1)} %collective-permute-done.1.two, ...), custom_call_target="tpu_custom_call" | custom-call | flops 1000000000 | bytes 1000000 | tf_op jit(solution)/shard_map/edge/pallas_call | solution.py:384
  13.8 0.1 collective-permute-start.4
  13.9 0.6 %collective-permute-start.2 = (bf16[9,16,128]{2,1,0:T(8,128)(2,1)S(1)}, bf16[9,16,128]{2,1,0:T(8,128)(2,1)S(1)}, u32[]{:S(2)}, u32[]{:S(2)}) collective-permute-start(bf16[9,16,128]{2,1,0:T(8,128)(2,1)S(1)} %get-tuple-element.32), channel_id=1, source_target_pairs={{0,1},{1,0},{2,3},{3,2},{4,5},{5,4},{6,7},{7,6},{8,9},{9,8},{10,11... | collective-permute-start | bytes 110600 | tf_op jit(solution)/shard_map/ppermute | solution.py:608
  14.5 1.4 %collective-permute-start.3 = (bf16[9,16,128]{2,1,0:T(8,128)(2,1)S(1)}, bf16[9,16,128]{2,1,0:T(8,128)(2,1)S(1)}, u32[]{:S(2)}, u32[]{:S(2)}) collective-permute-start(bf16[9,16,128]{2,1,0:T(8,128)(2,1)S(1)} %get-tuple-element.33), channel_id=1, source_target_pairs={{0,15},{1,2},{2,1},{3,4},{4,3},{5,6},{6,5},{7,8},{8,7},{9,10},{10,... | collective-permute-start | bytes 110600 | tf_op jit(solution)/shard_map/ppermute | solution.py:609
  15.8 0.0 copy-done
  15.8 0.0 copy-done.1
  15.8 0.0 copy-done.2
  15.8 0.0 copy-done.3
  15.8 0.0 copy-done.4
  15.8 0.0 copy-done.5
  15.9 2.5 %early.1 = (bf16[8,256,640]{2,1,0:T(8,128)(2,1)}, bf16[16,256,128]{2,1,0:T(8,128)(2,1)}, f32[32,1024]{1,0:T(8,128)S(1)}, f32[256,1024]{1,0:T(8,128)S(1)}, bf16[2...) custom-call(bf16[256,3840]{1,0:T(8,128)(2,1)S(1)} %get-tuple-element, ...), custom_call_target="tpu_custom_call" | custom-call | flops 1000000000 | bytes 6000000 | tf_op jit(solution)/shard_map/early/pallas_call | solution.py:465
  18.4 0.0 collective-permute-done.4.fold
  18.4 0.0 collective-permute-done.2.one
  18.4 2.2 %collective-permute-done.3.two = bf16[9,16,128]{2,1,0:T(8,128)(2,1)S(1)} collective-permute-done((bf16[9,16,128]{2,1,0:T(8,128)(2,1)S(1)}, bf16[9,16,128]{2,1,0:T(8,128)(2,1)S(1)}, u32[]{:S(2)}, u32[]{:S(2)}) %collective-permute-start.3) | collective-permute-done | bytes 36896 | tf_op jit(solution)/shard_map/ppermute | solution.py:609
  20.5 2.1 %late.1 = bf16[16,256,128]{2,1,0:T(8,128)(2,1)} custom-call(s32[16]{0:T(128)S(1)} %copy-done.5, bf16[9,16,128]{2,1,0:T(8,128)(2,1)S(1)} %collective-permute-done.2.one, bf16[9,16,128]{2,1,0:T(8,128)(2,1)S(1)} %collective-permute-done.3.two, bf16[16,128]{1,0:T(8,128)(2,1)S(1)} %collective-permute-done.4.fold, ...), custom_call_target="tpu_custom_call", output_to_operand_aliasing={{}: (10, {})} | custom-call | flops 1000000000 | bytes 1000000 | tf_op jit(solution)/shard_map/late/pallas_call | solution.py:560
Async XLA Ops:
  0.6 7.3 %copy-start.6 = (bf16[3,3,256,256]{3,2,1,0:T(8,128)(2,1)S(1)}, bf16[3,3,256,256]{3,2,1,0:T(8,128)(2,1)}, u32[]{:S(2)}) copy-start(bf16[3,3,256,256]{3,2,1,0:T(8,128)(2,1)} %conv.1) | copy-start | bytes 3538948
  0.6 7.3 %copy-start.7 = (bf16[8,48,640]{2,1,0:T(8,128)(2,1)S(1)}, bf16[8,48,640]{2,1,0:T(8,128)(2,1)}, u32[]{:S(2)}) copy-start(bf16[8,48,640]{2,1,0:T(8,128)(2,1)} %x_hbm.1) | copy-start | bytes 1474564
  0.7 7.3 %copy-start.8 = (bf16[48,256]{1,0:T(8,128)(2,1)S(1)}, bf16[48,256]{1,0:T(8,128)(2,1)}, u32[]{:S(2)}) copy-start(bf16[48,256]{1,0:T(8,128)(2,1)} %lift.1) | copy-start | bytes 73732
  0.7 7.3 %copy-start.9 = (bf16[256,16]{0,1:T(8,128)(2,1)S(1)}, bf16[256,16]{0,1:T(8,128)(2,1)}, u32[]{:S(2)}) copy-start(bf16[256,16]{0,1:T(8,128)(2,1)} %param.15) | copy-start | bytes 24580
  1.7 10.8 %collective-permute-start = (bf16[56,640]{1,0:T(8,128)(2,1)S(1)}, bf16[56,640]{1,0:T(8,128)(2,1)S(1)}, u32[]{:S(2)}, u32[]{:S(2)}) collective-permute-start(bf16[56,640]{1,0:T(8,128)(2,1)S(1)} %get-tuple-element.23), channel_id=1, source_target_pairs={{0,1},{1,0},{2,3},{3,2},{4,5},{5,4},{6,7},{7,6},{8,9},{9,8},{10,11... | collective-permute-start | bytes 215048 | tf_op jit(solution)/shard_map/ppermute | solution.py:605
  2.3 10.3 %collective-permute-start.1 = (bf16[56,640]{1,0:T(8,128)(2,1)S(1)}, bf16[56,640]{1,0:T(8,128)(2,1)S(1)}, u32[]{:S(2)}, u32[]{:S(2)}) collective-permute-start(bf16[56,640]{1,0:T(8,128)(2,1)S(1)} %get-tuple-element.24), channel_id=1, source_target_pairs={{0,15},{1,2},{2,1},{3,4},{4,3},{5,6},{6,5},{7,8},{8,7},{9,10},{10,... | collective-permute-start | bytes 215048 | tf_op jit(solution)/shard_map/ppermute | solution.py:604
  7.9 4.4 %copy-start.10 = (bf16[16,95,128]{2,0,1:T(8,128)(2,1)S(1)}, bf16[16,95,128]{2,0,1:T(8,128)(2,1)}, u32[]{:S(2)}) copy-start(bf16[16,95,128]{2,0,1:T(8,128)(2,1)} %param.12) | copy-start | bytes 1167364
  12.4 3.4 %copy-start = (bf16[16,4,128,128]{3,2,1,0:T(8,128)(2,1)S(1)}, bf16[16,4,128,128]{3,2,1,0:T(8,128)(2,1)}, u32[]{:S(2)}) copy-start(bf16[16,4,128,128]{3,2,1,0:T(8,128)(2,1)} %regrid.1) | copy-start | bytes 6291460
  12.5 3.4 %copy-start.1 = (bf16[256,256]{1,0:T(8,128)(2,1)S(1)}, bf16[256,256]{1,0:T(8,128)(2,1)}, u32[]{:S(2)}) copy-start(bf16[256,256]{1,0:T(8,128)(2,1)} %mw.1) | copy-start | bytes 393220
  12.5 3.4 %copy-start.2 = (bf16[95,256]{1,0:T(8,128)(2,1)S(1)}, bf16[95,256]{1,0:T(8,128)(2,1)}, u32[]{:S(2)}) copy-start(bf16[95,256]{1,0:T(8,128)(2,1)} %ow.1) | copy-start | bytes 145924
  12.5 3.4 %copy-start.3 = (bf16[16,256]{1,0:T(8,128)(2,1)S(1)}, bf16[16,256]{1,0:T(8,128)(2,1)}, u32[]{:S(2)}) copy-start(bf16[16,256]{1,0:T(8,128)(2,1)} %cw.1) | copy-start | bytes 24580
  12.5 3.3 %copy-start.4 = (s32[16,3]{0,1:T(4,128)S(1)}, s32[16,3]{0,1:T(4,128)}, u32[]{:S(2)}) copy-start(s32[16,3]{0,1:T(4,128)} %param.20) | copy-start | bytes 580
  12.5 3.3 %copy-start.5 = (s32[16]{0:T(128)S(1)}, s32[16]{0:T(128)}, u32[]{:S(2)}) copy-start(s32[16]{0:T(128)} %mask.3) | copy-start | bytes 196
  13.8 4.6 %collective-permute-start.4 = (bf16[16,128]{1,0:T(8,128)(2,1)S(1)}, bf16[16,128]{1,0:T(8,128)(2,1)S(1)}, u32[]{:S(2)}, u32[]{:S(2)}) collective-permute-start(bf16[16,128]{1,0:T(8,128)(2,1)S(1)} %get-tuple-element.34), channel_id=1, source_target_pairs={{0,8},{1,14},{2,13},{3,12},{4,11},{5,10},{6,9},{7,15},{8,0},{9,6},... | collective-permute-start | bytes 12296 | tf_op jit(solution)/shard_map/ppermute | solution.py:610
  13.9 4.5 %collective-permute-start.2 = (bf16[9,16,128]{2,1,0:T(8,128)(2,1)S(1)}, bf16[9,16,128]{2,1,0:T(8,128)(2,1)S(1)}, u32[]{:S(2)}, u32[]{:S(2)}) collective-permute-start(bf16[9,16,128]{2,1,0:T(8,128)(2,1)S(1)} %get-tuple-element.32), channel_id=1, source_target_pairs={{0,1},{1,0},{2,3},{3,2},{4,5},{5,4},{6,7},{7,6},{8,9},{9,8},{10,11... | collective-permute-start | bytes 110600 | tf_op jit(solution)/shard_map/ppermute | solution.py:608
  14.5 6.1 %collective-permute-start.3 = (bf16[9,16,128]{2,1,0:T(8,128)(2,1)S(1)}, bf16[9,16,128]{2,1,0:T(8,128)(2,1)S(1)}, u32[]{:S(2)}, u32[]{:S(2)}) collective-permute-start(bf16[9,16,128]{2,1,0:T(8,128)(2,1)S(1)} %get-tuple-element.33), channel_id=1, source_target_pairs={{0,15},{1,2},{2,1},{3,4},{4,3},{5,6},{6,5},{7,8},{8,7},{9,10},{10,... | collective-permute-start | bytes 110600 | tf_op jit(solution)/shard_map/ppermute | solution.py:609

commit v8 on v6

--- a/solution.py
+++ b/solution.py
@@ -16,7 +16,7 @@
 
 CHUNK = 256
 STRIP = 32
-ASK = 16
+ASK = 8
 
 HBM = pl.BlockSpec(memory_space=pltpu.HBM)
 VM = pl.BlockSpec(memory_space=pltpu.VMEM)
@@ -37,13 +37,13 @@
 
 def put_shifts(taps, at, column):
     chans, lats = column.shape
-    wide = column.astype(F32)
-    lane = lax.broadcasted_iota(jnp.int32, wide.shape, 1)
-    south = jnp.where(lane == 0, 0.0, pltpu.roll(wide, 1, 1))
-    north = jnp.where(lane == lats - 1, 0.0, pltpu.roll(wide, lats - 1, 1))
-    taps[:chans, pl.ds(at, lats)] = south.astype(BF16)
+    lane = lax.broadcasted_iota(jnp.int32, column.shape, 1)
+    zero = jnp.zeros(column.shape, BF16)
+    taps[:chans, pl.ds(at, lats)] = jnp.where(lane == 0, zero, pltpu.roll(column, 1, 1))
     taps[chans : 2 * chans, pl.ds(at, lats)] = column
-    taps[2 * chans :, pl.ds(at, lats)] = north.astype(BF16)
+    taps[2 * chans :, pl.ds(at, lats)] = jnp.where(
+        lane == lats - 1, zero, pltpu.roll(column, lats - 1, 1)
+    )
 
 
 def join(parts, axis):
@@ -145,7 +145,9 @@
     for a in range(3):
         for b in range(3):
             comp[pl.ds((3 * a + b) * chans, chans), :] = dot(half, conv[a, b])
-    wc[...] = comp[...].T.astype(BF16)
+    for side in range(2):
+        at = slice(side * width, side * width + width)
+        wc[:, at] = comp[at, :].T.astype(BF16)
     lt[...] = lift[...].astype(F32).T.astype(BF16)
     for i in range(columns):
         put_shifts(taps, i * lats, x[i])
@@ -253,8 +255,8 @@
     ]
     work = []
     full = lats // CHUNK * CHUNK
-    for side in range(2):
-        for lo in range(0, full, CHUNK):
+    for lo in range(0, full, CHUNK):
+        for side in range(2):
             work.append([(side, lo, CHUNK)])
     if full < lats:
         work.append([(0, full, lats - full), (1, full, lats - full)])
@@ -281,16 +283,10 @@
             flux[side, :, lo : lo + size] = got[:, at : at + size]
             at += size
 
-    feed(0)
-    for j in range(len(work)):
-        if j + 1 < len(work):
-            feed(j + 1)
-        finish(j)
-        if j:
-            head(j - 1)
-    head(len(work) - 1)
     group = 128 // TLAT
-    for g in range(lats // 128):
+    north_tile = lats // TLAT - 1
+
+    def swap(g):
         at = slice(g * 128, g * 128 + 128)
         values = [flux[0, :, at]]
         for i in range(columns - 2):
@@ -298,10 +294,29 @@
         values.append(flux[1, :, at])
         for a, v in enumerate(swap_blocks(values, 128)):
             tiles[g * group + a] = v.astype(BF16)
-            if g == lats // 128 - 1 and a == group - 1:
-                north[...] = v.astype(BF16)
-                send_one[MAXACT] = v.astype(BF16)
-                send_two[MAXACT] = v.astype(BF16)
+            if g * group + a == north_tile:
+                for ref in (north, send_one.at[MAXACT], send_two.at[MAXACT]):
+                    ref[...] = v.astype(BF16)
+
+    ready, seen = [], [0, 0]
+    for pieces in work:
+        for side, lo, size in pieces:
+            seen[side] = lo + size
+        ready.append(min(seen) // 128)
+    feed(0)
+    swapped = 0
+    for j in range(len(work)):
+        if j + 1 < len(work):
+            feed(j + 1)
+        finish(j)
+        if j:
+            head(j - 1)
+            for g in range(swapped, ready[j - 1]):
+                swap(g)
+            swapped = ready[j - 1]
+    head(len(work) - 1)
+    for g in range(swapped, lats // 128):
+        swap(g)
     for k in range(MAXACT):
         send_one[k] = tiles[lists[0][k]]
         send_two[k] = tiles[lists[1][k]]
@@ -342,7 +357,7 @@
 
 def early_kernel(
     hid, edges, pair, mask, tiles, ocean, regrid, ow, cw, mw,
-    hid_out, out_hbm, sums, base, cwt, mwt,
+    hid_out, out_hbm, sums, base, cwt, mwt, blocks, folds,
     zero, chosen, sems,
 ):
     count = ocean.shape[0]
@@ -376,6 +391,10 @@
         mine = jnp.concatenate([tiles[pair[1, t]], ones], 0)
         sums[:, at] = dot_t(mine, regrid[t, 1])
         base[:, at] = dot(owt, ocean[t])
+        for side in range(2):
+            blocks[at, side * cells : (side + 1) * cells] = regrid[t, 2 * side]
+        if k < FOLDB:
+            folds[at, :] = regrid[t, 3]
     for t in range(count - FOLDB):
 
         @pl.when(mask[t] != 1)
@@ -401,9 +420,11 @@
             jax.ShapeDtypeStruct((width, MAXACT * cells), F32),
             jax.ShapeDtypeStruct((width, fluxes), BF16),
             jax.ShapeDtypeStruct((width, width), BF16),
+            jax.ShapeDtypeStruct((MAXACT * cells, 2 * cells), BF16),
+            jax.ShapeDtypeStruct((FOLDB * cells, cells), BF16),
         ),
         in_specs=[VM, VM, SM, SM, VM, VM, VM, VM, VM, VM],
-        out_specs=(HBM, HBM, VM, VM, VM, VM),
+        out_specs=(HBM, HBM) + (VM,) * 6,
         scratch_shapes=[
             pltpu.VMEM((width, cells), BF16),
             pltpu.SMEM((MAXACT + 1,), jnp.int32),
@@ -416,45 +437,46 @@
 
 
 def late_kernel(
-    mask, one, two, fold, regrid_weight, sums, base, cwt, mwt, given_hbm,
+    mask, one, two, fold, sums, base, cwt, mwt, blocks, folds, given_hbm,
     out_hbm,
-    state, mixed, out, chosen, sems,
+    state, mixed_even, mixed_odd, out, chosen, sems,
 ):
-    count = out_hbm.shape[0]
     fluxes = fold.shape[0]
     cells = out.shape[2]
-    found = list_tiles(mask, chosen, count)
+    pairs = MAXACT // 2
+    wide = 2 * cells
     strip, strips = lax.axis_index("lon"), lax.axis_size("lon")
     odd = lax.rem(strip, 2)
     met = lax.rem(strip + 2 * odd - 1 + strips, strips) == strips - 1 - strip
     odd = odd == 1
     partner = jnp.where(met, two[MAXACT], fold[...])
     ones = jnp.ones(fold.shape, BF16)
-    wide = 2 * cells
-    totals = []
-    for k in range(MAXACT):
-        t = chosen[k]
+
+    def got(k):
         west = jnp.where(odd, one[k], two[k])
         east = jnp.where(odd, two[k], one[k])
-        got = jnp.concatenate([jnp.concatenate([west, ones], 0), jnp.concatenate([east, ones], 0)], 1)
-        weights = jnp.concatenate([regrid_weight[t, 0], regrid_weight[t, 2]], 1)
-        total = sums[:, k * cells : (k + 1) * cells] + dot_t(got, weights)
-        if k < FOLDB:
-            total = total + dot_t(jnp.concatenate([partner, ones], 0), regrid_weight[t, 3])
+        return [jnp.concatenate([west, east], 1), jnp.concatenate([ones, ones], 1)]
+
+    half = 2 * fluxes
+    totals = []
+    for p in range(pairs):
+        at = slice(p * wide, p * wide + wide)
+        product = dot_t(jnp.concatenate(got(2 * p) + got(2 * p + 1), 0), blocks[at, :])
+        total = jnp.concatenate([product[:half, :cells], product[half:, cells:]], 1) + sums[:, at]
+        if 2 * p < FOLDB:
+            total = total + dot_t(jnp.concatenate([partner, ones], 0), folds[at, :])
         totals.append(total)
-    for p in range(MAXACT // 2):
+    for p in range(pairs):
         at = slice(p * wide, p * wide + wide)
-        total = jnp.concatenate(totals[2 * p : 2 * p + 2], 1)
-        regrid = (total[:fluxes] / total[fluxes : fluxes + 1]).astype(BF16)
+        regrid = (totals[p][:fluxes] / totals[p][fluxes : fluxes + 1]).astype(BF16)
         state[:, at] = (base[:, at] + dot(cwt[...], regrid)).astype(BF16)
+
+    mixed = (mixed_even, mixed_odd)
 
     def mix(p):
         mixed[p % 2][...] = dot(mwt[...], state[:, p * wide : p * wide + wide])
 
-    mix(0)
-    for p in range(MAXACT // 2):
-        if p + 1 < MAXACT // 2:
-            mix(p + 1)
+    def finish(p):
         for r in range(0, state.shape[0], STRIP):
             at = slice(r, r + STRIP)
             for side in range(2):
@@ -462,8 +484,14 @@
                 own = state[at, k * cells : (k + 1) * cells].astype(F32)
                 half = mixed[p % 2][at, side * cells : (side + 1) * cells]
                 out[k, at, :] = (own + gelu_of_half(half)).astype(BF16)
-        for side in range(2):
-            k = 2 * p + side
+
+    found = list_tiles(mask, chosen, out_hbm.shape[0])
+    mix(0)
+    for p in range(pairs):
+        if p + 1 < pairs:
+            mix(p + 1)
+        finish(p)
+        for k in (2 * p, 2 * p + 1):
 
             @pl.when(k < found)
             def _():
@@ -476,17 +504,12 @@
             pltpu.make_async_copy(out.at[k], out_hbm.at[0], sems.at[k]).wait()
 
 
-def late(mask, one, two, fold, regrid, sums, base, cwt, mwt, given):
+def late(mask, one, two, fold, sums, base, cwt, mwt, blocks, folds, given):
     count, width, cells = given.shape
-
-    def body(*refs):
-        head, (state, ma, mb, out, chosen, sems) = refs[:11], refs[11:]
-        late_kernel(*head, state, (ma, mb), out, chosen, sems)
-
     return pl.pallas_call(
-        body,
+        late_kernel,
         out_shape=jax.ShapeDtypeStruct((count, width, cells), BF16),
-        in_specs=[SM, VM, VM, VM, VM, VM, VM, VM, VM, HBM],
+        in_specs=[SM] + [VM] * 9 + [HBM],
         out_specs=HBM,
         scratch_shapes=[
             pltpu.VMEM((width, MAXACT * cells), BF16),
@@ -496,11 +519,11 @@
             pltpu.SMEM((MAXACT + 1,), jnp.int32),
             pltpu.SemaphoreType.DMA((MAXACT,)),
         ],
-        input_output_aliases={9: 0},
+        input_output_aliases={10: 0},
         compiler_params=pltpu.CompilerParams(vmem_limit_bytes=12 * 2**20),
         cost_estimate=pl.CostEstimate(flops=10**9, bytes_accessed=10**6, transcendentals=3 * 10**5),
         name="late",
-    )(mask, one, two, fold, regrid, sums, base, cwt, mwt, given)
+    )(mask, one, two, fold, sums, base, cwt, mwt, blocks, folds, given)
 
 
 def per_device(
@@ -534,11 +557,13 @@
     one = lax.ppermute(send_one, "lon", inward)
     two = lax.ppermute(send_two, "lon", outward)
     fold = lax.ppermute(north, "lon", mirror)
-    atm_hidden, given, sums, base, cwt, mwt = early(
+    atm_hidden, given, sums, base, cwt, mwt, blocks, folds = early(
         hid, edges, pair, ocean_mask, tiles, ocean_in, regrid_weight,
         ocean_weight, couple_weight, mix_weight,
     )
-    ocean_hidden = late(ocean_mask, one, two, fold, regrid_weight, sums, base, cwt, mwt, given)
+    ocean_hidden = late(
+        ocean_mask, one, two, fold, sums, base, cwt, mwt, blocks, folds, given
+    )
     return (atm_hidden, ocean_hidden)
 
 

time: 22.1 us -> 22.1 us (level)
  no operation moved by 1% of the time
where the time goes in v8:
time: 22.1 us; the launch traced here: 21.9 us
  Pallas kernels  10.5 us (48%)
  starting transfers between devices  9.08 us (41%)
  waiting for transfers between devices  1.34 us (6%)
  between operations  0.82 us (4%)
    ppermute x2, starting transfers between devices, per_device(): two = lax.ppermute(send_two, 'lon', outward)  7.85 us
    pallas_call x1, Pallas kernels, interior(): pl.pallas_call(inner_kernel, out_shape=(jax.ShapeDtypeStruct((width, inne...  3.56 us
    pallas_call x1, Pallas kernels, early(): pl.pallas_call(early_kernel, out_shape=(jax.ShapeDtypeStruct((columns, wi...  2.5 us
    pallas_call x1, Pallas kernels, late(): pl.pallas_call(late_kernel, out_shape=jax.ShapeDtypeStruct((count, width,...  2.15 us
    ppermute x2, waiting for transfers between devices, per_device(): two = lax.ppermute(send_two, 'lon', outward)  1.33 us
    pallas_call x1, Pallas kernels, edge(): pl.pallas_call(edge_kernel, out_shape=(jax.ShapeDtypeStruct((2, width, la...  1.29 us
    ppermute x2, starting transfers between devices, per_device(): one = lax.ppermute(send_one, 'lon', inward)  1.17 us
    pallas_call x1, Pallas kernels, first(): pl.pallas_call(first_kernel, out_shape=(column, column), in_specs=[HBM] *...  1.02 us
  transfers between devices with their start and end apart: 5, of which 1 were waited for; matrix products, arithmetic and copies ran while one was open for 0% of the time, Pallas kernels for 28%

profile of v8, /device:TPU:0, one launch (start us, length us, event | category | flops | bytes accessed | tf_op | source)
XLA Modules:
  0.0 21.9 jit_solution(4460724711644558936)
XLA Ops:
  0.6 0.0 copy-start.6
  0.6 0.0 copy-start.7
  0.7 0.0 copy-start.8
  0.7 0.0 copy-start.9
  0.7 1.0 %first.1 = (bf16[56,640]{1,0:T(8,128)(2,1)S(1)}, bf16[56,640]{1,0:T(8,128)(2,1)S(1)}) custom-call(bf16[8,48,640]{2,1,0:T(8,128)(2,1)} %x_hbm.1, s32[3,16]{1,0:T(4,128)} %bitcast.2, s32[16]{0:T(128)} %mask.3), custom_call_target="tpu_custom_call" | custom-call | flops 4000000000 | bytes 1000000 | tf_op jit(solution)/shard_map/first/pallas_call | solution.py:119
  1.7 0.6 %collective-permute-start = (bf16[56,640]{1,0:T(8,128)(2,1)S(1)}, bf16[56,640]{1,0:T(8,128)(2,1)S(1)}, u32[]{:S(2)}, u32[]{:S(2)}) collective-permute-start(bf16[56,640]{1,0:T(8,128)(2,1)S(1)} %get-tuple-element.23), channel_id=1, source_target_pairs={{0,1},{1,0},{2,3},{3,2},{4,5},{5,4},{6,7},{7,6},{8,9},{9,8},{10,11... | collective-permute-start | bytes 215048 | tf_op jit(solution)/shard_map/ppermute | solution.py:554
  2.3 5.7 %collective-permute-start.1 = (bf16[56,640]{1,0:T(8,128)(2,1)S(1)}, bf16[56,640]{1,0:T(8,128)(2,1)S(1)}, u32[]{:S(2)}, u32[]{:S(2)}) collective-permute-start(bf16[56,640]{1,0:T(8,128)(2,1)S(1)} %get-tuple-element.24), channel_id=1, source_target_pairs={{0,15},{1,2},{2,1},{3,4},{4,3},{5,6},{6,5},{7,8},{8,7},{9,10},{10,... | collective-permute-start | bytes 215048 | tf_op jit(solution)/shard_map/ppermute | solution.py:553
  7.9 0.0 copy-done.6
  7.9 0.0 copy-done.7
  7.9 0.0 copy-done.8
  7.9 0.0 copy-done.9
  7.9 0.0 copy-start.10
  7.9 3.6 %interior.1 = (bf16[256,3840]{1,0:T(8,128)(2,1)S(1)}, f32[16,3840]{1,0:T(8,128)S(1)}, bf16[144,5120]{1,0:T(8,128)(2,1)S(1)}, bf16[256,512]{1,0:T(8,128)(2,1)S(1)}, bf16[256,48]{1,0:T(8,128)(2,1)S(1)}) custom-call(bf16[8,48,640]{2,1,0:T(8,128)(2,1)S(1)} %copy-done.7, bf16[48,256]{1,0:T(8,128)(2,1)S(1)} %copy-done.8, bf16[3,3,256,256]{3,2,1,0:T(8,128)(2,1)S(1)} %copy-done.6, ...), custom_call_target="tpu_custom_call" | custom-call | flops 4000000000 | bytes 4000000 | tf_op jit(solution)/shard_map/interior/pallas_call | solution.py:191
  11.5 0.0 copy-done.10
  11.5 0.1 copy.14.ocean
  11.6 0.0 copy-start
  11.6 0.0 copy-start.1
  11.6 0.0 copy-start.2
  11.7 0.0 copy-start.3
  11.7 0.0 copy-start.4
  11.7 0.0 copy-start.5
  11.7 0.0 collective-permute-done.one
  11.7 0.0 collective-permute-done.1.two
  11.7 1.3 %edge.1 = (bf16[2,256,640]{2,1,0:T(8,128)(2,1)S(1)}, bf16[40,16,128]{2,1,0:T(8,128)(2,1)S(1)}, bf16[16,128]{1,0:T(8,128)(2,1)S(1)}, bf16[9,16,128]{2,1,0:T(8,128)(2,1)S(1)}, bf16[9,16,128]{2,1,0:T(8,128)(2,1)S(1)}) custom-call(bf16[56,640]{1,0:T(8,128)(2,1)S(1)} %collective-permute-done.one, bf16[56,640]{1,0:T(8,128)(2,1)S(1)} %collective-permute-done.1.two, ...), custom_call_target="tpu_custom_call" | custom-call | flops 1000000000 | bytes 1000000 | tf_op jit(solution)/shard_map/edge/pallas_call | solution.py:331
  13.0 0.1 collective-permute-start.4
  13.1 0.6 %collective-permute-start.2 = (bf16[9,16,128]{2,1,0:T(8,128)(2,1)S(1)}, bf16[9,16,128]{2,1,0:T(8,128)(2,1)S(1)}, u32[]{:S(2)}, u32[]{:S(2)}) collective-permute-start(bf16[9,16,128]{2,1,0:T(8,128)(2,1)S(1)} %get-tuple-element.32), channel_id=1, source_target_pairs={{0,1},{1,0},{2,3},{3,2},{4,5},{5,4},{6,7},{7,6},{8,9},{9,8},{10,11... | collective-permute-start | bytes 110600 | tf_op jit(solution)/shard_map/ppermute | solution.py:557
  13.7 2.2 %collective-permute-start.3 = (bf16[9,16,128]{2,1,0:T(8,128)(2,1)S(1)}, bf16[9,16,128]{2,1,0:T(8,128)(2,1)S(1)}, u32[]{:S(2)}, u32[]{:S(2)}) collective-permute-start(bf16[9,16,128]{2,1,0:T(8,128)(2,1)S(1)} %get-tuple-element.33), channel_id=1, source_target_pairs={{0,15},{1,2},{2,1},{3,4},{4,3},{5,6},{6,5},{7,8},{8,7},{9,10},{10,... | collective-permute-start | bytes 110600 | tf_op jit(solution)/shard_map/ppermute | solution.py:558
  15.9 0.0 copy-done
  15.9 0.0 copy-done.1
  15.9 0.0 copy-done.2
  15.9 0.0 copy-done.3
  15.9 0.0 copy-done.4
  15.9 0.0 copy-done.5
  15.9 2.5 %early.1 = (bf16[8,256,640]{2,1,0:T(8,128)(2,1)}, bf16[16,256,128]{2,1,0:T(8,128)(2,1)}, f32[32,1024]{1,0:T(8,128)S(1)}, f32[256,1024]{1,0:T(8,128)S(1)}, bf16[2...) custom-call(bf16[256,3840]{1,0:T(8,128)(2,1)S(1)} %get-tuple-element, ...), custom_call_target="tpu_custom_call" | custom-call | flops 1000000000 | bytes 6000000 | tf_op jit(solution)/shard_map/early/pallas_call | solution.py:414
  18.4 0.0 collective-permute-done.4.fold
  18.4 0.0 collective-permute-done.2.one
  18.4 1.3 %collective-permute-done.3.two = bf16[9,16,128]{2,1,0:T(8,128)(2,1)S(1)} collective-permute-done((bf16[9,16,128]{2,1,0:T(8,128)(2,1)S(1)}, bf16[9,16,128]{2,1,0:T(8,128)(2,1)S(1)}, u32[]{:S(2)}, u32[]{:S(2)}) %collective-permute-start.3) | collective-permute-done | bytes 36896 | tf_op jit(solution)/shard_map/ppermute | solution.py:558
  19.8 2.1 %late.1 = bf16[16,256,128]{2,1,0:T(8,128)(2,1)} custom-call(s32[16]{0:T(128)S(1)} %copy-done.5, bf16[9,16,128]{2,1,0:T(8,128)(2,1)S(1)} %collective-permute-done.2.one, bf16[9,16,128]{2,1,0:T(8,128)(2,1)S(1)} %collective-permute-done.3.two, bf16[16,128]{1,0:T(8,128)(2,1)S(1)} %collective-permute-done.4.fold, ...), custom_call_target="tpu_custom_call", output_to_operand_aliasing={{}: (10, {})} | custom-call | flops 1000000000 | bytes 1000000 | tf_op jit(solution)/shard_map/late/pallas_call | solution.py:509
Async XLA Ops:
  0.6 7.3 %copy-start.6 = (bf16[3,3,256,256]{3,2,1,0:T(8,128)(2,1)S(1)}, bf16[3,3,256,256]{3,2,1,0:T(8,128)(2,1)}, u32[]{:S(2)}) copy-start(bf16[3,3,256,256]{3,2,1,0:T(8,128)(2,1)} %conv.1) | copy-start | bytes 3538948
  0.6 7.3 %copy-start.7 = (bf16[8,48,640]{2,1,0:T(8,128)(2,1)S(1)}, bf16[8,48,640]{2,1,0:T(8,128)(2,1)}, u32[]{:S(2)}) copy-start(bf16[8,48,640]{2,1,0:T(8,128)(2,1)} %x_hbm.1) | copy-start | bytes 1474564
  0.7 7.3 %copy-start.8 = (bf16[48,256]{1,0:T(8,128)(2,1)S(1)}, bf16[48,256]{1,0:T(8,128)(2,1)}, u32[]{:S(2)}) copy-start(bf16[48,256]{1,0:T(8,128)(2,1)} %lift.1) | copy-start | bytes 73732
  0.7 7.3 %copy-start.9 = (bf16[256,16]{0,1:T(8,128)(2,1)S(1)}, bf16[256,16]{0,1:T(8,128)(2,1)}, u32[]{:S(2)}) copy-start(bf16[256,16]{0,1:T(8,128)(2,1)} %param.15) | copy-start | bytes 24580
  1.7 10.0 %collective-permute-start = (bf16[56,640]{1,0:T(8,128)(2,1)S(1)}, bf16[56,640]{1,0:T(8,128)(2,1)S(1)}, u32[]{:S(2)}, u32[]{:S(2)}) collective-permute-start(bf16[56,640]{1,0:T(8,128)(2,1)S(1)} %get-tuple-element.23), channel_id=1, source_target_pairs={{0,1},{1,0},{2,3},{3,2},{4,5},{5,4},{6,7},{7,6},{8,9},{9,8},{10,11... | collective-permute-start | bytes 215048 | tf_op jit(solution)/shard_map/ppermute | solution.py:554
  2.3 9.4 %collective-permute-start.1 = (bf16[56,640]{1,0:T(8,128)(2,1)S(1)}, bf16[56,640]{1,0:T(8,128)(2,1)S(1)}, u32[]{:S(2)}, u32[]{:S(2)}) collective-permute-start(bf16[56,640]{1,0:T(8,128)(2,1)S(1)} %get-tuple-element.24), channel_id=1, source_target_pairs={{0,15},{1,2},{2,1},{3,4},{4,3},{5,6},{6,5},{7,8},{8,7},{9,10},{10,... | collective-permute-start | bytes 215048 | tf_op jit(solution)/shard_map/ppermute | solution.py:553
  7.9 3.6 %copy-start.10 = (bf16[16,95,128]{2,0,1:T(8,128)(2,1)S(1)}, bf16[16,95,128]{2,0,1:T(8,128)(2,1)}, u32[]{:S(2)}) copy-start(bf16[16,95,128]{2,0,1:T(8,128)(2,1)} %param.12) | copy-start | bytes 1167364
  11.6 4.3 %copy-start = (bf16[16,4,128,128]{3,2,1,0:T(8,128)(2,1)S(1)}, bf16[16,4,128,128]{3,2,1,0:T(8,128)(2,1)}, u32[]{:S(2)}) copy-start(bf16[16,4,128,128]{3,2,1,0:T(8,128)(2,1)} %regrid.1) | copy-start | bytes 6291460
  11.6 4.3 %copy-start.1 = (bf16[256,256]{1,0:T(8,128)(2,1)S(1)}, bf16[256,256]{1,0:T(8,128)(2,1)}, u32[]{:S(2)}) copy-start(bf16[256,256]{1,0:T(8,128)(2,1)} %mw.1) | copy-start | bytes 393220
  11.6 4.3 %copy-start.2 = (bf16[95,256]{1,0:T(8,128)(2,1)S(1)}, bf16[95,256]{1,0:T(8,128)(2,1)}, u32[]{:S(2)}) copy-start(bf16[95,256]{1,0:T(8,128)(2,1)} %ow.1) | copy-start | bytes 145924
  11.7 4.3 %copy-start.3 = (bf16[16,256]{1,0:T(8,128)(2,1)S(1)}, bf16[16,256]{1,0:T(8,128)(2,1)}, u32[]{:S(2)}) copy-start(bf16[16,256]{1,0:T(8,128)(2,1)} %cw.1) | copy-start | bytes 24580
  11.7 4.2 %copy-start.4 = (s32[16,3]{0,1:T(4,128)S(1)}, s32[16,3]{0,1:T(4,128)}, u32[]{:S(2)}) copy-start(s32[16,3]{0,1:T(4,128)} %param.20) | copy-start | bytes 580
  11.7 4.2 %copy-start.5 = (s32[16]{0:T(128)S(1)}, s32[16]{0:T(128)}, u32[]{:S(2)}) copy-start(s32[16]{0:T(128)} %mask.3) | copy-start | bytes 196
  13.0 5.4 %collective-permute-start.4 = (bf16[16,128]{1,0:T(8,128)(2,1)S(1)}, bf16[16,128]{1,0:T(8,128)(2,1)S(1)}, u32[]{:S(2)}, u32[]{:S(2)}) collective-permute-start(bf16[16,128]{1,0:T(8,128)(2,1)S(1)} %get-tuple-element.34), channel_id=1, source_target_pairs={{0,8},{1,14},{2,13},{3,12},{4,11},{5,10},{6,9},{7,15},{8,0},{9,6},... | collective-permute-start | bytes 12296 | tf_op jit(solution)/shard_map/ppermute | solution.py:559
  13.1 5.4 %collective-permute-start.2 = (bf16[9,16,128]{2,1,0:T(8,128)(2,1)S(1)}, bf16[9,16,128]{2,1,0:T(8,128)(2,1)S(1)}, u32[]{:S(2)}, u32[]{:S(2)}) collective-permute-start(bf16[9,16,128]{2,1,0:T(8,128)(2,1)S(1)} %get-tuple-element.32), channel_id=1, source_target_pairs={{0,1},{1,0},{2,3},{3,2},{4,5},{5,4},{6,7},{7,6},{8,9},{9,8},{10,11... | collective-permute-start | bytes 110600 | tf_op jit(solution)/shard_map/ppermute | solution.py:557
  13.7 6.1 %collective-permute-start.3 = (bf16[9,16,128]{2,1,0:T(8,128)(2,1)S(1)}, bf16[9,16,128]{2,1,0:T(8,128)(2,1)S(1)}, u32[]{:S(2)}, u32[]{:S(2)}) collective-permute-start(bf16[9,16,128]{2,1,0:T(8,128)(2,1)S(1)} %get-tuple-element.33), channel_id=1, source_target_pairs={{0,15},{1,2},{2,1},{3,4},{4,3},{5,6},{6,5},{7,8},{8,7},{9,10},{10,... | collective-permute-start | bytes 110600 | tf_op jit(solution)/shard_map/ppermute | solution.py:558

commit v9 on v8

--- a/solution.py
+++ b/solution.py
@@ -16,6 +16,8 @@
 
 CHUNK = 256
 STRIP = 32
+BUFS = 2
+AHEAD = 1
 ASK = 8
 
 HBM = pl.BlockSpec(memory_space=pltpu.HBM)
@@ -136,9 +138,10 @@
 def inner_kernel(
     x, lift, conv, fwt,
     hid, flux, taps, wc, lt,
-    comp, ca, cb, la, lb, oa, ob,
+    comp, *bufs,
 ):
     columns, chans, lats = x.shape
+    convs, lifts, outs = bufs[:BUFS], bufs[BUFS : 2 * BUFS], bufs[2 * BUFS :]
     width = lift.shape[1]
     comp[pl.ds(9 * chans, 2 * width - 9 * chans), :] = jnp.zeros((2 * width - 9 * chans, width), F32)
     half = 0.5 * lift[...]
@@ -152,35 +155,26 @@
     for i in range(columns):
         put_shifts(taps, i * lats, x[i])
 
-    def feed(j, conv_to, lifted_to):
-        at = [pl.multiple_of(j * CHUNK + a * lats, 128) for a in range(3)]
-        multiply([[(taps, p) for p in at] + [CHUNK]], wc, lt, conv_to, lifted_to)
-
-    def finish(j, conv_of, lifted_of, out):
-        activate(conv_of, lifted_of, out, [(hid, pl.multiple_of(j * CHUNK, 128), 0, CHUNK)])
-
-    def head(j, out):
-        flux[:, pl.ds(pl.multiple_of(j * CHUNK, 128), CHUNK)] = dot(fwt[...], out[...])
+    def feed(j):
+        at = [j * CHUNK + a * lats for a in range(3)]
+        multiply([[(taps, p) for p in at] + [CHUNK]], wc, lt, convs[j % BUFS], lifts[j % BUFS])
+
+    def finish(j):
+        activate(convs[j % BUFS], lifts[j % BUFS], outs[j % 2], [(hid, j * CHUNK, 0, CHUNK)])
+
+    def head(j):
+        flux[:, j * CHUNK : (j + 1) * CHUNK] = dot(fwt[...], outs[j % 2][...])
 
     chunks = (columns - 2) * lats // CHUNK
-    feed(0, ca, la)
-
-    def two(i, _):
-        j = 2 * i
-        feed(j + 1, cb, lb)
-        finish(j, ca, la, oa)
-        head(jnp.maximum(j - 1, 0), ob)
-
-        feed(jnp.minimum(j + 2, chunks - 1), ca, la)
-        finish(j + 1, cb, lb, ob)
-        head(j, oa)
-        return 0
-
-    lax.fori_loop(0, chunks // 2, two, 0)
-    head(chunks // 2 * 2 - 1, ob)
-    if chunks % 2:
-        finish(chunks - 1, ca, la, oa)
-        head(chunks - 1, oa)
+    for j in range(AHEAD):
+        feed(j)
+    for j in range(chunks):
+        if j + AHEAD < chunks:
+            feed(j + AHEAD)
+        finish(j)
+        if j:
+            head(j - 1)
+    head(chunks - 1)
 
 
 def interior(x, lift, conv, fwt):
@@ -201,13 +195,9 @@
         out_specs=(VM,) * 5,
         scratch_shapes=[
             pltpu.VMEM((2 * width, width), F32),
-            pltpu.VMEM((width, CHUNK), F32),
-            pltpu.VMEM((width, CHUNK), F32),
-            pltpu.VMEM((width, CHUNK), BF16),
-            pltpu.VMEM((width, CHUNK), BF16),
-            pltpu.VMEM((width, CHUNK), BF16),
-            pltpu.VMEM((width, CHUNK), BF16),
-        ],
+        ]
+        + [pltpu.VMEM((width, CHUNK), F32)] * BUFS
+        + [pltpu.VMEM((width, CHUNK), BF16)] * (BUFS + 2),
         compiler_params=pltpu.CompilerParams(vmem_limit_bytes=12 * 2**20),
         cost_estimate=pl.CostEstimate(flops=4 * 10**9, bytes_accessed=4 * 10**6, transcendentals=10**6),
         name="interior",

time: 22.1 us -> 21.5 us (0.973)
  starting transfers between devices: 9.08 us -> 10.2 us
  Pallas kernels: 10.5 us -> 9.44 us
  waiting for transfers between devices: 1.34 us -> 0.76 us
    pallas_call x1, Pallas kernels: 3.56 us -> 2.48 us  [interior(): pl.pallas_call(inner_kernel, out_shape=(jax.ShapeDtypeStruct((width, inne...]
    ppermute x2, waiting for transfers between devices: 1.33 us -> 0.75 us  [per_device(): two = lax.ppermute(send_two, 'lon', outward)]
    ppermute x2, starting transfers between devices: 7.85 us -> 8.43 us  [per_device(): two = lax.ppermute(send_two, 'lon', outward)]
    ppermute x2, starting transfers between devices: 1.17 us -> 1.64 us  [per_device(): one = lax.ppermute(send_one, 'lon', inward)]
  transfers between devices with their start and end apart: 5 -> 5, of which waited for: 1 -> 1; matrix products, arithmetic and copies ran while one was open for 0% -> 0% of each run, Pallas kernels for 28% -> 23%
where the time goes in v9:
time: 21.5 us; the launch traced here: 21.3 us
  starting transfers between devices  10.2 us (47%)
  Pallas kernels  9.44 us (44%)
  between operations  0.81 us (4%)
  waiting for transfers between devices  0.76 us (4%)
    ppermute x2, starting transfers between devices, per_device(): two = lax.ppermute(send_two, 'lon', outward)  8.43 us
    pallas_call x1, Pallas kernels, early(): pl.pallas_call(early_kernel, out_shape=(jax.ShapeDtypeStruct((columns, wi...  2.5 us
    pallas_call x1, Pallas kernels, interior(): pl.pallas_call(inner_kernel, out_shape=(jax.ShapeDtypeStruct((width, inne...  2.48 us
    pallas_call x1, Pallas kernels, late(): pl.pallas_call(late_kernel, out_shape=jax.ShapeDtypeStruct((count, width,...  2.14 us
    ppermute x2, starting transfers between devices, per_device(): one = lax.ppermute(send_one, 'lon', inward)  1.64 us
    pallas_call x1, Pallas kernels, edge(): pl.pallas_call(edge_kernel, out_shape=(jax.ShapeDtypeStruct((2, width, la...  1.29 us
    pallas_call x1, Pallas kernels, first(): pl.pallas_call(first_kernel, out_shape=(column, column), in_specs=[HBM] *...  1.02 us
    ppermute x2, waiting for transfers between devices, per_device(): two = lax.ppermute(send_two, 'lon', outward)  0.75 us
  transfers between devices with their start and end apart: 5, of which 1 were waited for; matrix products, arithmetic and copies ran while one was open for 0% of the time, Pallas kernels for 23%

profile of v9, /device:TPU:0, one launch (start us, length us, event | category | flops | bytes accessed | tf_op | source)
XLA Modules:
  0.0 21.3 jit_solution(2882123267145889416)
XLA Ops:
  0.6 0.0 copy-start.6
  0.6 0.0 copy-start.7
  0.7 0.0 copy-start.8
  0.7 0.0 copy-start.9
  0.7 1.0 %first.1 = (bf16[56,640]{1,0:T(8,128)(2,1)S(1)}, bf16[56,640]{1,0:T(8,128)(2,1)S(1)}) custom-call(bf16[8,48,640]{2,1,0:T(8,128)(2,1)} %x_hbm.1, s32[3,16]{1,0:T(4,128)} %bitcast.2, s32[16]{0:T(128)} %mask.3), custom_call_target="tpu_custom_call" | custom-call | flops 4000000000 | bytes 1000000 | tf_op jit(solution)/shard_map/first/pallas_call | solution.py:121
  1.7 0.6 %collective-permute-start = (bf16[56,640]{1,0:T(8,128)(2,1)S(1)}, bf16[56,640]{1,0:T(8,128)(2,1)S(1)}, u32[]{:S(2)}, u32[]{:S(2)}) collective-permute-start(bf16[56,640]{1,0:T(8,128)(2,1)S(1)} %get-tuple-element.23), channel_id=1, source_target_pairs={{0,1},{1,0},{2,3},{3,2},{4,5},{5,4},{6,7},{7,6},{8,9},{9,8},{10,11... | collective-permute-start | bytes 215048 | tf_op jit(solution)/shard_map/ppermute | solution.py:544
  2.3 5.7 %collective-permute-start.1 = (bf16[56,640]{1,0:T(8,128)(2,1)S(1)}, bf16[56,640]{1,0:T(8,128)(2,1)S(1)}, u32[]{:S(2)}, u32[]{:S(2)}) collective-permute-start(bf16[56,640]{1,0:T(8,128)(2,1)S(1)} %get-tuple-element.24), channel_id=1, source_target_pairs={{0,15},{1,2},{2,1},{3,4},{4,3},{5,6},{6,5},{7,8},{8,7},{9,10},{10,... | collective-permute-start | bytes 215048 | tf_op jit(solution)/shard_map/ppermute | solution.py:543
  7.9 0.0 copy-done.6
  7.9 0.0 copy-done.7
  7.9 0.0 copy-done.8
  7.9 0.0 copy-done.9
  7.9 0.0 copy-start.10
  7.9 2.5 %interior.1 = (bf16[256,3840]{1,0:T(8,128)(2,1)S(1)}, f32[16,3840]{1,0:T(8,128)S(1)}, bf16[144,5120]{1,0:T(8,128)(2,1)S(1)}, bf16[256,512]{1,0:T(8,128)(2,1)S(1)}, bf16[256,48]{1,0:T(8,128)(2,1)S(1)}) custom-call(bf16[8,48,640]{2,1,0:T(8,128)(2,1)S(1)} %copy-done.7, bf16[48,256]{1,0:T(8,128)(2,1)S(1)} %copy-done.8, bf16[3,3,256,256]{3,2,1,0:T(8,128)(2,1)S(1)} %copy-done.6, ...), custom_call_target="tpu_custom_call" | custom-call | flops 4000000000 | bytes 4000000 | tf_op jit(solution)/shard_map/interior/pallas_call | solution.py:185
  10.4 0.0 copy-done.10
  10.4 0.1 copy.14.ocean
  10.5 0.0 copy-start
  10.5 0.0 copy-start.1
  10.6 0.0 copy-start.2
  10.6 0.0 copy-start.3
  10.6 0.0 copy-start.4
  10.6 0.0 copy-start.5
  10.6 0.0 collective-permute-done.one
  10.6 0.0 collective-permute-done.1.two
  10.6 1.3 %edge.1 = (bf16[2,256,640]{2,1,0:T(8,128)(2,1)S(1)}, bf16[40,16,128]{2,1,0:T(8,128)(2,1)S(1)}, bf16[16,128]{1,0:T(8,128)(2,1)S(1)}, bf16[9,16,128]{2,1,0:T(8,128)(2,1)S(1)}, bf16[9,16,128]{2,1,0:T(8,128)(2,1)S(1)}) custom-call(bf16[56,640]{1,0:T(8,128)(2,1)S(1)} %collective-permute-done.one, bf16[56,640]{1,0:T(8,128)(2,1)S(1)} %collective-permute-done.1.two, ...), custom_call_target="tpu_custom_call" | custom-call | flops 1000000000 | bytes 1000000 | tf_op jit(solution)/shard_map/edge/pallas_call | solution.py:321
  11.9 0.1 collective-permute-start.4
  12.0 1.1 %collective-permute-start.2 = (bf16[9,16,128]{2,1,0:T(8,128)(2,1)S(1)}, bf16[9,16,128]{2,1,0:T(8,128)(2,1)S(1)}, u32[]{:S(2)}, u32[]{:S(2)}) collective-permute-start(bf16[9,16,128]{2,1,0:T(8,128)(2,1)S(1)} %get-tuple-element.32), channel_id=1, source_target_pairs={{0,1},{1,0},{2,3},{3,2},{4,5},{5,4},{6,7},{7,6},{8,9},{9,8},{10,11... | collective-permute-start | bytes 110600 | tf_op jit(solution)/shard_map/ppermute | solution.py:547
  13.1 2.8 %collective-permute-start.3 = (bf16[9,16,128]{2,1,0:T(8,128)(2,1)S(1)}, bf16[9,16,128]{2,1,0:T(8,128)(2,1)S(1)}, u32[]{:S(2)}, u32[]{:S(2)}) collective-permute-start(bf16[9,16,128]{2,1,0:T(8,128)(2,1)S(1)} %get-tuple-element.33), channel_id=1, source_target_pairs={{0,15},{1,2},{2,1},{3,4},{4,3},{5,6},{6,5},{7,8},{8,7},{9,10},{10,... | collective-permute-start | bytes 110600 | tf_op jit(solution)/shard_map/ppermute | solution.py:548
  15.9 0.0 copy-done
  15.9 0.0 copy-done.1
  15.9 0.0 copy-done.2
  15.9 0.0 copy-done.3
  15.9 0.0 copy-done.4
  15.9 0.0 copy-done.5
  15.9 2.5 %early.1 = (bf16[8,256,640]{2,1,0:T(8,128)(2,1)}, bf16[16,256,128]{2,1,0:T(8,128)(2,1)}, f32[32,1024]{1,0:T(8,128)S(1)}, f32[256,1024]{1,0:T(8,128)S(1)}, bf16[2...) custom-call(bf16[256,3840]{1,0:T(8,128)(2,1)S(1)} %get-tuple-element, ...), custom_call_target="tpu_custom_call" | custom-call | flops 1000000000 | bytes 6000000 | tf_op jit(solution)/shard_map/early/pallas_call | solution.py:404
  18.4 0.0 collective-permute-done.4.fold
  18.4 0.0 collective-permute-done.2.one
  18.4 0.7 %collective-permute-done.3.two = bf16[9,16,128]{2,1,0:T(8,128)(2,1)S(1)} collective-permute-done((bf16[9,16,128]{2,1,0:T(8,128)(2,1)S(1)}, bf16[9,16,128]{2,1,0:T(8,128)(2,1)S(1)}, u32[]{:S(2)}, u32[]{:S(2)}) %collective-permute-start.3) | collective-permute-done | bytes 36896 | tf_op jit(solution)/shard_map/ppermute | solution.py:548
  19.2 2.1 %late.1 = bf16[16,256,128]{2,1,0:T(8,128)(2,1)} custom-call(s32[16]{0:T(128)S(1)} %copy-done.5, bf16[9,16,128]{2,1,0:T(8,128)(2,1)S(1)} %collective-permute-done.2.one, bf16[9,16,128]{2,1,0:T(8,128)(2,1)S(1)} %collective-permute-done.3.two, bf16[16,128]{1,0:T(8,128)(2,1)S(1)} %collective-permute-done.4.fold, ...), custom_call_target="tpu_custom_call", output_to_operand_aliasing={{}: (10, {})} | custom-call | flops 1000000000 | bytes 1000000 | tf_op jit(solution)/shard_map/late/pallas_call | solution.py:499
Async XLA Ops:
  0.6 7.3 %copy-start.6 = (bf16[3,3,256,256]{3,2,1,0:T(8,128)(2,1)S(1)}, bf16[3,3,256,256]{3,2,1,0:T(8,128)(2,1)}, u32[]{:S(2)}) copy-start(bf16[3,3,256,256]{3,2,1,0:T(8,128)(2,1)} %conv.1) | copy-start | bytes 3538948
  0.6 7.3 %copy-start.7 = (bf16[8,48,640]{2,1,0:T(8,128)(2,1)S(1)}, bf16[8,48,640]{2,1,0:T(8,128)(2,1)}, u32[]{:S(2)}) copy-start(bf16[8,48,640]{2,1,0:T(8,128)(2,1)} %x_hbm.1) | copy-start | bytes 1474564
  0.7 7.3 %copy-start.8 = (bf16[48,256]{1,0:T(8,128)(2,1)S(1)}, bf16[48,256]{1,0:T(8,128)(2,1)}, u32[]{:S(2)}) copy-start(bf16[48,256]{1,0:T(8,128)(2,1)} %lift.1) | copy-start | bytes 73732
  0.7 7.3 %copy-start.9 = (bf16[256,16]{0,1:T(8,128)(2,1)S(1)}, bf16[256,16]{0,1:T(8,128)(2,1)}, u32[]{:S(2)}) copy-start(bf16[256,16]{0,1:T(8,128)(2,1)} %param.15) | copy-start | bytes 24580
  1.7 8.9 %collective-permute-start = (bf16[56,640]{1,0:T(8,128)(2,1)S(1)}, bf16[56,640]{1,0:T(8,128)(2,1)S(1)}, u32[]{:S(2)}, u32[]{:S(2)}) collective-permute-start(bf16[56,640]{1,0:T(8,128)(2,1)S(1)} %get-tuple-element.23), channel_id=1, source_target_pairs={{0,1},{1,0},{2,3},{3,2},{4,5},{5,4},{6,7},{7,6},{8,9},{9,8},{10,11... | collective-permute-start | bytes 215048 | tf_op jit(solution)/shard_map/ppermute | solution.py:544
  2.3 8.4 %collective-permute-start.1 = (bf16[56,640]{1,0:T(8,128)(2,1)S(1)}, bf16[56,640]{1,0:T(8,128)(2,1)S(1)}, u32[]{:S(2)}, u32[]{:S(2)}) collective-permute-start(bf16[56,640]{1,0:T(8,128)(2,1)S(1)} %get-tuple-element.24), channel_id=1, source_target_pairs={{0,15},{1,2},{2,1},{3,4},{4,3},{5,6},{6,5},{7,8},{8,7},{9,10},{10,... | collective-permute-start | bytes 215048 | tf_op jit(solution)/shard_map/ppermute | solution.py:543
  7.9 2.5 %copy-start.10 = (bf16[16,95,128]{2,0,1:T(8,128)(2,1)S(1)}, bf16[16,95,128]{2,0,1:T(8,128)(2,1)}, u32[]{:S(2)}) copy-start(bf16[16,95,128]{2,0,1:T(8,128)(2,1)} %param.12) | copy-start | bytes 1167364
  10.5 5.4 %copy-start = (bf16[16,4,128,128]{3,2,1,0:T(8,128)(2,1)S(1)}, bf16[16,4,128,128]{3,2,1,0:T(8,128)(2,1)}, u32[]{:S(2)}) copy-start(bf16[16,4,128,128]{3,2,1,0:T(8,128)(2,1)} %regrid.1) | copy-start | bytes 6291460
  10.5 5.3 %copy-start.1 = (bf16[256,256]{1,0:T(8,128)(2,1)S(1)}, bf16[256,256]{1,0:T(8,128)(2,1)}, u32[]{:S(2)}) copy-start(bf16[256,256]{1,0:T(8,128)(2,1)} %mw.1) | copy-start | bytes 393220
  10.6 5.3 %copy-start.2 = (bf16[95,256]{1,0:T(8,128)(2,1)S(1)}, bf16[95,256]{1,0:T(8,128)(2,1)}, u32[]{:S(2)}) copy-start(bf16[95,256]{1,0:T(8,128)(2,1)} %ow.1) | copy-start | bytes 145924
  10.6 5.3 %copy-start.3 = (bf16[16,256]{1,0:T(8,128)(2,1)S(1)}, bf16[16,256]{1,0:T(8,128)(2,1)}, u32[]{:S(2)}) copy-start(bf16[16,256]{1,0:T(8,128)(2,1)} %cw.1) | copy-start | bytes 24580
  10.6 5.3 %copy-start.4 = (s32[16,3]{0,1:T(4,128)S(1)}, s32[16,3]{0,1:T(4,128)}, u32[]{:S(2)}) copy-start(s32[16,3]{0,1:T(4,128)} %param.20) | copy-start | bytes 580
  10.6 5.3 %copy-start.5 = (s32[16]{0:T(128)S(1)}, s32[16]{0:T(128)}, u32[]{:S(2)}) copy-start(s32[16]{0:T(128)} %mask.3) | copy-start | bytes 196
  11.9 6.5 %collective-permute-start.4 = (bf16[16,128]{1,0:T(8,128)(2,1)S(1)}, bf16[16,128]{1,0:T(8,128)(2,1)S(1)}, u32[]{:S(2)}, u32[]{:S(2)}) collective-permute-start(bf16[16,128]{1,0:T(8,128)(2,1)S(1)} %get-tuple-element.34), channel_id=1, source_target_pairs={{0,8},{1,14},{2,13},{3,12},{4,11},{5,10},{6,9},{7,15},{8,0},{9,6},... | collective-permute-start | bytes 12296 | tf_op jit(solution)/shard_map/ppermute | solution.py:549
  12.0 6.4 %collective-permute-start.2 = (bf16[9,16,128]{2,1,0:T(8,128)(2,1)S(1)}, bf16[9,16,128]{2,1,0:T(8,128)(2,1)S(1)}, u32[]{:S(2)}, u32[]{:S(2)}) collective-permute-start(bf16[9,16,128]{2,1,0:T(8,128)(2,1)S(1)} %get-tuple-element.32), channel_id=1, source_target_pairs={{0,1},{1,0},{2,3},{3,2},{4,5},{5,4},{6,7},{7,6},{8,9},{9,8},{10,11... | collective-permute-start | bytes 110600 | tf_op jit(solution)/shard_map/ppermute | solution.py:547
  13.1 6.1 %collective-permute-start.3 = (bf16[9,16,128]{2,1,0:T(8,128)(2,1)S(1)}, bf16[9,16,128]{2,1,0:T(8,128)(2,1)S(1)}, u32[]{:S(2)}, u32[]{:S(2)}) collective-permute-start(bf16[9,16,128]{2,1,0:T(8,128)(2,1)S(1)} %get-tuple-element.33), channel_id=1, source_target_pairs={{0,15},{1,2},{2,1},{3,4},{4,3},{5,6},{6,5},{7,8},{8,7},{9,10},{10,... | collective-permute-start | bytes 110600 | tf_op jit(solution)/shard_map/ppermute | solution.py:548

commit v10 on v9

--- a/solution.py
+++ b/solution.py
@@ -19,10 +19,10 @@
 BUFS = 2
 AHEAD = 1
 ASK = 8
+TILE, OWN, WATER, COUNT = range(4)
 
 HBM = pl.BlockSpec(memory_space=pltpu.HBM)
 VM = pl.BlockSpec(memory_space=pltpu.VMEM)
-SM = pl.BlockSpec(memory_space=pltpu.SMEM)
 
 
 def dot(a, b):
@@ -89,7 +89,7 @@
     return jnp.minimum(found, MAXACT)
 
 
-def first_kernel(x_hbm, pair_hbm, mask_hbm, one, two, pair, mask, chosen, sems):
+def first_kernel(x_hbm, pair_hbm, mask_hbm, one, two, plan, pair, mask, chosen, sems):
     odd = parity()
     last = x_hbm.shape[0] - 1
     chans = x_hbm.shape[1]
@@ -102,8 +102,17 @@
     for c in copies:
         c.start()
     copies[0].wait()
-    list_tiles(mask, chosen, mask.shape[0])
+    found = list_tiles(mask, chosen, mask.shape[0])
     copies[1].wait()
+    row = lax.broadcasted_iota(jnp.int32, plan.shape, 0)
+    spot = lax.broadcasted_iota(jnp.int32, plan.shape, 1)
+    facts = jnp.where(row == COUNT, found, jnp.zeros(plan.shape, jnp.int32))
+    for k in range(MAXACT):
+        facts = jnp.where((row == TILE) & (spot == k), chosen[k], facts)
+        facts = jnp.where((row == OWN) & (spot == k), pair[1, chosen[k]], facts)
+    for t in range(mask.shape[0]):
+        facts = jnp.where((row == WATER) & (spot == t), mask[t], facts)
+    plan[...] = facts
     lane = lax.broadcasted_iota(jnp.int32, (ASK, 128), 1)
     for ref, side in ((one, 2 - 2 * odd), (two, 2 * odd)):
         asked = jnp.zeros((ASK, 128), jnp.int32)
@@ -120,9 +129,9 @@
     given = [pltpu.with_memory_space_constraint(v, pltpu.HBM) for v in (x, pair, mask)]
     return pl.pallas_call(
         first_kernel,
-        out_shape=(column, column),
+        out_shape=(column, column, jax.ShapeDtypeStruct((8, 128), jnp.int32)),
         in_specs=[HBM] * 3,
-        out_specs=(VM, VM),
+        out_specs=(VM,) * 3,
         scratch_shapes=[
             pltpu.SMEM(pair.shape, jnp.int32),
             pltpu.SMEM(mask.shape, jnp.int32),
@@ -346,9 +355,9 @@
 
 
 def early_kernel(
-    hid, edges, pair, mask, tiles, ocean, regrid, ow, cw, mw,
+    hid, edges, plan, tiles, ocean, regrid, ow, cw, mw,
     hid_out, out_hbm, sums, base, cwt, mwt, blocks, folds,
-    zero, chosen, sems,
+    zero, sems,
 ):
     count = ocean.shape[0]
     cells = ocean.shape[2]
@@ -364,10 +373,11 @@
         )
     for c in out:
         c.start()
-    list_tiles(mask, chosen, count)
+    facts = plan[...]
+    water = [facts[WATER, t] == 1 for t in range(count - FOLDB)]
     for t in range(count - FOLDB):
 
-        @pl.when(mask[t] != 1)
+        @pl.when(jnp.logical_not(water[t]))
         def _():
             pltpu.make_async_copy(zero, out_hbm.at[t], sems.at[columns]).start()
 
@@ -376,9 +386,9 @@
     owt = ow[...].astype(F32).T.astype(BF16)
     ones = jnp.ones(tiles.shape[1:], BF16)
     for k in range(MAXACT):
-        t = chosen[k]
+        t = facts[TILE, k]
         at = slice(k * cells, k * cells + cells)
-        mine = jnp.concatenate([tiles[pair[1, t]], ones], 0)
+        mine = jnp.concatenate([tiles[facts[OWN, k]], ones], 0)
         sums[:, at] = dot_t(mine, regrid[t, 1])
         base[:, at] = dot(owt, ocean[t])
         for side in range(2):
@@ -387,7 +397,7 @@
             folds[at, :] = regrid[t, 3]
     for t in range(count - FOLDB):
 
-        @pl.when(mask[t] != 1)
+        @pl.when(jnp.logical_not(water[t]))
         def _():
             pltpu.make_async_copy(zero, out_hbm.at[t], sems.at[columns]).wait()
 
@@ -395,7 +405,7 @@
         c.wait()
 
 
-def early(hid, edges, pair, mask, tiles, ocean, regrid, ow, cw, mw):
+def early(hid, edges, plan, tiles, ocean, regrid, ow, cw, mw):
     count, _, cells = ocean.shape
     width = mw.shape[0]
     fluxes = cw.shape[0]
@@ -413,23 +423,22 @@
             jax.ShapeDtypeStruct((MAXACT * cells, 2 * cells), BF16),
             jax.ShapeDtypeStruct((FOLDB * cells, cells), BF16),
         ),
-        in_specs=[VM, VM, SM, SM, VM, VM, VM, VM, VM, VM],
+        in_specs=[VM] * 9,
         out_specs=(HBM, HBM) + (VM,) * 6,
         scratch_shapes=[
             pltpu.VMEM((width, cells), BF16),
-            pltpu.SMEM((MAXACT + 1,), jnp.int32),
             pltpu.SemaphoreType.DMA((columns + 1,)),
         ],
         compiler_params=pltpu.CompilerParams(vmem_limit_bytes=12 * 2**20),
         cost_estimate=pl.CostEstimate(flops=10**9, bytes_accessed=6 * 10**6, transcendentals=0),
         name="early",
-    )(hid, edges, pair, mask, tiles, ocean, regrid, ow, cw, mw)
+    )(hid, edges, plan, tiles, ocean, regrid, ow, cw, mw)
 
 
 def late_kernel(
-    mask, one, two, fold, sums, base, cwt, mwt, blocks, folds, given_hbm,
+    plan, one, two, fold, sums, base, cwt, mwt, blocks, folds, given_hbm,
     out_hbm,
-    state, mixed_even, mixed_odd, out, chosen, sems,
+    state, mixed_even, mixed_odd, out, sems,
 ):
     fluxes = fold.shape[0]
     cells = out.shape[2]
@@ -475,7 +484,9 @@
                 half = mixed[p % 2][at, side * cells : (side + 1) * cells]
                 out[k, at, :] = (own + gelu_of_half(half)).astype(BF16)
 
-    found = list_tiles(mask, chosen, out_hbm.shape[0])
+    facts = plan[...]
+    found = facts[COUNT, 0]
+    chosen = [facts[TILE, k] for k in range(MAXACT)]
     mix(0)
     for p in range(pairs):
         if p + 1 < pairs:
@@ -494,26 +505,25 @@
             pltpu.make_async_copy(out.at[k], out_hbm.at[0], sems.at[k]).wait()
 
 
-def late(mask, one, two, fold, sums, base, cwt, mwt, blocks, folds, given):
+def late(plan, one, two, fold, sums, base, cwt, mwt, blocks, folds, given):
     count, width, cells = given.shape
     return pl.pallas_call(
         late_kernel,
         out_shape=jax.ShapeDtypeStruct((count, width, cells), BF16),
-        in_specs=[SM] + [VM] * 9 + [HBM],
+        in_specs=[VM] * 10 + [HBM],
         out_specs=HBM,
         scratch_shapes=[
             pltpu.VMEM((width, MAXACT * cells), BF16),
             pltpu.VMEM((width, 2 * cells), F32),
             pltpu.VMEM((width, 2 * cells), F32),
             pltpu.VMEM((MAXACT, width, cells), BF16),
-            pltpu.SMEM((MAXACT + 1,), jnp.int32),
             pltpu.SemaphoreType.DMA((MAXACT,)),
         ],
         input_output_aliases={10: 0},
         compiler_params=pltpu.CompilerParams(vmem_limit_bytes=12 * 2**20),
         cost_estimate=pl.CostEstimate(flops=10**9, bytes_accessed=10**6, transcendentals=3 * 10**5),
         name="late",
-    )(mask, one, two, fold, sums, base, cwt, mwt, blocks, folds, given)
+    )(plan, one, two, fold, sums, base, cwt, mwt, blocks, folds, given)
 
 
 def per_device(
@@ -538,8 +548,7 @@
         for i in range(strips)
     ]
     fwt = flux_weight.T
-    pair = pair_tile.T
-    send_one, send_two = first(atm_in, pair, ocean_mask)
+    send_one, send_two, plan = first(atm_in, pair_tile.T, ocean_mask)
     two = lax.ppermute(send_two, "lon", outward)
     one = lax.ppermute(send_one, "lon", inward)
     hid, flux, taps, wc, lt = interior(atm_in, lift_weight, conv_weight, fwt)
@@ -548,11 +557,11 @@
     two = lax.ppermute(send_two, "lon", outward)
     fold = lax.ppermute(north, "lon", mirror)
     atm_hidden, given, sums, base, cwt, mwt, blocks, folds = early(
-        hid, edges, pair, ocean_mask, tiles, ocean_in, regrid_weight,
+        hid, edges, plan, tiles, ocean_in, regrid_weight,
         ocean_weight, couple_weight, mix_weight,
     )
     ocean_hidden = late(
-        ocean_mask, one, two, fold, sums, base, cwt, mwt, blocks, folds, given
+        plan, one, two, fold, sums, base, cwt, mwt, blocks, folds, given
     )
     return (atm_hidden, ocean_hidden)
 

time: 21.5 us -> 21 us (0.977)
  Pallas kernels: 9.44 us -> 8.28 us
  waiting for transfers between devices: 0.76 us -> 1.53 us
    ppermute x2, waiting for transfers between devices: 0.75 us -> 1.52 us  [per_device(): two = lax.ppermute(send_two, 'lon', outward)]
    pallas_call x1, Pallas kernels: 2.5 us -> 1.74 us  [early(): pl.pallas_call(early_kernel, out_shape=(jax.ShapeDtypeStruct((columns, wi...]
    pallas_call x1, Pallas kernels: 2.14 us -> 1.61 us  [late(): pl.pallas_call(late_kernel, out_shape=jax.ShapeDtypeStruct((count, width,...]
  transfers between devices with their start and end apart: 5 -> 5, of which waited for: 1 -> 1; matrix products, arithmetic and copies ran while one was open for 0% -> 1% of each run, Pallas kernels for 23% -> 21%
where the time goes in v10:
time: 21 us; the launch traced here: 20.8 us
  starting transfers between devices  10.1 us (48%)
  Pallas kernels  8.28 us (39%)
  waiting for transfers between devices  1.53 us (7%)
  between operations  0.79 us (4%)
    ppermute x2, starting transfers between devices, per_device(): two = lax.ppermute(send_two, 'lon', outward)  8.43 us
    pallas_call x1, Pallas kernels, interior(): pl.pallas_call(inner_kernel, out_shape=(jax.ShapeDtypeStruct((width, inne...  2.59 us
    pallas_call x1, Pallas kernels, early(): pl.pallas_call(early_kernel, out_shape=(jax.ShapeDtypeStruct((columns, wi...  1.74 us
    pallas_call x1, Pallas kernels, late(): pl.pallas_call(late_kernel, out_shape=jax.ShapeDtypeStruct((count, width,...  1.61 us
    ppermute x2, starting transfers between devices, per_device(): one = lax.ppermute(send_one, 'lon', inward)  1.58 us
    ppermute x2, waiting for transfers between devices, per_device(): two = lax.ppermute(send_two, 'lon', outward)  1.52 us
    pallas_call x1, Pallas kernels, edge(): pl.pallas_call(edge_kernel, out_shape=(jax.ShapeDtypeStruct((2, width, la...  1.31 us
    pallas_call x1, Pallas kernels, first(): pl.pallas_call(first_kernel, out_shape=(column, column, jax.ShapeDtypeStr...  1.02 us
  transfers between devices with their start and end apart: 5, of which 1 were waited for; matrix products, arithmetic and copies ran while one was open for 1% of the time, Pallas kernels for 21%

profile of v10, /device:TPU:0, one launch (start us, length us, event | category | flops | bytes accessed | tf_op | source)
XLA Modules:
  0.0 20.8 jit_solution(4540231217082181876)
XLA Ops:
  0.6 0.0 copy-start.4
  0.6 0.0 copy-start.5
  0.7 0.0 copy-start.6
  0.7 0.0 copy-start.7
  0.7 1.0 %first.1 = (bf16[56,640]{1,0:T(8,128)(2,1)S(1)}, bf16[56,640]{1,0:T(8,128)(2,1)S(1)}, s32[8,128]{1,0:T(8,128)S(1)}) custom-call(bf16[8,48,640]{2,1,0:T(8,128)(2,1)} %x_hbm.1, s32[3,16]{1,0:T(4,128)} %bitcast.4, s32[16]{0:T(128)} %mask_hbm.1), custom_call_target="tpu_custom_call" | custom-call | flops 4000000000 | bytes 1000000 | tf_op jit(solution)/shard_map/first/pallas_call | solution.py:130
  1.7 0.6 %collective-permute-start = (bf16[56,640]{1,0:T(8,128)(2,1)S(1)}, bf16[56,640]{1,0:T(8,128)(2,1)S(1)}, u32[]{:S(2)}, u32[]{:S(2)}) collective-permute-start(bf16[56,640]{1,0:T(8,128)(2,1)S(1)} %get-tuple-element.24), channel_id=1, source_target_pairs={{0,1},{1,0},{2,3},{3,2},{4,5},{5,4},{6,7},{7,6},{8,9},{9,8},{10,11... | collective-permute-start | bytes 215048 | tf_op jit(solution)/shard_map/ppermute | solution.py:553
  2.3 5.7 %collective-permute-start.1 = (bf16[56,640]{1,0:T(8,128)(2,1)S(1)}, bf16[56,640]{1,0:T(8,128)(2,1)S(1)}, u32[]{:S(2)}, u32[]{:S(2)}) collective-permute-start(bf16[56,640]{1,0:T(8,128)(2,1)S(1)} %get-tuple-element.25), channel_id=1, source_target_pairs={{0,15},{1,2},{2,1},{3,4},{4,3},{5,6},{6,5},{7,8},{8,7},{9,10},{10,... | collective-permute-start | bytes 215048 | tf_op jit(solution)/shard_map/ppermute | solution.py:552
  7.9 0.0 copy-done.4
  7.9 0.0 copy-done.5
  7.9 0.0 copy-done.6
  7.9 0.0 copy-done.7
  7.9 0.0 copy-start.8
  7.9 2.6 %interior.1 = (bf16[256,3840]{1,0:T(8,128)(2,1)S(1)}, f32[16,3840]{1,0:T(8,128)S(1)}, bf16[144,5120]{1,0:T(8,128)(2,1)S(1)}, bf16[256,512]{1,0:T(8,128)(2,1)S(1)}, bf16[256,48]{1,0:T(8,128)(2,1)S(1)}) custom-call(bf16[8,48,640]{2,1,0:T(8,128)(2,1)S(1)} %copy-done.5, bf16[48,256]{1,0:T(8,128)(2,1)S(1)} %copy-done.6, bf16[3,3,256,256]{3,2,1,0:T(8,128)(2,1)S(1)} %copy-done.4, ...), custom_call_target="tpu_custom_call" | custom-call | flops 4000000000 | bytes 4000000 | tf_op jit(solution)/shard_map/interior/pallas_call | solution.py:194
  10.5 0.0 copy-done.8
  10.5 0.1 copy.14.ocean
  10.6 0.0 copy-start
  10.7 0.0 copy-start.1
  10.7 0.0 copy-start.2
  10.7 0.0 copy-start.3
  10.7 0.0 collective-permute-done.one
  10.7 0.0 collective-permute-done.1.two
  10.7 1.3 %edge.1 = (bf16[2,256,640]{2,1,0:T(8,128)(2,1)S(1)}, bf16[40,16,128]{2,1,0:T(8,128)(2,1)S(1)}, bf16[16,128]{1,0:T(8,128)(2,1)S(1)}, bf16[9,16,128]{2,1,0:T(8,128)(2,1)S(1)}, bf16[9,16,128]{2,1,0:T(8,128)(2,1)S(1)}) custom-call(bf16[56,640]{1,0:T(8,128)(2,1)S(1)} %collective-permute-done.one, bf16[56,640]{1,0:T(8,128)(2,1)S(1)} %collective-permute-done.1.two, ...), custom_call_target="tpu_custom_call" | custom-call | flops 1000000000 | bytes 1000000 | tf_op jit(solution)/shard_map/edge/pallas_call | solution.py:330
  12.0 0.1 collective-permute-start.4
  12.1 1.0 %collective-permute-start.2 = (bf16[9,16,128]{2,1,0:T(8,128)(2,1)S(1)}, bf16[9,16,128]{2,1,0:T(8,128)(2,1)S(1)}, u32[]{:S(2)}, u32[]{:S(2)}) collective-permute-start(bf16[9,16,128]{2,1,0:T(8,128)(2,1)S(1)} %get-tuple-element.34), channel_id=1, source_target_pairs={{0,1},{1,0},{2,3},{3,2},{4,5},{5,4},{6,7},{7,6},{8,9},{9,8},{10,11... | collective-permute-start | bytes 110600 | tf_op jit(solution)/shard_map/ppermute | solution.py:556
  13.1 2.8 %collective-permute-start.3 = (bf16[9,16,128]{2,1,0:T(8,128)(2,1)S(1)}, bf16[9,16,128]{2,1,0:T(8,128)(2,1)S(1)}, u32[]{:S(2)}, u32[]{:S(2)}) collective-permute-start(bf16[9,16,128]{2,1,0:T(8,128)(2,1)S(1)} %get-tuple-element.35), channel_id=1, source_target_pairs={{0,15},{1,2},{2,1},{3,4},{4,3},{5,6},{6,5},{7,8},{8,7},{9,10},{10,... | collective-permute-start | bytes 110600 | tf_op jit(solution)/shard_map/ppermute | solution.py:557
  15.9 0.0 copy-done
  15.9 0.0 copy-done.1
  15.9 0.0 copy-done.2
  15.9 0.0 copy-done.3
  15.9 1.7 %early.1 = (bf16[8,256,640]{2,1,0:T(8,128)(2,1)}, bf16[16,256,128]{2,1,0:T(8,128)(2,1)}, f32[32,1024]{1,0:T(8,128)S(1)}, f32[256,1024]{1,0:T(8,128)S(1)}, bf16[2...) custom-call(bf16[256,3840]{1,0:T(8,128)(2,1)S(1)} %get-tuple-element, ...), custom_call_target="tpu_custom_call" | custom-call | flops 1000000000 | bytes 6000000 | tf_op jit(solution)/shard_map/early/pallas_call | solution.py:414
  17.7 0.0 collective-permute-done.4.fold
  17.7 0.0 collective-permute-done.2.one
  17.7 1.5 %collective-permute-done.3.two = bf16[9,16,128]{2,1,0:T(8,128)(2,1)S(1)} collective-permute-done((bf16[9,16,128]{2,1,0:T(8,128)(2,1)S(1)}, bf16[9,16,128]{2,1,0:T(8,128)(2,1)S(1)}, u32[]{:S(2)}, u32[]{:S(2)}) %collective-permute-start.3) | collective-permute-done | bytes 36896 | tf_op jit(solution)/shard_map/ppermute | solution.py:557
  19.2 1.6 %late.1 = bf16[16,256,128]{2,1,0:T(8,128)(2,1)} custom-call(s32[8,128]{1,0:T(8,128)S(1)} %get-tuple-element.31.plan, bf16[9,16,128]{2,1,0:T(8,128)(2,1)S(1)} %collective-permute-done.2.one, bf16[9,16,128]{2,1,0:T(8,128)(2,1)S(1)} %collective-permute-done.3.two, bf16[16,128]{1,0:T(8,128)(2,1)S(1)} %collective-permute-done.4.fold, ...), custom_call_target="tpu_custom_call", output_to_operand_aliasing={{}: (10, {})} | custom-call | flops 1000000000 | bytes 1000000 | tf_op jit(solution)/shard_map/late/pallas_call | solution.py:510
Async XLA Ops:
  0.6 7.3 %copy-start.4 = (bf16[3,3,256,256]{3,2,1,0:T(8,128)(2,1)S(1)}, bf16[3,3,256,256]{3,2,1,0:T(8,128)(2,1)}, u32[]{:S(2)}) copy-start(bf16[3,3,256,256]{3,2,1,0:T(8,128)(2,1)} %conv.1) | copy-start | bytes 3538948
  0.6 7.3 %copy-start.5 = (bf16[8,48,640]{2,1,0:T(8,128)(2,1)S(1)}, bf16[8,48,640]{2,1,0:T(8,128)(2,1)}, u32[]{:S(2)}) copy-start(bf16[8,48,640]{2,1,0:T(8,128)(2,1)} %x_hbm.1) | copy-start | bytes 1474564
  0.7 7.3 %copy-start.6 = (bf16[48,256]{1,0:T(8,128)(2,1)S(1)}, bf16[48,256]{1,0:T(8,128)(2,1)}, u32[]{:S(2)}) copy-start(bf16[48,256]{1,0:T(8,128)(2,1)} %lift.1) | copy-start | bytes 73732
  0.7 7.3 %copy-start.7 = (bf16[256,16]{0,1:T(8,128)(2,1)S(1)}, bf16[256,16]{0,1:T(8,128)(2,1)}, u32[]{:S(2)}) copy-start(bf16[256,16]{0,1:T(8,128)(2,1)} %param.15) | copy-start | bytes 24580
  1.7 9.0 %collective-permute-start = (bf16[56,640]{1,0:T(8,128)(2,1)S(1)}, bf16[56,640]{1,0:T(8,128)(2,1)S(1)}, u32[]{:S(2)}, u32[]{:S(2)}) collective-permute-start(bf16[56,640]{1,0:T(8,128)(2,1)S(1)} %get-tuple-element.24), channel_id=1, source_target_pairs={{0,1},{1,0},{2,3},{3,2},{4,5},{5,4},{6,7},{7,6},{8,9},{9,8},{10,11... | collective-permute-start | bytes 215048 | tf_op jit(solution)/shard_map/ppermute | solution.py:553
  2.3 8.4 %collective-permute-start.1 = (bf16[56,640]{1,0:T(8,128)(2,1)S(1)}, bf16[56,640]{1,0:T(8,128)(2,1)S(1)}, u32[]{:S(2)}, u32[]{:S(2)}) collective-permute-start(bf16[56,640]{1,0:T(8,128)(2,1)S(1)} %get-tuple-element.25), channel_id=1, source_target_pairs={{0,15},{1,2},{2,1},{3,4},{4,3},{5,6},{6,5},{7,8},{8,7},{9,10},{10,... | collective-permute-start | bytes 215048 | tf_op jit(solution)/shard_map/ppermute | solution.py:552
  7.9 2.6 %copy-start.8 = (bf16[16,95,128]{2,0,1:T(8,128)(2,1)S(1)}, bf16[16,95,128]{2,0,1:T(8,128)(2,1)}, u32[]{:S(2)}) copy-start(bf16[16,95,128]{2,0,1:T(8,128)(2,1)} %param.12) | copy-start | bytes 1167364
  10.6 5.3 %copy-start = (bf16[16,4,128,128]{3,2,1,0:T(8,128)(2,1)S(1)}, bf16[16,4,128,128]{3,2,1,0:T(8,128)(2,1)}, u32[]{:S(2)}) copy-start(bf16[16,4,128,128]{3,2,1,0:T(8,128)(2,1)} %regrid.1) | copy-start | bytes 6291460
  10.7 5.3 %copy-start.1 = (bf16[256,256]{1,0:T(8,128)(2,1)S(1)}, bf16[256,256]{1,0:T(8,128)(2,1)}, u32[]{:S(2)}) copy-start(bf16[256,256]{1,0:T(8,128)(2,1)} %mw.1) | copy-start | bytes 393220
  10.7 5.2 %copy-start.2 = (bf16[95,256]{1,0:T(8,128)(2,1)S(1)}, bf16[95,256]{1,0:T(8,128)(2,1)}, u32[]{:S(2)}) copy-start(bf16[95,256]{1,0:T(8,128)(2,1)} %ow.1) | copy-start | bytes 145924
  10.7 5.2 %copy-start.3 = (bf16[16,256]{1,0:T(8,128)(2,1)S(1)}, bf16[16,256]{1,0:T(8,128)(2,1)}, u32[]{:S(2)}) copy-start(bf16[16,256]{1,0:T(8,128)(2,1)} %cw.1) | copy-start | bytes 24580
  12.0 5.6 %collective-permute-start.4 = (bf16[16,128]{1,0:T(8,128)(2,1)S(1)}, bf16[16,128]{1,0:T(8,128)(2,1)S(1)}, u32[]{:S(2)}, u32[]{:S(2)}) collective-permute-start(bf16[16,128]{1,0:T(8,128)(2,1)S(1)} %get-tuple-element.36), channel_id=1, source_target_pairs={{0,8},{1,14},{2,13},{3,12},{4,11},{5,10},{6,9},{7,15},{8,0},{9,6},... | collective-permute-start | bytes 12296 | tf_op jit(solution)/shard_map/ppermute | solution.py:558
  12.1 5.6 %collective-permute-start.2 = (bf16[9,16,128]{2,1,0:T(8,128)(2,1)S(1)}, bf16[9,16,128]{2,1,0:T(8,128)(2,1)S(1)}, u32[]{:S(2)}, u32[]{:S(2)}) collective-permute-start(bf16[9,16,128]{2,1,0:T(8,128)(2,1)S(1)} %get-tuple-element.34), channel_id=1, source_target_pairs={{0,1},{1,0},{2,3},{3,2},{4,5},{5,4},{6,7},{7,6},{8,9},{9,8},{10,11... | collective-permute-start | bytes 110600 | tf_op jit(solution)/shard_map/ppermute | solution.py:556
  13.1 6.1 %collective-permute-start.3 = (bf16[9,16,128]{2,1,0:T(8,128)(2,1)S(1)}, bf16[9,16,128]{2,1,0:T(8,128)(2,1)S(1)}, u32[]{:S(2)}, u32[]{:S(2)}) collective-permute-start(bf16[9,16,128]{2,1,0:T(8,128)(2,1)S(1)} %get-tuple-element.35), channel_id=1, source_target_pairs={{0,15},{1,2},{2,1},{3,4},{4,3},{5,6},{6,5},{7,8},{8,7},{9,10},{10,... | collective-permute-start | bytes 110600 | tf_op jit(solution)/shard_map/ppermute | solution.py:557

commit v11 on v10

--- a/solution.py
+++ b/solution.py
@@ -457,18 +457,20 @@
         return [jnp.concatenate([west, east], 1), jnp.concatenate([ones, ones], 1)]
 
     half = 2 * fluxes
-    totals = []
-    for p in range(pairs):
-        at = slice(p * wide, p * wide + wide)
-        product = dot_t(jnp.concatenate(got(2 * p) + got(2 * p + 1), 0), blocks[at, :])
-        total = jnp.concatenate([product[:half, :cells], product[half:, cells:]], 1) + sums[:, at]
-        if 2 * p < FOLDB:
-            total = total + dot_t(jnp.concatenate([partner, ones], 0), folds[at, :])
-        totals.append(total)
-    for p in range(pairs):
-        at = slice(p * wide, p * wide + wide)
-        regrid = (totals[p][:fluxes] / totals[p][fluxes : fluxes + 1]).astype(BF16)
-        state[:, at] = (base[:, at] + dot(cwt[...], regrid)).astype(BF16)
+
+    def settle(group):
+        totals = []
+        for p in group:
+            at = slice(p * wide, p * wide + wide)
+            product = dot_t(jnp.concatenate(got(2 * p) + got(2 * p + 1), 0), blocks[at, :])
+            total = jnp.concatenate([product[:half, :cells], product[half:, cells:]], 1) + sums[:, at]
+            if 2 * p < FOLDB:
+                total = total + dot_t(jnp.concatenate([partner, ones], 0), folds[at, :])
+            totals.append(total)
+        for p, total in zip(group, totals):
+            at = slice(p * wide, p * wide + wide)
+            regrid = (total[:fluxes] / total[fluxes : fluxes + 1]).astype(BF16)
+            state[:, at] = (base[:, at] + dot(cwt[...], regrid)).astype(BF16)
 
     mixed = (mixed_even, mixed_odd)
 
@@ -481,28 +483,40 @@
             for side in range(2):
                 k = 2 * p + side
                 own = state[at, k * cells : (k + 1) * cells].astype(F32)
-                half = mixed[p % 2][at, side * cells : (side + 1) * cells]
-                out[k, at, :] = (own + gelu_of_half(half)).astype(BF16)
+                gate = mixed[p % 2][at, side * cells : (side + 1) * cells]
+                out[k, at, :] = (own + gelu_of_half(gate)).astype(BF16)
 
     facts = plan[...]
     found = facts[COUNT, 0]
     chosen = [facts[TILE, k] for k in range(MAXACT)]
-    mix(0)
-    for p in range(pairs):
-        if p + 1 < pairs:
-            mix(p + 1)
-        finish(p)
-        for k in (2 * p, 2 * p + 1):
-
-            @pl.when(k < found)
-            def _():
-                pltpu.make_async_copy(out.at[k], out_hbm.at[chosen[k]], sems.at[k]).start()
+
+    def send(k):
+        return pltpu.make_async_copy(out.at[k], out_hbm.at[chosen[k]], sems.at[k])
+
+    def run(group):
+        settle(group)
+        mix(group[0])
+        for p in group:
+            if p + 1 in group:
+                mix(p + 1)
+            finish(p)
+            for k in (2 * p, 2 * p + 1):
+                if k < FOLDB:
+                    send(k).start()
+                else:
+                    pl.when(k < found)(lambda k=k: send(k).start())
+
+    run(range(pairs // 2))
+
+    @pl.when(found > pairs // 2 * 2)
+    def _():
+        run(range(pairs // 2, pairs))
 
     for k in range(MAXACT):
-
-        @pl.when(k < found)
-        def _():
-            pltpu.make_async_copy(out.at[k], out_hbm.at[0], sems.at[k]).wait()
+        if k < FOLDB:
+            send(k).wait()
+        else:
+            pl.when(k < found)(lambda k=k: send(k).wait())
 
 
 def late(plan, one, two, fold, sums, base, cwt, mwt, blocks, folds, given):

time: 21 us -> 21.5 us (1.024)
  Pallas kernels: 8.28 us -> 8.81 us
    pallas_call x1, Pallas kernels: 1.61 us -> 2.15 us  [late(): pl.pallas_call(late_kernel, out_shape=jax.ShapeDtypeStruct((count, width,...]
  transfers between devices with their start and end apart: 5 -> 5, of which waited for: 1 -> 1; matrix products, arithmetic and copies ran while one was open for 1% -> 0% of each run, Pallas kernels for 21% -> 20%
where the time goes in v11:
time: 21.5 us; the launch traced here: 21.4 us
  starting transfers between devices  10.1 us (47%)
  Pallas kernels  8.81 us (41%)
  waiting for transfers between devices  1.53 us (7%)
  between operations  0.79 us (4%)
    ppermute x2, starting transfers between devices, per_device(): two = lax.ppermute(send_two, 'lon', outward)  8.43 us
    pallas_call x1, Pallas kernels, interior(): pl.pallas_call(inner_kernel, out_shape=(jax.ShapeDtypeStruct((width, inne...  2.59 us
    pallas_call x1, Pallas kernels, late(): pl.pallas_call(late_kernel, out_shape=jax.ShapeDtypeStruct((count, width,...  2.15 us
    pallas_call x1, Pallas kernels, early(): pl.pallas_call(early_kernel, out_shape=(jax.ShapeDtypeStruct((columns, wi...  1.74 us
    ppermute x2, starting transfers between devices, per_device(): one = lax.ppermute(send_one, 'lon', inward)  1.58 us
    ppermute x2, waiting for transfers between devices, per_device(): two = lax.ppermute(send_two, 'lon', outward)  1.52 us
    pallas_call x1, Pallas kernels, edge(): pl.pallas_call(edge_kernel, out_shape=(jax.ShapeDtypeStruct((2, width, la...  1.31 us
    pallas_call x1, Pallas kernels, first(): pl.pallas_call(first_kernel, out_shape=(column, column, jax.ShapeDtypeStr...  1.02 us
  transfers between devices with their start and end apart: 5, of which 1 were waited for; matrix products, arithmetic and copies ran while one was open for 0% of the time, Pallas kernels for 20%

profile of v11, /device:TPU:0, one launch (start us, length us, event | category | flops | bytes accessed | tf_op | source)
XLA Modules:
  0.0 21.4 jit_solution(14626249381605581731)
XLA Ops:
  0.6 0.0 copy-start.4
  0.6 0.0 copy-start.5
  0.7 0.0 copy-start.6
  0.7 0.0 copy-start.7
  0.7 1.0 %first.1 = (bf16[56,640]{1,0:T(8,128)(2,1)S(1)}, bf16[56,640]{1,0:T(8,128)(2,1)S(1)}, s32[8,128]{1,0:T(8,128)S(1)}) custom-call(bf16[8,48,640]{2,1,0:T(8,128)(2,1)} %x_hbm.1, s32[3,16]{1,0:T(4,128)} %bitcast.4, s32[16]{0:T(128)} %mask_hbm.1), custom_call_target="tpu_custom_call" | custom-call | flops 4000000000 | bytes 1000000 | tf_op jit(solution)/shard_map/first/pallas_call | solution.py:130
  1.7 0.6 %collective-permute-start = (bf16[56,640]{1,0:T(8,128)(2,1)S(1)}, bf16[56,640]{1,0:T(8,128)(2,1)S(1)}, u32[]{:S(2)}, u32[]{:S(2)}) collective-permute-start(bf16[56,640]{1,0:T(8,128)(2,1)S(1)} %get-tuple-element.24), channel_id=1, source_target_pairs={{0,1},{1,0},{2,3},{3,2},{4,5},{5,4},{6,7},{7,6},{8,9},{9,8},{10,11... | collective-permute-start | bytes 215048 | tf_op jit(solution)/shard_map/ppermute | solution.py:567
  2.3 5.7 %collective-permute-start.1 = (bf16[56,640]{1,0:T(8,128)(2,1)S(1)}, bf16[56,640]{1,0:T(8,128)(2,1)S(1)}, u32[]{:S(2)}, u32[]{:S(2)}) collective-permute-start(bf16[56,640]{1,0:T(8,128)(2,1)S(1)} %get-tuple-element.25), channel_id=1, source_target_pairs={{0,15},{1,2},{2,1},{3,4},{4,3},{5,6},{6,5},{7,8},{8,7},{9,10},{10,... | collective-permute-start | bytes 215048 | tf_op jit(solution)/shard_map/ppermute | solution.py:566
  7.9 0.0 copy-done.4
  7.9 0.0 copy-done.5
  7.9 0.0 copy-done.6
  7.9 0.0 copy-done.7
  7.9 0.0 copy-start.8
  7.9 2.6 %interior.1 = (bf16[256,3840]{1,0:T(8,128)(2,1)S(1)}, f32[16,3840]{1,0:T(8,128)S(1)}, bf16[144,5120]{1,0:T(8,128)(2,1)S(1)}, bf16[256,512]{1,0:T(8,128)(2,1)S(1)}, bf16[256,48]{1,0:T(8,128)(2,1)S(1)}) custom-call(bf16[8,48,640]{2,1,0:T(8,128)(2,1)S(1)} %copy-done.5, bf16[48,256]{1,0:T(8,128)(2,1)S(1)} %copy-done.6, bf16[3,3,256,256]{3,2,1,0:T(8,128)(2,1)S(1)} %copy-done.4, ...), custom_call_target="tpu_custom_call" | custom-call | flops 4000000000 | bytes 4000000 | tf_op jit(solution)/shard_map/interior/pallas_call | solution.py:194
  10.5 0.0 copy-done.8
  10.5 0.1 copy.14.ocean
  10.6 0.0 copy-start
  10.7 0.0 copy-start.1
  10.7 0.0 copy-start.2
  10.7 0.0 copy-start.3
  10.7 0.0 collective-permute-done.one
  10.7 0.0 collective-permute-done.1.two
  10.7 1.3 %edge.1 = (bf16[2,256,640]{2,1,0:T(8,128)(2,1)S(1)}, bf16[40,16,128]{2,1,0:T(8,128)(2,1)S(1)}, bf16[16,128]{1,0:T(8,128)(2,1)S(1)}, bf16[9,16,128]{2,1,0:T(8,128)(2,1)S(1)}, bf16[9,16,128]{2,1,0:T(8,128)(2,1)S(1)}) custom-call(bf16[56,640]{1,0:T(8,128)(2,1)S(1)} %collective-permute-done.one, bf16[56,640]{1,0:T(8,128)(2,1)S(1)} %collective-permute-done.1.two, ...), custom_call_target="tpu_custom_call" | custom-call | flops 1000000000 | bytes 1000000 | tf_op jit(solution)/shard_map/edge/pallas_call | solution.py:330
  12.0 0.1 collective-permute-start.4
  12.1 1.0 %collective-permute-start.2 = (bf16[9,16,128]{2,1,0:T(8,128)(2,1)S(1)}, bf16[9,16,128]{2,1,0:T(8,128)(2,1)S(1)}, u32[]{:S(2)}, u32[]{:S(2)}) collective-permute-start(bf16[9,16,128]{2,1,0:T(8,128)(2,1)S(1)} %get-tuple-element.34), channel_id=1, source_target_pairs={{0,1},{1,0},{2,3},{3,2},{4,5},{5,4},{6,7},{7,6},{8,9},{9,8},{10,11... | collective-permute-start | bytes 110600 | tf_op jit(solution)/shard_map/ppermute | solution.py:570
  13.1 2.8 %collective-permute-start.3 = (bf16[9,16,128]{2,1,0:T(8,128)(2,1)S(1)}, bf16[9,16,128]{2,1,0:T(8,128)(2,1)S(1)}, u32[]{:S(2)}, u32[]{:S(2)}) collective-permute-start(bf16[9,16,128]{2,1,0:T(8,128)(2,1)S(1)} %get-tuple-element.35), channel_id=1, source_target_pairs={{0,15},{1,2},{2,1},{3,4},{4,3},{5,6},{6,5},{7,8},{8,7},{9,10},{10,... | collective-permute-start | bytes 110600 | tf_op jit(solution)/shard_map/ppermute | solution.py:571
  15.9 0.0 copy-done
  15.9 0.0 copy-done.1
  15.9 0.0 copy-done.2
  15.9 0.0 copy-done.3
  15.9 1.7 %early.1 = (bf16[8,256,640]{2,1,0:T(8,128)(2,1)}, bf16[16,256,128]{2,1,0:T(8,128)(2,1)}, f32[32,1024]{1,0:T(8,128)S(1)}, f32[256,1024]{1,0:T(8,128)S(1)}, bf16[2...) custom-call(bf16[256,3840]{1,0:T(8,128)(2,1)S(1)} %get-tuple-element, ...), custom_call_target="tpu_custom_call" | custom-call | flops 1000000000 | bytes 6000000 | tf_op jit(solution)/shard_map/early/pallas_call | solution.py:414
  17.7 0.0 collective-permute-done.4.fold
  17.7 0.0 collective-permute-done.2.one
  17.7 1.5 %collective-permute-done.3.two = bf16[9,16,128]{2,1,0:T(8,128)(2,1)S(1)} collective-permute-done((bf16[9,16,128]{2,1,0:T(8,128)(2,1)S(1)}, bf16[9,16,128]{2,1,0:T(8,128)(2,1)S(1)}, u32[]{:S(2)}, u32[]{:S(2)}) %collective-permute-start.3) | collective-permute-done | bytes 36896 | tf_op jit(solution)/shard_map/ppermute | solution.py:571
  19.2 2.1 %late.1 = bf16[16,256,128]{2,1,0:T(8,128)(2,1)} custom-call(s32[8,128]{1,0:T(8,128)S(1)} %get-tuple-element.31.plan, bf16[9,16,128]{2,1,0:T(8,128)(2,1)S(1)} %collective-permute-done.2.one, bf16[9,16,128]{2,1,0:T(8,128)(2,1)S(1)} %collective-permute-done.3.two, bf16[16,128]{1,0:T(8,128)(2,1)S(1)} %collective-permute-done.4.fold, ...), custom_call_target="tpu_custom_call", output_to_operand_aliasing={{}: (10, {})} | custom-call | flops 1000000000 | bytes 1000000 | tf_op jit(solution)/shard_map/late/pallas_call | solution.py:524
Async XLA Ops:
  0.6 7.3 %copy-start.4 = (bf16[3,3,256,256]{3,2,1,0:T(8,128)(2,1)S(1)}, bf16[3,3,256,256]{3,2,1,0:T(8,128)(2,1)}, u32[]{:S(2)}) copy-start(bf16[3,3,256,256]{3,2,1,0:T(8,128)(2,1)} %conv.1) | copy-start | bytes 3538948
  0.6 7.3 %copy-start.5 = (bf16[8,48,640]{2,1,0:T(8,128)(2,1)S(1)}, bf16[8,48,640]{2,1,0:T(8,128)(2,1)}, u32[]{:S(2)}) copy-start(bf16[8,48,640]{2,1,0:T(8,128)(2,1)} %x_hbm.1) | copy-start | bytes 1474564
  0.7 7.3 %copy-start.6 = (bf16[48,256]{1,0:T(8,128)(2,1)S(1)}, bf16[48,256]{1,0:T(8,128)(2,1)}, u32[]{:S(2)}) copy-start(bf16[48,256]{1,0:T(8,128)(2,1)} %lift.1) | copy-start | bytes 73732
  0.7 7.3 %copy-start.7 = (bf16[256,16]{0,1:T(8,128)(2,1)S(1)}, bf16[256,16]{0,1:T(8,128)(2,1)}, u32[]{:S(2)}) copy-start(bf16[256,16]{0,1:T(8,128)(2,1)} %param.15) | copy-start | bytes 24580
  1.7 9.0 %collective-permute-start = (bf16[56,640]{1,0:T(8,128)(2,1)S(1)}, bf16[56,640]{1,0:T(8,128)(2,1)S(1)}, u32[]{:S(2)}, u32[]{:S(2)}) collective-permute-start(bf16[56,640]{1,0:T(8,128)(2,1)S(1)} %get-tuple-element.24), channel_id=1, source_target_pairs={{0,1},{1,0},{2,3},{3,2},{4,5},{5,4},{6,7},{7,6},{8,9},{9,8},{10,11... | collective-permute-start | bytes 215048 | tf_op jit(solution)/shard_map/ppermute | solution.py:567
  2.3 8.4 %collective-permute-start.1 = (bf16[56,640]{1,0:T(8,128)(2,1)S(1)}, bf16[56,640]{1,0:T(8,128)(2,1)S(1)}, u32[]{:S(2)}, u32[]{:S(2)}) collective-permute-start(bf16[56,640]{1,0:T(8,128)(2,1)S(1)} %get-tuple-element.25), channel_id=1, source_target_pairs={{0,15},{1,2},{2,1},{3,4},{4,3},{5,6},{6,5},{7,8},{8,7},{9,10},{10,... | collective-permute-start | bytes 215048 | tf_op jit(solution)/shard_map/ppermute | solution.py:566
  7.9 2.6 %copy-start.8 = (bf16[16,95,128]{2,0,1:T(8,128)(2,1)S(1)}, bf16[16,95,128]{2,0,1:T(8,128)(2,1)}, u32[]{:S(2)}) copy-start(bf16[16,95,128]{2,0,1:T(8,128)(2,1)} %param.12) | copy-start | bytes 1167364
  10.6 5.3 %copy-start = (bf16[16,4,128,128]{3,2,1,0:T(8,128)(2,1)S(1)}, bf16[16,4,128,128]{3,2,1,0:T(8,128)(2,1)}, u32[]{:S(2)}) copy-start(bf16[16,4,128,128]{3,2,1,0:T(8,128)(2,1)} %regrid.1) | copy-start | bytes 6291460
  10.7 5.3 %copy-start.1 = (bf16[256,256]{1,0:T(8,128)(2,1)S(1)}, bf16[256,256]{1,0:T(8,128)(2,1)}, u32[]{:S(2)}) copy-start(bf16[256,256]{1,0:T(8,128)(2,1)} %mw.1) | copy-start | bytes 393220
  10.7 5.2 %copy-start.2 = (bf16[95,256]{1,0:T(8,128)(2,1)S(1)}, bf16[95,256]{1,0:T(8,128)(2,1)}, u32[]{:S(2)}) copy-start(bf16[95,256]{1,0:T(8,128)(2,1)} %ow.1) | copy-start | bytes 145924
  10.7 5.2 %copy-start.3 = (bf16[16,256]{1,0:T(8,128)(2,1)S(1)}, bf16[16,256]{1,0:T(8,128)(2,1)}, u32[]{:S(2)}) copy-start(bf16[16,256]{1,0:T(8,128)(2,1)} %cw.1) | copy-start | bytes 24580
  12.0 5.6 %collective-permute-start.4 = (bf16[16,128]{1,0:T(8,128)(2,1)S(1)}, bf16[16,128]{1,0:T(8,128)(2,1)S(1)}, u32[]{:S(2)}, u32[]{:S(2)}) collective-permute-start(bf16[16,128]{1,0:T(8,128)(2,1)S(1)} %get-tuple-element.36), channel_id=1, source_target_pairs={{0,8},{1,14},{2,13},{3,12},{4,11},{5,10},{6,9},{7,15},{8,0},{9,6},... | collective-permute-start | bytes 12296 | tf_op jit(solution)/shard_map/ppermute | solution.py:572
  12.1 5.6 %collective-permute-start.2 = (bf16[9,16,128]{2,1,0:T(8,128)(2,1)S(1)}, bf16[9,16,128]{2,1,0:T(8,128)(2,1)S(1)}, u32[]{:S(2)}, u32[]{:S(2)}) collective-permute-start(bf16[9,16,128]{2,1,0:T(8,128)(2,1)S(1)} %get-tuple-element.34), channel_id=1, source_target_pairs={{0,1},{1,0},{2,3},{3,2},{4,5},{5,4},{6,7},{7,6},{8,9},{9,8},{10,11... | collective-permute-start | bytes 110600 | tf_op jit(solution)/shard_map/ppermute | solution.py:570
  13.1 6.1 %collective-permute-start.3 = (bf16[9,16,128]{2,1,0:T(8,128)(2,1)S(1)}, bf16[9,16,128]{2,1,0:T(8,128)(2,1)S(1)}, u32[]{:S(2)}, u32[]{:S(2)}) collective-permute-start(bf16[9,16,128]{2,1,0:T(8,128)(2,1)S(1)} %get-tuple-element.35), channel_id=1, source_target_pairs={{0,15},{1,2},{2,1},{3,4},{4,3},{5,6},{6,5},{7,8},{8,7},{9,10},{10,... | collective-permute-start | bytes 110600 | tf_op jit(solution)/shard_map/ppermute | solution.py:571

commit v12 on v11

--- a/solution.py
+++ b/solution.py
@@ -438,7 +438,7 @@
 def late_kernel(
     plan, one, two, fold, sums, base, cwt, mwt, blocks, folds, given_hbm,
     out_hbm,
-    state, mixed_even, mixed_odd, out, sems,
+    state, mixed, out, sems,
 ):
     fluxes = fold.shape[0]
     cells = out.shape[2]
@@ -472,10 +472,9 @@
             regrid = (total[:fluxes] / total[fluxes : fluxes + 1]).astype(BF16)
             state[:, at] = (base[:, at] + dot(cwt[...], regrid)).astype(BF16)
 
-    mixed = (mixed_even, mixed_odd)
 
     def mix(p):
-        mixed[p % 2][...] = dot(mwt[...], state[:, p * wide : p * wide + wide])
+        mixed[p] = dot(mwt[...], state[:, p * wide : p * wide + wide])
 
     def finish(p):
         for r in range(0, state.shape[0], STRIP):
@@ -483,7 +482,7 @@
             for side in range(2):
                 k = 2 * p + side
                 own = state[at, k * cells : (k + 1) * cells].astype(F32)
-                gate = mixed[p % 2][at, side * cells : (side + 1) * cells]
+                gate = mixed[p, at, side * cells : (side + 1) * cells]
                 out[k, at, :] = (own + gelu_of_half(gate)).astype(BF16)
 
     facts = plan[...]
@@ -493,24 +492,30 @@
     def send(k):
         return pltpu.make_async_copy(out.at[k], out_hbm.at[chosen[k]], sems.at[k])
 
-    def run(group):
-        settle(group)
-        mix(group[0])
-        for p in group:
-            if p + 1 in group:
-                mix(p + 1)
-            finish(p)
-            for k in (2 * p, 2 * p + 1):
-                if k < FOLDB:
-                    send(k).start()
-                else:
-                    pl.when(k < found)(lambda k=k: send(k).start())
-
-    run(range(pairs // 2))
+    def close(p):
+        finish(p)
+        for k in (2 * p, 2 * p + 1):
+            if k < FOLDB:
+                send(k).start()
+            else:
+                pl.when(k < found)(lambda k=k: send(k).start())
+
+    settle(range(pairs))
+    for p in range(pairs):
+        mix(p)
+    for p in range(pairs // 2):
+        finish(p)
+    for p in range(pairs // 2):
+        for k in (2 * p, 2 * p + 1):
+            if k < FOLDB:
+                send(k).start()
+            else:
+                pl.when(k < found)(lambda k=k: send(k).start())
 
     @pl.when(found > pairs // 2 * 2)
     def _():
-        run(range(pairs // 2, pairs))
+        for p in range(pairs // 2, pairs):
+            close(p)
 
     for k in range(MAXACT):
         if k < FOLDB:
@@ -528,8 +533,7 @@
         out_specs=HBM,
         scratch_shapes=[
             pltpu.VMEM((width, MAXACT * cells), BF16),
-            pltpu.VMEM((width, 2 * cells), F32),
-            pltpu.VMEM((width, 2 * cells), F32),
+            pltpu.VMEM((MAXACT // 2, width, 2 * cells), F32),
             pltpu.VMEM((MAXACT, width, cells), BF16),
             pltpu.SemaphoreType.DMA((MAXACT,)),
         ],

time: 21.5 us -> 21 us (0.977)
  Pallas kernels: 8.81 us -> 8.28 us
    pallas_call x1, Pallas kernels: 2.15 us -> 1.62 us  [late(): pl.pallas_call(late_kernel, out_shape=jax.ShapeDtypeStruct((count, width,...]
  transfers between devices with their start and end apart: 5 -> 5, of which waited for: 1 -> 1; matrix products, arithmetic and copies ran while one was open for 0% -> 1% of each run, Pallas kernels for 20% -> 21%
where the time goes in v12:
time: 21 us; the launch traced here: 20.8 us
  starting transfers between devices  10.1 us (48%)
  Pallas kernels  8.28 us (39%)
  waiting for transfers between devices  1.53 us (7%)
  between operations  0.79 us (4%)
    ppermute x2, starting transfers between devices, per_device(): two = lax.ppermute(send_two, 'lon', outward)  8.43 us
    pallas_call x1, Pallas kernels, interior(): pl.pallas_call(inner_kernel, out_shape=(jax.ShapeDtypeStruct((width, inne...  2.59 us
    pallas_call x1, Pallas kernels, early(): pl.pallas_call(early_kernel, out_shape=(jax.ShapeDtypeStruct((columns, wi...  1.74 us
    pallas_call x1, Pallas kernels, late(): pl.pallas_call(late_kernel, out_shape=jax.ShapeDtypeStruct((count, width,...  1.62 us
    ppermute x2, starting transfers between devices, per_device(): one = lax.ppermute(send_one, 'lon', inward)  1.58 us
    ppermute x2, waiting for transfers between devices, per_device(): two = lax.ppermute(send_two, 'lon', outward)  1.52 us
    pallas_call x1, Pallas kernels, edge(): pl.pallas_call(edge_kernel, out_shape=(jax.ShapeDtypeStruct((2, width, la...  1.31 us
    pallas_call x1, Pallas kernels, first(): pl.pallas_call(first_kernel, out_shape=(column, column, jax.ShapeDtypeStr...  1.02 us
  transfers between devices with their start and end apart: 5, of which 1 were waited for; matrix products, arithmetic and copies ran while one was open for 1% of the time, Pallas kernels for 21%

profile of v12, /device:TPU:0, one launch (start us, length us, event | category | flops | bytes accessed | tf_op | source)
XLA Modules:
  0.0 20.8 jit_solution(9328862136385970708)
XLA Ops:
  0.6 0.0 copy-start.4
  0.6 0.0 copy-start.5
  0.7 0.0 copy-start.6
  0.7 0.0 copy-start.7
  0.7 1.0 %first.1 = (bf16[56,640]{1,0:T(8,128)(2,1)S(1)}, bf16[56,640]{1,0:T(8,128)(2,1)S(1)}, s32[8,128]{1,0:T(8,128)S(1)}) custom-call(bf16[8,48,640]{2,1,0:T(8,128)(2,1)} %x_hbm.1, s32[3,16]{1,0:T(4,128)} %bitcast.4, s32[16]{0:T(128)} %mask_hbm.1), custom_call_target="tpu_custom_call" | custom-call | flops 4000000000 | bytes 1000000 | tf_op jit(solution)/shard_map/first/pallas_call | solution.py:130
  1.7 0.6 %collective-permute-start = (bf16[56,640]{1,0:T(8,128)(2,1)S(1)}, bf16[56,640]{1,0:T(8,128)(2,1)S(1)}, u32[]{:S(2)}, u32[]{:S(2)}) collective-permute-start(bf16[56,640]{1,0:T(8,128)(2,1)S(1)} %get-tuple-element.24), channel_id=1, source_target_pairs={{0,1},{1,0},{2,3},{3,2},{4,5},{5,4},{6,7},{7,6},{8,9},{9,8},{10,11... | collective-permute-start | bytes 215048 | tf_op jit(solution)/shard_map/ppermute | solution.py:571
  2.3 5.7 %collective-permute-start.1 = (bf16[56,640]{1,0:T(8,128)(2,1)S(1)}, bf16[56,640]{1,0:T(8,128)(2,1)S(1)}, u32[]{:S(2)}, u32[]{:S(2)}) collective-permute-start(bf16[56,640]{1,0:T(8,128)(2,1)S(1)} %get-tuple-element.25), channel_id=1, source_target_pairs={{0,15},{1,2},{2,1},{3,4},{4,3},{5,6},{6,5},{7,8},{8,7},{9,10},{10,... | collective-permute-start | bytes 215048 | tf_op jit(solution)/shard_map/ppermute | solution.py:570
  7.9 0.0 copy-done.4
  7.9 0.0 copy-done.5
  7.9 0.0 copy-done.6
  7.9 0.0 copy-done.7
  7.9 0.0 copy-start.8
  7.9 2.6 %interior.1 = (bf16[256,3840]{1,0:T(8,128)(2,1)S(1)}, f32[16,3840]{1,0:T(8,128)S(1)}, bf16[144,5120]{1,0:T(8,128)(2,1)S(1)}, bf16[256,512]{1,0:T(8,128)(2,1)S(1)}, bf16[256,48]{1,0:T(8,128)(2,1)S(1)}) custom-call(bf16[8,48,640]{2,1,0:T(8,128)(2,1)S(1)} %copy-done.5, bf16[48,256]{1,0:T(8,128)(2,1)S(1)} %copy-done.6, bf16[3,3,256,256]{3,2,1,0:T(8,128)(2,1)S(1)} %copy-done.4, ...), custom_call_target="tpu_custom_call" | custom-call | flops 4000000000 | bytes 4000000 | tf_op jit(solution)/shard_map/interior/pallas_call | solution.py:194
  10.5 0.0 copy-done.8
  10.5 0.1 copy.14.ocean
  10.6 0.0 copy-start
  10.7 0.0 copy-start.1
  10.7 0.0 copy-start.2
  10.7 0.0 copy-start.3
  10.7 0.0 collective-permute-done.one
  10.7 0.0 collective-permute-done.1.two
  10.7 1.3 %edge.1 = (bf16[2,256,640]{2,1,0:T(8,128)(2,1)S(1)}, bf16[40,16,128]{2,1,0:T(8,128)(2,1)S(1)}, bf16[16,128]{1,0:T(8,128)(2,1)S(1)}, bf16[9,16,128]{2,1,0:T(8,128)(2,1)S(1)}, bf16[9,16,128]{2,1,0:T(8,128)(2,1)S(1)}) custom-call(bf16[56,640]{1,0:T(8,128)(2,1)S(1)} %collective-permute-done.one, bf16[56,640]{1,0:T(8,128)(2,1)S(1)} %collective-permute-done.1.two, ...), custom_call_target="tpu_custom_call" | custom-call | flops 1000000000 | bytes 1000000 | tf_op jit(solution)/shard_map/edge/pallas_call | solution.py:330
  12.0 0.1 collective-permute-start.4
  12.1 1.0 %collective-permute-start.2 = (bf16[9,16,128]{2,1,0:T(8,128)(2,1)S(1)}, bf16[9,16,128]{2,1,0:T(8,128)(2,1)S(1)}, u32[]{:S(2)}, u32[]{:S(2)}) collective-permute-start(bf16[9,16,128]{2,1,0:T(8,128)(2,1)S(1)} %get-tuple-element.34), channel_id=1, source_target_pairs={{0,1},{1,0},{2,3},{3,2},{4,5},{5,4},{6,7},{7,6},{8,9},{9,8},{10,11... | collective-permute-start | bytes 110600 | tf_op jit(solution)/shard_map/ppermute | solution.py:574
  13.1 2.8 %collective-permute-start.3 = (bf16[9,16,128]{2,1,0:T(8,128)(2,1)S(1)}, bf16[9,16,128]{2,1,0:T(8,128)(2,1)S(1)}, u32[]{:S(2)}, u32[]{:S(2)}) collective-permute-start(bf16[9,16,128]{2,1,0:T(8,128)(2,1)S(1)} %get-tuple-element.35), channel_id=1, source_target_pairs={{0,15},{1,2},{2,1},{3,4},{4,3},{5,6},{6,5},{7,8},{8,7},{9,10},{10,... | collective-permute-start | bytes 110600 | tf_op jit(solution)/shard_map/ppermute | solution.py:575
  15.9 0.0 copy-done
  15.9 0.0 copy-done.1
  15.9 0.0 copy-done.2
  15.9 0.0 copy-done.3
  15.9 1.7 %early.1 = (bf16[8,256,640]{2,1,0:T(8,128)(2,1)}, bf16[16,256,128]{2,1,0:T(8,128)(2,1)}, f32[32,1024]{1,0:T(8,128)S(1)}, f32[256,1024]{1,0:T(8,128)S(1)}, bf16[2...) custom-call(bf16[256,3840]{1,0:T(8,128)(2,1)S(1)} %get-tuple-element, ...), custom_call_target="tpu_custom_call" | custom-call | flops 1000000000 | bytes 6000000 | tf_op jit(solution)/shard_map/early/pallas_call | solution.py:414
  17.7 0.0 collective-permute-done.4.fold
  17.7 0.0 collective-permute-done.2.one
  17.7 1.5 %collective-permute-done.3.two = bf16[9,16,128]{2,1,0:T(8,128)(2,1)S(1)} collective-permute-done((bf16[9,16,128]{2,1,0:T(8,128)(2,1)S(1)}, bf16[9,16,128]{2,1,0:T(8,128)(2,1)S(1)}, u32[]{:S(2)}, u32[]{:S(2)}) %collective-permute-start.3) | collective-permute-done | bytes 36896 | tf_op jit(solution)/shard_map/ppermute | solution.py:575
  19.2 1.6 %late.1 = bf16[16,256,128]{2,1,0:T(8,128)(2,1)} custom-call(s32[8,128]{1,0:T(8,128)S(1)} %get-tuple-element.31.plan, bf16[9,16,128]{2,1,0:T(8,128)(2,1)S(1)} %collective-permute-done.2.one, bf16[9,16,128]{2,1,0:T(8,128)(2,1)S(1)} %collective-permute-done.3.two, bf16[16,128]{1,0:T(8,128)(2,1)S(1)} %collective-permute-done.4.fold, ...), custom_call_target="tpu_custom_call", output_to_operand_aliasing={{}: (10, {})} | custom-call | flops 1000000000 | bytes 1000000 | tf_op jit(solution)/shard_map/late/pallas_call | solution.py:529
Async XLA Ops:
  0.6 7.3 %copy-start.4 = (bf16[3,3,256,256]{3,2,1,0:T(8,128)(2,1)S(1)}, bf16[3,3,256,256]{3,2,1,0:T(8,128)(2,1)}, u32[]{:S(2)}) copy-start(bf16[3,3,256,256]{3,2,1,0:T(8,128)(2,1)} %conv.1) | copy-start | bytes 3538948
  0.6 7.3 %copy-start.5 = (bf16[8,48,640]{2,1,0:T(8,128)(2,1)S(1)}, bf16[8,48,640]{2,1,0:T(8,128)(2,1)}, u32[]{:S(2)}) copy-start(bf16[8,48,640]{2,1,0:T(8,128)(2,1)} %x_hbm.1) | copy-start | bytes 1474564
  0.7 7.3 %copy-start.6 = (bf16[48,256]{1,0:T(8,128)(2,1)S(1)}, bf16[48,256]{1,0:T(8,128)(2,1)}, u32[]{:S(2)}) copy-start(bf16[48,256]{1,0:T(8,128)(2,1)} %lift.1) | copy-start | bytes 73732
  0.7 7.3 %copy-start.7 = (bf16[256,16]{0,1:T(8,128)(2,1)S(1)}, bf16[256,16]{0,1:T(8,128)(2,1)}, u32[]{:S(2)}) copy-start(bf16[256,16]{0,1:T(8,128)(2,1)} %param.15) | copy-start | bytes 24580
  1.7 9.0 %collective-permute-start = (bf16[56,640]{1,0:T(8,128)(2,1)S(1)}, bf16[56,640]{1,0:T(8,128)(2,1)S(1)}, u32[]{:S(2)}, u32[]{:S(2)}) collective-permute-start(bf16[56,640]{1,0:T(8,128)(2,1)S(1)} %get-tuple-element.24), channel_id=1, source_target_pairs={{0,1},{1,0},{2,3},{3,2},{4,5},{5,4},{6,7},{7,6},{8,9},{9,8},{10,11... | collective-permute-start | bytes 215048 | tf_op jit(solution)/shard_map/ppermute | solution.py:571
  2.3 8.4 %collective-permute-start.1 = (bf16[56,640]{1,0:T(8,128)(2,1)S(1)}, bf16[56,640]{1,0:T(8,128)(2,1)S(1)}, u32[]{:S(2)}, u32[]{:S(2)}) collective-permute-start(bf16[56,640]{1,0:T(8,128)(2,1)S(1)} %get-tuple-element.25), channel_id=1, source_target_pairs={{0,15},{1,2},{2,1},{3,4},{4,3},{5,6},{6,5},{7,8},{8,7},{9,10},{10,... | collective-permute-start | bytes 215048 | tf_op jit(solution)/shard_map/ppermute | solution.py:570
  7.9 2.6 %copy-start.8 = (bf16[16,95,128]{2,0,1:T(8,128)(2,1)S(1)}, bf16[16,95,128]{2,0,1:T(8,128)(2,1)}, u32[]{:S(2)}) copy-start(bf16[16,95,128]{2,0,1:T(8,128)(2,1)} %param.12) | copy-start | bytes 1167364
  10.6 5.3 %copy-start = (bf16[16,4,128,128]{3,2,1,0:T(8,128)(2,1)S(1)}, bf16[16,4,128,128]{3,2,1,0:T(8,128)(2,1)}, u32[]{:S(2)}) copy-start(bf16[16,4,128,128]{3,2,1,0:T(8,128)(2,1)} %regrid.1) | copy-start | bytes 6291460
  10.7 5.3 %copy-start.1 = (bf16[256,256]{1,0:T(8,128)(2,1)S(1)}, bf16[256,256]{1,0:T(8,128)(2,1)}, u32[]{:S(2)}) copy-start(bf16[256,256]{1,0:T(8,128)(2,1)} %mw.1) | copy-start | bytes 393220
  10.7 5.2 %copy-start.2 = (bf16[95,256]{1,0:T(8,128)(2,1)S(1)}, bf16[95,256]{1,0:T(8,128)(2,1)}, u32[]{:S(2)}) copy-start(bf16[95,256]{1,0:T(8,128)(2,1)} %ow.1) | copy-start | bytes 145924
  10.7 5.2 %copy-start.3 = (bf16[16,256]{1,0:T(8,128)(2,1)S(1)}, bf16[16,256]{1,0:T(8,128)(2,1)}, u32[]{:S(2)}) copy-start(bf16[16,256]{1,0:T(8,128)(2,1)} %cw.1) | copy-start | bytes 24580
  12.0 5.6 %collective-permute-start.4 = (bf16[16,128]{1,0:T(8,128)(2,1)S(1)}, bf16[16,128]{1,0:T(8,128)(2,1)S(1)}, u32[]{:S(2)}, u32[]{:S(2)}) collective-permute-start(bf16[16,128]{1,0:T(8,128)(2,1)S(1)} %get-tuple-element.36), channel_id=1, source_target_pairs={{0,8},{1,14},{2,13},{3,12},{4,11},{5,10},{6,9},{7,15},{8,0},{9,6},... | collective-permute-start | bytes 12296 | tf_op jit(solution)/shard_map/ppermute | solution.py:576
  12.1 5.6 %collective-permute-start.2 = (bf16[9,16,128]{2,1,0:T(8,128)(2,1)S(1)}, bf16[9,16,128]{2,1,0:T(8,128)(2,1)S(1)}, u32[]{:S(2)}, u32[]{:S(2)}) collective-permute-start(bf16[9,16,128]{2,1,0:T(8,128)(2,1)S(1)} %get-tuple-element.34), channel_id=1, source_target_pairs={{0,1},{1,0},{2,3},{3,2},{4,5},{5,4},{6,7},{7,6},{8,9},{9,8},{10,11... | collective-permute-start | bytes 110600 | tf_op jit(solution)/shard_map/ppermute | solution.py:574
  13.1 6.1 %collective-permute-start.3 = (bf16[9,16,128]{2,1,0:T(8,128)(2,1)S(1)}, bf16[9,16,128]{2,1,0:T(8,128)(2,1)S(1)}, u32[]{:S(2)}, u32[]{:S(2)}) collective-permute-start(bf16[9,16,128]{2,1,0:T(8,128)(2,1)S(1)} %get-tuple-element.35), channel_id=1, source_target_pairs={{0,15},{1,2},{2,1},{3,4},{4,3},{5,6},{6,5},{7,8},{8,7},{9,10},{10,... | collective-permute-start | bytes 110600 | tf_op jit(solution)/shard_map/ppermute | solution.py:575
